TPU v7x, 32 devices: a whole 2x2x4 slice. The times are simulated.
32 devices in a mesh: face: 4 (over z), tile: 8 (over y, x, core).
Axes of the slice: x: 2, y: 2, z: 4, core: 2. Of those that a mesh axis runs over, the one named last changes fastest.
Arguments:
- fields: bfloat16 [12, 128, 128, 256], P('face', 'tile'), may hold values from -6 to 6
- cotangent: bfloat16 [12, 128, 128, 256], P('face', 'tile'), may hold values from -6 to 6
- dw_kernel: float32 [256, 49], P('tile'), may hold values from -0.875 to 0.875
- dw_bias: float32 [256], P('tile'), may hold values from -3 to 3
- norm_gain: float32 [256], replicated, may hold values from 0.1 to 1.9
- norm_bias: float32 [256], replicated, may hold values from -3 to 3
- proj_in: bfloat16 [256, 1024], replicated, may hold values from -0.375 to 0.375
- bias_in: float32 [1024], replicated, may hold values from -3 to 3
- proj_out: bfloat16 [1024, 256], replicated, may hold values from -0.1875 to 0.1875
- bias_out: float32 [256], replicated, may hold values from -3 to 3
- layer_scale: float32 [256], replicated, may hold values from 0.3 to 1.5
- strip_source: int32 [48], replicated, may hold values from 0 to 47, each once
- strip_flip: int32 [48], replicated, may hold values 0 or 1
Outputs:
- section_out: bfloat16 [12, 128, 128, 256], P('face', 'tile')
- field_grad: bfloat16 [12, 128, 128, 256], P('face', 'tile')
Inputs may be any that keep to these rules, and one draw needn't show every extreme that they name: `strip_source`: entry 4 f + e names strip 4 f' + e', the edge e' of base face f' of the same sample whose rim pads edge e of face f; every strip is named exactly once.
All inputs are finite; a program needn't handle non-finite values.
Results may differ from a plain program's by a relative error of at most 0.0057.
Values may be sent and summed in bfloat16 or wider, within the bound.
No kernel may reach another device: no remote copies, remote signals or barrier semaphores. Data moves between devices by JAX's collectives and lax.ppermute only.
A program may use at most 192 MiB of HBM per device.

v0:
```python
import jax
import jax.numpy as jnp
from jax import lax
from jax.sharding import PartitionSpec as P

EPSILON = 1e-06
GELU_SCALE = 0.7978845608028654
GELU_CUBIC = 0.044715


def gelu_value(pre):
    inner = GELU_SCALE * (pre + GELU_CUBIC * pre * pre * pre)
    return 0.5 * pre * (1.0 + jnp.tanh(inner))


def gelu_slope(pre):
    tanh_val = jnp.tanh(GELU_SCALE * (pre + GELU_CUBIC * pre * pre * pre))
    return 0.5 * (1.0 + tanh_val) + 0.5 * pre * (1.0 - tanh_val * tanh_val) * GELU_SCALE * (
        1.0 + 3.0 * GELU_CUBIC * pre * pre
    )


def to_channels(cells):
    turned = jnp.transpose(cells, (0, 3, 1, 2))
    return lax.all_to_all(turned, "tile", split_axis=1, concat_axis=2, tiled=True)


def to_cells(planes):
    moved = lax.all_to_all(planes, "tile", split_axis=2, concat_axis=1, tiled=True)
    return jnp.transpose(moved, (0, 2, 3, 1))


def rims_of(planes):
    top = planes[:, :, 0:3, :]
    bottom = planes[:, :, ::-1, :][:, :, 0:3, :]
    left = jnp.swapaxes(planes[:, :, :, 0:3], 2, 3)
    right = jnp.swapaxes(planes[:, :, :, ::-1][:, :, :, 0:3], 2, 3)
    return jnp.stack([top, bottom, left, right], axis=1)


def edge_kernels(taps):
    kernel = taps.reshape(taps.shape[0], 7, 7)
    swapped = jnp.swapaxes(kernel, 1, 2)
    return jnp.stack([kernel, kernel[:, ::-1, :], swapped, swapped[:, ::-1, :]])


def edge_grads(band, kernels):
    size = band.shape[-1]
    padded = jnp.pad(band.astype(jnp.float32), ((0, 0), (0, 0), (0, 0), (0, 0), (3, 3)))
    layers = []
    for depth in range(3):
        total = jnp.zeros(band.shape[:3] + (size,), jnp.float32)
        for inner in range(3 - depth):
            for along in range(7):
                weight = kernels[:, :, 2 - depth - inner, along][None, :, :, None]
                total = total + weight * padded[:, :, :, inner, 6 - along : 6 - along + size]
        layers.append(total)
    return jnp.stack(layers, axis=3)


def grouped_conv(planes_wide, taps):
    chans = taps.shape[0]
    return lax.conv_general_dilated(
        planes_wide,
        taps.reshape(chans, 1, 7, 7),
        (1, 1),
        "VALID",
        dimension_numbers=("NCHW", "OIHW", "NCHW"),
        feature_group_count=chans,
        precision=lax.Precision.HIGHEST,
    )


def reader_tables(sample, strip_source, strip_flip):
    reader = (sample % 12)[:, None] * 4 + jnp.arange(4, dtype=jnp.int32)[None, :]
    source = (sample // 12)[:, None] * 48 + strip_source[reader]
    return (source, strip_flip[reader] == 1)


def shards(
    fields,
    cotangent,
    dw_kernel,
    dw_bias,
    norm_gain,
    norm_bias,
    proj_in,
    bias_in,
    proj_out,
    bias_out,
    layer_scale,
    strip_source,
    strip_flip,
):
    slots = fields.shape[0]
    size = fields.shape[2]
    chans = fields.shape[3]
    total_samples = slots * lax.axis_size("face")
    first = lax.axis_index("face") * slots
    own_samples = first + jnp.arange(slots, dtype=jnp.int32)
    source, mirror = reader_tables(own_samples, strip_source, strip_flip)
    planes = to_channels(fields)
    local_ch = planes.shape[1]
    all_rims = lax.all_gather(rims_of(planes), "face", axis=0, tiled=True)
    picked = jnp.take(
        all_rims.reshape(total_samples * 4, local_ch, 3, size), source.reshape(-1), axis=0
    )
    picked = picked.reshape(slots, 4, local_ch, 3, size)
    strips = jnp.where(mirror[:, :, None, None, None], picked[..., ::-1], picked)
    left = jnp.swapaxes(strips[:, 2][:, :, ::-1, :], 2, 3)
    right = jnp.swapaxes(strips[:, 3], 2, 3)
    middle = jnp.concatenate([left, planes, right], axis=3)
    edge_pad = ((0, 0), (0, 0), (0, 0), (3, 3))
    top = jnp.pad(strips[:, 0][:, :, ::-1, :], edge_pad)
    bottom = jnp.pad(strips[:, 1], edge_pad)
    padded = jnp.concatenate([top, middle, bottom], axis=2)
    conv_sum = grouped_conv(padded.astype(jnp.float32), dw_kernel) + dw_bias[None, :, None, None]
    conv = to_cells(conv_sum.astype(jnp.bfloat16))
    cells = conv.reshape(-1, chans).astype(jnp.float32)
    mean = jnp.mean(cells, axis=-1, keepdims=True)
    centred = cells - mean
    inv = lax.rsqrt(jnp.mean(centred * centred, axis=-1, keepdims=True) + EPSILON)
    nhat = centred * inv
    normed = (nhat * norm_gain + norm_bias).astype(jnp.bfloat16)
    pre = jnp.dot(normed, proj_in, preferred_element_type=jnp.float32) + bias_in
    act = gelu_value(pre).astype(jnp.bfloat16)
    mlp = jnp.dot(act, proj_out, preferred_element_type=jnp.float32) + bias_out
    section_out = (fields.reshape(-1, chans).astype(jnp.float32) + layer_scale * mlp).astype(
        jnp.bfloat16
    )
    dmix = (layer_scale * cotangent.reshape(-1, chans).astype(jnp.float32)).astype(jnp.bfloat16)
    dact = lax.dot_general(
        dmix, proj_out, (((1,), (1,)), ((), ())), preferred_element_type=jnp.float32
    )
    dpre = (dact * gelu_slope(pre)).astype(jnp.bfloat16)
    dnorm = (
        lax.dot_general(dpre, proj_in, (((1,), (1,)), ((), ())), preferred_element_type=jnp.float32)
        * norm_gain
    )
    dconv = inv * (
        dnorm
        - jnp.mean(dnorm, axis=-1, keepdims=True)
        - nhat * jnp.mean(dnorm * nhat, axis=-1, keepdims=True)
    )
    dconv = dconv.astype(jnp.bfloat16).reshape(fields.shape)
    dplanes = to_channels(dconv)
    dpadded = jnp.pad(dplanes.astype(jnp.float32), ((0, 0), (0, 0), (3, 3), (3, 3)))
    flipped = dw_kernel.reshape(local_ch, 7, 7)[:, ::-1, ::-1].reshape(local_ch, 49)
    interior = grouped_conv(dpadded, flipped)
    kernels = edge_kernels(dw_kernel)
    band = rims_of(dplanes)
    flat_width = local_ch * 3 * size
    strip_grad = edge_grads(band, kernels)
    strip_grad = jnp.where(mirror[:, :, None, None, None], strip_grad[..., ::-1], strip_grad)
    targets = jnp.arange(total_samples * 4, dtype=jnp.int32)
    onehot = (targets[:, None] == source.reshape(-1)[None, :]).astype(jnp.float32)
    spread = jnp.dot(
        onehot, strip_grad.reshape(slots * 4, flat_width), precision=lax.Precision.HIGHEST
    )
    spread = spread.reshape(total_samples, 4, local_ch, 3, size)
    owned = lax.psum_scatter(
        spread.astype(jnp.bfloat16), "face", scatter_dimension=0, tiled=True
    ).astype(jnp.float32)
    interior = interior.at[:, :, 0:3, :].add(owned[:, 0])
    interior = interior.at[:, :, size - 3 :, :].add(owned[:, 1][:, :, ::-1, :])
    interior = interior.at[:, :, :, 0:3].add(jnp.swapaxes(owned[:, 2], 2, 3))
    interior = interior.at[:, :, :, size - 3 :].add(jnp.swapaxes(owned[:, 3][:, :, ::-1, :], 2, 3))
    conv_grad = to_cells(interior.astype(jnp.bfloat16))
    field_grad = (cotangent.astype(jnp.float32) + conv_grad.astype(jnp.float32)).astype(
        jnp.bfloat16
    )
    return (section_out.reshape(fields.shape), field_grad)


def solution(mesh):
    placed = (
        P("face", "tile", None, None),
        P("face", "tile", None, None),
        P("tile", None),
        P("tile"),
        P(),
        P(),
        P(),
        P(),
        P(),
        P(),
        P(),
        P(),
        P(),
    )
    return jax.shard_map(
        shards,
        mesh=mesh,
        in_specs=placed,
        out_specs=(P("face", "tile", None, None), P("face", "tile", None, None)),
        check_vma=False,
    )
```

profile of v0, /device:TPU:0, one launch (start us, length us, event | category | flops | bytes accessed | tf_op | source)
XLA Modules:
  0.0 908.0 jit_solution(2985848319941584613)
XLA Ops:
  7.2 4.9 copy.214
  12.1 43.0 %all_to_all.57 = bf16[3,256,16,128]{3,2,0,1:T(8,128)(2,1)S(1)} all-to-all(bf16[3,256,16,128]{3,2,0,1:T(8,128)(2,1)} %bitcast.191), channel_id=1, replica_groups=mesh['face'=4,'tile'=8] {'tile'}, dimensions={1} | all-to-all | bytes 6291456 | tf_op jit(solution)/shard_map/all_to_all | solution.py:25
  56.1 3.9 slice_bitcast_fusion.2
  60.3 3.2 copy.219
  63.6 47.3 %slice.352 = bf16[3,32,128,3]{3,2,1,0:T(8,128)(2,1)} reverse(bf16[3,32,128,3]{3,2,1,0:T(8,128)(2,1)} %get-tuple-element.71), dimensions={3} | reverse | bytes 147456 | tf_op jit(solution)/shard_map/slice | solution.py:37
  110.9 3.2 copy.220
  117.7 27.2 %all-gather.2.cloned.1.call-done = bf16[12,4,32,3,128]{4,2,3,1,0:T(8,128)(2,1)} async-done(((bf16[3,4,32,3,128]{4,2,3,1,0:T(8,128)(2,1)}), bf16[12,4,32,3,128]{4,2,3,1,0:T(8,128)(2,1)}) %all-gather.2.cloned.1.call-update) | async-done | bytes 1179664 | tf_op jit(solution)/shard_map/all_gather | solution.py:104
  149.5 2.8 copy.222
  152.3 2.8 copy.223
  155.1 9.9 %fusion.29 = bf16[32,134,3,134]{3,1,0,2:T(8,128)(2,1)} fusion(bf16[3,32,3,128]{3,2,1,0:T(4,128)(2,1)S(1)} %get-tuple-element.77, bf16[3,32,3,128]{3,2,1,0:T(4,128)(2,1)S(1)} %rev.32, bf16[3,32,128,3]{3,2,1,0:T(8,128)(2,1)} %copy.223, bf16[3,32,128,128]{3,2,1,0:T(8,128)(2,1)} %bitcast.181, bf16[3,32,128,3]{3,2,1,0:T(8,128)(2,1)} %copy.222), kind=kLoop, calls=%fused_computation.35 | loop fusion | flops 24132864 | bytes 6888192 | tf_op jit(solution)/shard_map/concatenate | solution.py:116
  165.1 12.0 %copy.270 = bf16[32,134,3,134]{1,0,3,2:T(8,128)(2,1)} copy(bf16[32,134,3,134]{3,1,0,2:T(8,128)(2,1)} %fusion.29) | data formatting | bytes 6895104
  177.1 4.8 pad.24.clone
  182.1 5.2 fusion.19
  187.3 23.3 %copy.225 = bf16[32,134,3,8,23]{0,3,2,4,1:T(8,128)(2,1)} copy(bf16[32,134,3,8,23]{1,0,4,3,2:T(8,128)(2,1)} %fusion.19) | data formatting | bytes 9467904 | tf_op jit(solution)/shard_map/conv_general_dilated | solution.py:63
  210.5 90.3 %fusion.7 = f32[128,24,17,32]{3,1,2,0:T(8,128)} fusion(f32[32,1,7,7]{0,1,3,2:T(1,128)S(1)} %reshape.452, bf16[32,134,3,8,23]{0,3,2,4,1:T(8,128)(2,1)} %copy.225), kind=kOutput, calls=%fused_computation.13 | convolution fusion | flops 982646784 | bytes 11424896 | tf_op jit(solution)/shard_map/conv_general_dilated | solution.py:63
  300.9 22.9 %copy.228 = f32[128,24,17,32]{0,3,2,1:T(8,128)} copy(f32[128,24,17,32]{3,1,2,0:T(8,128)} %fusion.7) | data formatting | bytes 13369344 | tf_op jit(solution)/shard_map/conv_general_dilated | solution.py:63
  323.7 4.1 add_convert_fusion
  330.1 5.2 copy.229
  335.3 4.7 all-to-all-start.1
  340.0 4.8 copy.233
  344.8 5.9 copy.234
  350.7 4.9 fusion.31
  355.7 22.2 %all-to-all-done.1 = bf16[3,32,128,128]{3,1,0,2:T(8,128)(2,1)} async-done(((bf16[3,32,128,128]{3,1,0,2:T(8,128)(2,1)}), bf16[3,32,128,128]{3,1,0,2:T(8,128)(2,1)}, u32[]{:S(2)}, u32[]{:S(2)}) %all-to-all-start.1) | async-done | bytes 3145760 | tf_op jit(solution)/shard_map/all_to_all | solution.py:29
  377.9 3.1 copy.230
  381.9 3.5 copy.231
  385.4 6.7 copy.232
  392.1 3.2 reduce_sum.36
  395.3 3.6 multiply_reduce_fusion.1
  399.9 3.3 add_convert_fusion.2
  403.2 10.1 %fusion.73 = f32[6144,1024]{1,0:T(8,128)} fusion(bf16[6144,256]{1,0:T(8,128)(2,1)S(1)} %add_convert_fusion.2, bf16[256,1024]{1,0:T(8,128)(2,1)S(1)} %copy-done), kind=kOutput, calls=%fused_computation.173 | convolution fusion | flops 3221225472 | bytes 28835840 | tf_op jit(solution)/shard_map/dot_general | solution.py:125
  413.3 25.1 %fusion.71 = (f32[6144]{0:T(1024)S(1)}, f32[6144]{0:T(1024)S(1)}, f32[6144,256]{1,0:T(8,128)}) fusion(f32[6144]{0:T(1024)S(1)} %bitcast.227, f32[6144]{0:T(1024)S(1)} %bitcast.224, f32[3,16,128,256]{3,2,1,0:T(8,128)} %copy.232, f32[256]{0:T(256)S(1)} %copy-done.21, bf16[256,1024]{1,0:T(8,128)(2,1)S(1)} %copy-done, f32[6144,1024]{1,0:T(8,128)} %fusion.73, ...), kind=kOutput, calls=%fused_computation.171 | convolution fusion | flops 6577704960 | bytes 42046464 | tf_op jit(solution)/shard_map/dot_general | solution.py:137
  438.4 7.7 multiply_convert_fusion.10
  446.1 5.0 copy.235
  451.1 4.5 all-to-all-start.2
  455.9 37.5 %all-to-all-done.2 = bf16[3,256,16,128]{3,2,0,1:T(8,128)(2,1)} async-done(((bf16[3,256,16,128]{3,2,0,1:T(8,128)(2,1)}), bf16[3,256,16,128]{3,2,0,1:T(8,128)(2,1)}, u32[]{:S(2)}, u32[]{:S(2)}) %all-to-all-start.2) | async-done | bytes 3145760 | tf_op jit(solution)/shard_map/all_to_all | solution.py:25
  493.4 2.8 copy.237
  496.3 3.9 fusion.72
  500.5 5.4 copy.271
  508.4 2.6 fusion.33
  511.0 3.2 copy.267
  514.2 3.2 copy.268
  518.0 9.9 %multiply_add_fusion.2 = (f32[3,4,32,1,128]{4,3,2,0,1:T(1,128)S(1)}, f32[3,4,32,1,128]{4,3,2,0,1:T(1,128)S(1)}) fusion(f32[3,4,32,3,128]{4,3,2,0,1:T(4,128)S(1)} %maximum_convert_fusion, f32[4,32]{1,0:T(4,128)S(1)} %bitcast.231, f32[4,32]{1,0:T(4,128)S(1)} %bitcast.253, f32[4,32]{1,0:T(4,128)S(1)} %bitcast.255, f32[4,32]{1,0:T(4,128)S(1)} %bitcast.257, ...), kind=kLoop, calls=%fused_computation.97 | loop fusion | flops 1966080 | bytes 1601536 | tf_op jit(solution)/shard_map/add | solution.py:56
  527.9 10.8 %fusion.48 = f32[3,4,32,1,128]{4,3,2,0,1:T(1,128)S(1)} fusion(f32[3,4,32,3,128]{4,3,2,0,1:T(4,128)S(1)} %maximum_convert_fusion, f32[4,32]{1,0:T(4,128)S(1)} %bitcast.232, f32[4,32]{1,0:T(4,128)S(1)} %bitcast.254, f32[4,32]{1,0:T(4,128)S(1)} %bitcast.256, f32[4,32]{1,0:T(4,128)S(1)} %bitcast.258, f32[4,32]{1,0:T(4,128)S(1)} %bitcast.248, ...), kind=kLoop, calls=%fused_computation.94 | loop fusion | flops 2015232 | bytes 1615872 | tf_op jit(solution)/shard_map/add | solution.py:56
  545.2 25.9 %copy.239 = bf16[32,128,3,8,23]{0,3,2,4,1:T(8,128)(2,1)} copy(bf16[32,128,3,8,23]{1,0,4,3,2:T(8,128)(2,1)} %fusion.33) | data formatting | bytes 9043968 | tf_op jit(solution)/shard_map/conv_general_dilated | solution.py:63
  571.1 91.0 %fusion.9 = f32[128,24,17,32]{3,1,2,0:T(8,128)} fusion(bf16[32,128,3,8,23]{0,3,2,4,1:T(8,128)(2,1)} %copy.239, f32[32,1,7,7]{0,3,2,1:T(8,128)S(1)} %bitcast.230), kind=kOutput, calls=%fused_computation.16 | convolution fusion | flops 969486336 | bytes 11212928 | tf_op jit(solution)/shard_map/conv_general_dilated | solution.py:63
  662.2 22.9 %copy.242 = f32[128,24,17,32]{0,3,2,1:T(8,128)} copy(f32[128,24,17,32]{3,1,2,0:T(8,128)} %fusion.9) | data formatting | bytes 13369344 | tf_op jit(solution)/shard_map/conv_general_dilated | solution.py:63
  685.0 3.3 broadcast_select_fusion
  688.4 2.8 copy-done.5
  691.1 3.4 slice.438
  694.5 5.3 copy.266
  699.8 6.2 slice_bitcast_fusion
  707.1 6.0 copy.254
  713.2 31.9 %scatter-add.14 = f32[3,32,128,128]{2,1,3,0:T(8,128)} dynamic-update-slice(f32[3,32,128,128]{2,1,3,0:T(8,128)} %slice_bitcast_fusion, f32[3,32,3,128]{2,1,3,0:T(8,128)} %copy.254, s32[]{:T(128)} %constant.165.clone.1, s32[]{:T(128)} %constant.165.clone.1, s32[]{:T(128)} %constant.165.clone.1, s32[]{:T(128)} %constant.165.clone.1) | dynamic-update-slice | bytes 294916 | tf_op jit(solution)/shard_map/scatter-add | solution.py:164
  745.1 7.1 slice.447
  752.2 5.5 copy.269
  757.8 6.0 copy.256
  763.8 67.9 %scatter-add.15 = f32[3,32,128,128]{2,1,3,0:T(8,128)} dynamic-update-slice(f32[3,32,128,128]{2,1,3,0:T(8,128)} %scatter-add.14, f32[3,32,3,128]{2,1,3,0:T(8,128)} %copy.256, s32[]{:T(128)} %constant.165.clone.1, s32[]{:T(128)} %constant.165.clone.1, s32[]{:T(128)} %constant.181.clone.1, s32[]{:T(128)} %constant.165.clone.1) | dynamic-update-slice | bytes 294916 | tf_op jit(solution)/shard_map/scatter-add | solution.py:165
  834.8 5.2 convert_element_type.122
  840.0 5.5 copy.257
  845.5 4.5 all-to-all-start.3
  850.0 16.3 %fusion.24 = bf16[6144,256]{1,0:T(8,128)(2,1)} fusion(bf16[1024,256]{1,0:T(8,128)(2,1)S(1)} %copy-done.24, f32[6144,1024]{1,0:T(8,128)} %fusion.73, f32[1024]{0:T(1024)S(1)} %copy-done.26, bf16[6144,256]{1,0:T(8,128)(2,1)} %bitcast.197, f32[256]{0:T(256)S(1)} %copy-done.27, f32[256]{0:T(256)S(1)} %copy-done.19), kind=kOutput, calls=%fused_computation.32 | convolution fusion | flops 3292004352 | bytes 31987712 | tf_op jit(solution)/shard_map/dot_general | solution.py:127
  866.3 21.5 %all-to-all-done.3 = bf16[3,32,128,128]{3,1,0,2:T(8,128)(2,1)} async-done(((bf16[3,32,128,128]{3,1,0,2:T(8,128)(2,1)}), bf16[3,32,128,128]{3,1,0,2:T(8,128)(2,1)}, u32[]{:S(2)}, u32[]{:S(2)}) %all-to-all-start.3) | async-done | bytes 3145760 | tf_op jit(solution)/shard_map/all_to_all | solution.py:29
  887.9 3.1 copy.258
  896.0 4.9 copy.260
  (135 shorter events, 33.0 us)
Async XLA Ops:
  7.2 396.0 %copy-start = (bf16[256,1024]{1,0:T(8,128)(2,1)S(1)}, bf16[256,1024]{1,0:T(8,128)(2,1)}, u32[]{:S(2)}) copy-start(bf16[256,1024]{1,0:T(8,128)(2,1)} %param.27) | copy-start | bytes 1572868
  7.2 137.7 %all-gather.2.cloned.1.call-start = ((), (), s32[]{:S(2)}) async-start(), calls=%async_computation.5 | async-start | bytes 1474560 | tf_op jit(solution)/shard_map/all_gather | solution.py:104
  56.0 4.1 copy-start.7
  60.3 54.8 %copy-start.2 = (s32[48]{0:T(128)S(1)}, s32[48]{0:T(128)}, u32[]{:S(2)}) copy-start(s32[48]{0:T(128)} %param.32) | copy-start | bytes 580
  63.6 52.2 %copy-start.3 = (s32[48]{0:T(128)S(1)}, s32[48]{0:T(128)}, u32[]{:S(2)}) copy-start(s32[48]{0:T(128)} %param.33) | copy-start | bytes 580
  63.6 53.9 %copy-start.13 = (f32[32,49]{1,0:T(8,128)S(1)}, f32[32,49]{1,0:T(8,128)}, u32[]{:S(2)}) copy-start(f32[32,49]{1,0:T(8,128)} %param.23) | copy-start | bytes 18820
  116.7 48.4 %copy-start.16 = (pred[3,4]{0,1:T(4,128)(4,1)}, pred[3,4]{0,1:T(4,128)(4,1)S(1)}, u32[]{:S(2)}) copy-start(pred[3,4]{0,1:T(4,128)(4,1)S(1)} %copy.212) | copy-start | bytes 40
  116.8 0.6 copy-start.11
  117.6 27.3 %copy-start.9 = (f32[32,49]{0,1:T(8,128)}, f32[32,49]{0,1:T(8,128)S(1)}, u32[]{:S(2)}) copy-start(f32[32,49]{0,1:T(8,128)S(1)} %copy.226) | copy-start | bytes 18820
  300.8 22.9 %copy-start.14 = (pred[24,17]{1,0:T(8,128)(4,1)S(1)}, pred[24,17]{1,0:T(8,128)(4,1)}, u32[]{:S(2)}) copy-start(pred[24,17]{1,0:T(8,128)(4,1)} %constant.198) | copy-start | bytes 1228
  300.8 22.9 %copy-start.22 = (f32[32]{0:T(128)S(1)}, f32[32]{0:T(128)}, u32[]{:S(2)}) copy-start(f32[32]{0:T(128)} %param.24) | copy-start | bytes 388
  335.3 42.6 %all-to-all-start.1 = ((bf16[3,32,128,128]{3,1,0,2:T(8,128)(2,1)}), bf16[3,32,128,128]{3,1,0,2:T(8,128)(2,1)}, u32[]{:S(2)}, u32[]{:S(2)}) async-start(bf16[3,32,128,128]{3,1,0,2:T(8,128)(2,1)} %copy.229), calls=%async_computation.1 | async-start | bytes 6291456 | tf_op jit(solution)/shard_map/all_to_all | solution.py:29
  340.0 10.8 %copy-start.18 = (f32[256]{0:T(256)S(1)}, f32[256]{0:T(256)}, u32[]{:S(2)}) copy-start(f32[256]{0:T(256)} %param.31) | copy-start | bytes 3076
  392.1 6.8 copy-start.20
  392.1 6.8 copy-start.21
  395.3 4.6 copy-start.4
  403.2 10.1 %copy-start.23 = (bf16[1024,256]{1,0:T(8,128)(2,1)S(1)}, bf16[1024,256]{1,0:T(8,128)(2,1)}, u32[]{:S(2)}) copy-start(bf16[1024,256]{1,0:T(8,128)(2,1)} %param.29) | copy-start | bytes 1572868
  403.2 10.1 %copy-start.25 = (f32[1024]{0:T(1024)S(1)}, f32[1024]{0:T(1024)}, u32[]{:S(2)}) copy-start(f32[1024]{0:T(1024)} %param.28) | copy-start | bytes 12292
  446.1 9.5 %copy-start.12 = (s32[3,4]{1,0:T(4,128)S(1)}, s32[3,4]{1,0:T(4,128)}, u32[]{:S(2)}) copy-start(s32[3,4]{1,0:T(4,128)} %copy-done.11) | copy-start | bytes 148
  446.1 9.6 %copy-start.10 = (f32[32,49]{0,1:T(8,128)S(1)}, f32[32,49]{0,1:T(8,128)}, u32[]{:S(2)}) copy-start(f32[32,49]{0,1:T(8,128)} %copy-done.9) | copy-start | bytes 18820
  451.1 42.3 %all-to-all-start.2 = ((bf16[3,256,16,128]{3,2,0,1:T(8,128)(2,1)}), bf16[3,256,16,128]{3,2,0,1:T(8,128)(2,1)}, u32[]{:S(2)}, u32[]{:S(2)}) async-start(bf16[3,256,16,128]{3,2,0,1:T(8,128)(2,1)} %bitcast.188), calls=%async_computation.2 | async-start | bytes 6291456 | tf_op jit(solution)/shard_map/all_to_all | solution.py:25
  455.5 250.5 %reduce-scatter.2.cloned.1.call-start = ((), (), s32[]{:S(2)}) async-start(), calls=%async_computation.6 | async-start | bytes 1474560 | tf_op jit(solution)/shard_map/reduce_scatter | solution.py:161
  496.2 4.0 copy-start.6
  511.0 29.9 %copy-start.17 = (pred[3,4]{0,1:T(4,128)(4,1)S(1)}, pred[3,4]{0,1:T(4,128)(4,1)}, u32[]{:S(2)}) copy-start(pred[3,4]{0,1:T(4,128)(4,1)} %copy-done.16) | copy-start | bytes 40
  662.2 22.9 %copy-start.15 = (pred[24,17]{1,0:T(8,128)(4,1)S(1)}, pred[24,17]{1,0:T(8,128)(4,1)}, u32[]{:S(2)}) copy-start(pred[24,17]{1,0:T(8,128)(4,1)} %constant.198) | copy-start | bytes 1228
  688.4 2.8 copy-start.5
  840.0 9.9 %copy-start.19 = (f32[256]{0:T(256)S(1)}, f32[256]{0:T(256)}, u32[]{:S(2)}) copy-start(f32[256]{0:T(256)} %param.31) | copy-start | bytes 3076
  840.0 9.9 %copy-start.24 = (bf16[1024,256]{1,0:T(8,128)(2,1)S(1)}, bf16[1024,256]{1,0:T(8,128)(2,1)}, u32[]{:S(2)}) copy-start(bf16[1024,256]{1,0:T(8,128)(2,1)} %param.29) | copy-start | bytes 1572868
  840.0 10.0 %copy-start.26 = (f32[1024]{0:T(1024)S(1)}, f32[1024]{0:T(1024)}, u32[]{:S(2)}) copy-start(f32[1024]{0:T(1024)} %param.28) | copy-start | bytes 12292
  840.0 10.0 %copy-start.27 = (f32[256]{0:T(256)S(1)}, f32[256]{0:T(256)}, u32[]{:S(2)}) copy-start(f32[256]{0:T(256)} %param.30) | copy-start | bytes 3076
  845.5 42.3 %all-to-all-start.3 = ((bf16[3,32,128,128]{3,1,0,2:T(8,128)(2,1)}), bf16[3,32,128,128]{3,1,0,2:T(8,128)(2,1)}, u32[]{:S(2)}, u32[]{:S(2)}) async-start(bf16[3,32,128,128]{3,1,0,2:T(8,128)(2,1)} %copy.257), calls=%async_computation.4 | async-start | bytes 6291456 | tf_op jit(solution)/shard_map/all_to_all | solution.py:29
  891.9 1.9 copy-start.8
  893.8 7.1 copy-start.1
Sparse Core Ops, SparseCore 0:
  115.1 29.8 all-gather.1
  545.3 26.5 reduce-scatter.1
where the time goes:
time: 926 us; the launch traced here: 908 us
  local copies, waits for them, and re-layouts  408 us (44%)
  matrix products  234 us (25%)
  waiting for transfers between devices  109 us (12%)
  other arithmetic  85.1 us (9%)
  blocking collectives  43 us (5%)
  between operations  15 us (2%)
  starting transfers between devices  13.7 us (1%)
    conv_general_dilated x2, matrix products, grouped_conv(): lax.conv_general_dilated(planes_wide, taps.reshape(chans, 1, 7, 7), (1, 1...  181 us
    conv_general_dilated x8, local copies, waits for them, and re-layouts, grouped_conv(): lax.conv_general_dilated(planes_wide, taps.reshape(chans, 1, 7, 7), (1, 1...  105 us
    scatter-add x1, local copies, waits for them, and re-layouts, shards(): interior = interior.at[:, :, size - 3:, :].add(owned[:, 1][:, :, ::-1, :])  67.9 us
    unnamed x66, local copies, waits for them, and re-layouts  54.8 us
    slice x2, local copies, waits for them, and re-layouts, rims_of(): right = jnp.swapaxes(planes[:, :, :, ::-1][:, :, :, 0:3], 2, 3)  47.5 us
    all_to_all x2, waiting for transfers between devices, to_cells(): lax.all_to_all(planes, 'tile', split_axis=2, concat_axis=1, tiled=True)  43.7 us
    all_to_all x1, blocking collectives, to_channels(): lax.all_to_all(turned, 'tile', split_axis=1, concat_axis=2, tiled=True)  43 us
    all_to_all x1, waiting for transfers between devices, to_channels(): lax.all_to_all(turned, 'tile', split_axis=1, concat_axis=2, tiled=True)  37.5 us
  transfers between devices with their start and end apart: 5, of which 4 were waited for; matrix products, arithmetic and copies ran while one was open for 21% of the time, Pallas kernels for 0%

commit v1 on v0

--- a/solution.py
+++ b/solution.py
@@ -1,6 +1,10 @@
+import functools
+
 import jax
 import jax.numpy as jnp
 from jax import lax
+from jax.experimental import pallas as pl
+from jax.experimental.pallas import tpu as pltpu
 from jax.sharding import PartitionSpec as P
 
 EPSILON = 1e-06
@@ -171,6 +175,366 @@
     )
     return (section_out.reshape(fields.shape), field_grad)
 
+DEPTH = 3
+TAPS = 7
+SUB = 8
+LANES = 128
+
+
+def conv_rows(xs, w, half, col, rows_out, row_base):
+    acc = [None] * rows_out
+    for q in range(TAPS):
+        taps = [w[half, pl.ds(TAPS * p + q, 1), :] for p in range(TAPS)]
+        for row in range(rows_out + TAPS - 1):
+            x = xs[half, row_base + row, pl.ds(col + q, SUB), :]
+            for p in range(TAPS):
+                i = row - p
+                if 0 <= i < rows_out:
+                    part = x * taps[p]
+                    acc[i] = part if acc[i] is None else acc[i] + part
+    return acc
+
+
+def fill(xs, x_ref, top_ref, bot_ref, lead):
+    rows, width = x_ref.shape[1], x_ref.shape[2]
+    for half in range(x_ref.shape[3] // LANES):
+        lanes = pl.ds(half * LANES, LANES)
+        xs[half, pl.ds(0, DEPTH), pl.ds(lead, width), :] = top_ref[0, :, :, lanes].astype(jnp.float32)
+        xs[half, pl.ds(DEPTH + rows, DEPTH), pl.ds(lead, width), :] = bot_ref[0, :, :, lanes].astype(
+            jnp.float32
+        )
+
+        def one(row, carry):
+            xs[half, DEPTH + row, pl.ds(lead, width), :] = x_ref[0, row, :, lanes].astype(jnp.float32)
+            return carry
+
+        lax.fori_loop(0, rows, one, 0)
+
+
+def conv_forward_kernel(x_ref, top_ref, bot_ref, left_ref, right_ref, w_ref, out_ref, xs):
+    rows, width, chans = x_ref.shape[1:]
+    fill(xs, x_ref, top_ref, bot_ref, SUB)
+    for half in range(chans // LANES):
+        lanes = pl.ds(half * LANES, LANES)
+        xs[half, :, pl.ds(0, SUB), :] = left_ref[0, :, :, lanes].astype(jnp.float32)
+        xs[half, :, pl.ds(SUB + width, SUB), :] = right_ref[0, :, :, lanes].astype(jnp.float32)
+    step = min(rows, 16)
+    for half in range(chans // LANES):
+        lanes = pl.ds(half * LANES, LANES)
+
+        def one(block, carry):
+            start = pl.multiple_of(block * SUB, SUB)
+            for base in range(0, rows, step):
+                acc = conv_rows(xs, w_ref, half, start + SUB - DEPTH, step, base)
+                for i in range(step):
+                    out_ref[0, base + i, pl.ds(start, SUB), lanes] = (
+                        acc[i] + w_ref[half, pl.ds(TAPS * TAPS, 1), :]
+                    )
+            return carry
+
+        lax.fori_loop(0, width // SUB, one, 0)
+
+
+def conv_backward_kernel(x_ref, top_ref, bot_ref, w_ref, out_ref, left_ref, right_ref, above_ref, below_ref, xs):
+    rows, width, chans = x_ref.shape[1:]
+    lead = 2 * SUB
+    for half in range(chans // LANES):
+        xs[half, :, pl.ds(0, lead), :] = jnp.zeros((rows + 2 * DEPTH, lead, LANES), jnp.float32)
+        xs[half, :, pl.ds(lead + width, lead), :] = jnp.zeros((rows + 2 * DEPTH, lead, LANES), jnp.float32)
+    fill(xs, x_ref, top_ref, bot_ref, lead)
+    step = min(rows, 16)
+    for half in range(chans // LANES):
+        lanes = pl.ds(half * LANES, LANES)
+
+        def one(block, carry):
+            start = pl.multiple_of(block * SUB, SUB)
+            for base in range(0, rows, step):
+                acc = conv_rows(xs, w_ref, half, start + lead - DEPTH, step, base)
+                for i in range(step):
+                    out_ref[0, base + i, pl.ds(start, SUB), lanes] = acc[i]
+            above = [None] * DEPTH
+            below = [None] * DEPTH
+            for q in range(TAPS):
+                for edge in range(DEPTH):
+                    x_top = xs[half, DEPTH + edge, pl.ds(start + lead - DEPTH + q, SUB), :]
+                    x_bot = xs[half, DEPTH + rows - 1 - edge, pl.ds(start + lead - DEPTH + q, SUB), :]
+                    for d in range(DEPTH - edge):
+                        p = edge + d + DEPTH + 1
+                        up = x_top * w_ref[half, pl.ds(TAPS * p + q, 1), :]
+                        down = x_bot * w_ref[half, pl.ds(TAPS * (TAPS - 1 - p) + q, 1), :]
+                        above[d] = up if above[d] is None else above[d] + up
+                        below[d] = down if below[d] is None else below[d] + down
+            for d in range(DEPTH):
+                above_ref[0, d, pl.ds(start, SUB), lanes] = above[d]
+                below_ref[0, d, pl.ds(start, SUB), lanes] = below[d]
+            return carry
+
+        lax.fori_loop(0, width // SUB, one, 0)
+        for base in range(0, rows, step):
+            for ref, start in ((left_ref, lead - SUB), (right_ref, lead + width)):
+                acc = conv_rows(xs, w_ref, half, start - DEPTH, step, base)
+                for i in range(step):
+                    ref[0, base + i, :, lanes] = acc[i]
+
+
+def cell_kernel(conv_ref, x_ref, cot_ref, vec_ref, bias_in_ref, w_in_ref, w_out_ref, w_out_t_ref, w_in_t_ref, out_ref, dconv_ref, *, chunk):
+    chans = conv_ref.shape[1]
+    gain, shift = vec_ref[0:1, :], vec_ref[1:2, :]
+    bias_out, scale = vec_ref[2:3, :], vec_ref[3:4, :]
+    hidden = w_in_ref.shape[1]
+    piece = 256
+
+    def one(block, carry):
+        at = pl.ds(pl.multiple_of(block * chunk, chunk), chunk)
+        cells = conv_ref[at, :].astype(jnp.bfloat16).astype(jnp.float32)
+        mean = jnp.sum(cells, axis=-1, keepdims=True) * (1.0 / chans)
+        centred = cells - mean
+        inv = lax.rsqrt(jnp.sum(centred * centred, axis=-1, keepdims=True) * (1.0 / chans) + EPSILON)
+        nhat = centred * inv
+        normed = (nhat * gain + shift).astype(jnp.bfloat16)
+        dmix = (scale * cot_ref[at, :].astype(jnp.float32)).astype(jnp.bfloat16)
+        mlp = None
+        dnorm = None
+        for first in range(0, hidden, piece):
+            cut = pl.ds(first, piece)
+            pre = jnp.dot(normed, w_in_ref[:, cut], preferred_element_type=jnp.float32)
+            pre = pre + bias_in_ref[0:1, cut]
+            dact = jnp.dot(dmix, w_out_t_ref[:, cut], preferred_element_type=jnp.float32)
+            square = pre * pre
+            tanh_val = jnp.tanh(pre * (GELU_SCALE + (GELU_SCALE * GELU_CUBIC) * square))
+            lifted = 0.5 + 0.5 * tanh_val
+            act = (pre * lifted).astype(jnp.bfloat16)
+            bend = (0.5 * GELU_SCALE) * pre + (1.5 * GELU_SCALE * GELU_CUBIC) * (pre * square)
+            slope = lifted + (1.0 - tanh_val * tanh_val) * bend
+            dpre = (dact * slope).astype(jnp.bfloat16)
+            mlp_part = jnp.dot(act, w_out_ref[cut, :], preferred_element_type=jnp.float32)
+            dnorm_part = jnp.dot(dpre, w_in_t_ref[cut, :], preferred_element_type=jnp.float32)
+            mlp = mlp_part if mlp is None else mlp + mlp_part
+            dnorm = dnorm_part if dnorm is None else dnorm + dnorm_part
+        out_ref[at, :] = (x_ref[at, :].astype(jnp.float32) + scale * (mlp + bias_out)).astype(jnp.bfloat16)
+        dnorm = dnorm * gain
+        first_mean = jnp.sum(dnorm, axis=-1, keepdims=True) * (1.0 / chans)
+        second_mean = jnp.sum(dnorm * nhat, axis=-1, keepdims=True) * (1.0 / chans)
+        dconv_ref[at, :] = (inv * (dnorm - first_mean - nhat * second_mean)).astype(jnp.bfloat16)
+        return carry
+
+    lax.fori_loop(0, conv_ref.shape[0] // chunk, one, 0)
+
+
+def join_kernel(grad_ref, cot_ref, top_ref, bot_ref, left_ref, right_ref, out_ref, total):
+    rows, width, chans = grad_ref.shape[1:]
+    total[...] = grad_ref[0]
+    total[pl.ds(0, DEPTH)] += top_ref[0].astype(jnp.float32)
+    total[pl.ds(rows - DEPTH, DEPTH)] += bot_ref[0].astype(jnp.float32)
+    total[:, pl.ds(0, SUB), :] += left_ref[0].astype(jnp.float32)
+    total[:, pl.ds(width - SUB, SUB), :] += right_ref[0].astype(jnp.float32)
+
+    def one(row, carry):
+        conv_grad = total[row].astype(jnp.bfloat16).astype(jnp.float32)
+        out_ref[0, row] = (cot_ref[0, row].astype(jnp.float32) + conv_grad).astype(jnp.bfloat16)
+        return carry
+
+    lax.fori_loop(0, rows, one, 0)
+
+
+def by_slot(shape):
+    return pl.BlockSpec((1,) + tuple(shape[1:]), lambda s: (s,) + (0,) * (len(shape) - 1))
+
+
+def whole(shape):
+    return pl.BlockSpec(tuple(shape), lambda s: (0,) * len(shape))
+
+
+def params():
+    return pltpu.CompilerParams(vmem_limit_bytes=56 * 1024 * 1024)
+
+
+def conv_forward(fields, top, bot, left, right, weights):
+    slots, rows, width, chans = fields.shape
+    ins = (fields, top, bot, left, right)
+    return pl.pallas_call(
+        conv_forward_kernel,
+        grid=(slots,),
+        in_specs=[by_slot(x.shape) for x in ins] + [whole(weights.shape)],
+        out_specs=by_slot(fields.shape),
+        out_shape=jax.ShapeDtypeStruct(fields.shape, jnp.float32),
+        scratch_shapes=[
+            pltpu.VMEM((chans // LANES, rows + 2 * DEPTH, width + 2 * SUB, LANES), jnp.float32)
+        ],
+        compiler_params=params(),
+        name="conv_forward",
+    )(*ins, weights)
+
+
+def conv_backward(dconv, top, bot, weights):
+    slots, rows, width, chans = dconv.shape
+    ins = (dconv, top, bot)
+    outs = [
+        (slots, rows, width, chans),
+        (slots, rows, SUB, chans),
+        (slots, rows, SUB, chans),
+        (slots, DEPTH, width, chans),
+        (slots, DEPTH, width, chans),
+    ]
+    return pl.pallas_call(
+        conv_backward_kernel,
+        grid=(slots,),
+        in_specs=[by_slot(x.shape) for x in ins] + [whole(weights.shape)],
+        out_specs=[by_slot(s) for s in outs],
+        out_shape=[jax.ShapeDtypeStruct(s, jnp.float32) for s in outs],
+        scratch_shapes=[
+            pltpu.VMEM((chans // LANES, rows + 2 * DEPTH, width + 4 * SUB, LANES), jnp.float32)
+        ],
+        compiler_params=params(),
+        name="conv_backward",
+    )(*ins, weights)
+
+
+def cell_block(conv, fields, cotangent, vectors, bias_in, proj_in, proj_out):
+    cells, chans = conv.shape
+    block, chunk = 1024, 256
+    tiled = pl.BlockSpec((block, chans), lambda s: (s, 0))
+    rest = (vectors, bias_in, proj_in, proj_out, proj_out.T, proj_in.T)
+    out = jax.ShapeDtypeStruct(conv.shape, jnp.bfloat16)
+    return pl.pallas_call(
+        functools.partial(cell_kernel, chunk=chunk),
+        grid=(cells // block,),
+        in_specs=[tiled] * 3 + [whole(x.shape) for x in rest],
+        out_specs=[tiled, tiled],
+        out_shape=[out, out],
+        compiler_params=params(),
+        name="cell_block",
+    )(conv, fields, cotangent, *rest)
+
+
+def join(grad, cotangent, top, bot, left, right):
+    ins = (grad, cotangent, top, bot, left, right)
+    return pl.pallas_call(
+        join_kernel,
+        grid=(grad.shape[0],),
+        in_specs=[by_slot(x.shape) for x in ins],
+        out_specs=by_slot(grad.shape),
+        out_shape=jax.ShapeDtypeStruct(grad.shape, jnp.bfloat16),
+        scratch_shapes=[pltpu.VMEM(grad.shape[1:], jnp.float32)],
+        compiler_params=params(),
+        name="join",
+    )(*ins)
+
+
+def face_all(blocks):
+    groups = lax.axis_size("face")
+    parts = [blocks]
+    for step in range(1, groups):
+        parts.append(lax.ppermute(blocks, "face", [(g, (g + step) % groups) for g in range(groups)]))
+    return jnp.concatenate(parts, axis=0)
+
+
+def exchange(ends, sides, index, flip):
+    slots, _, width, chans = ends.shape
+    tiles, groups = lax.axis_size("tile"), lax.axis_size("face")
+    tile, group = lax.axis_index("tile"), lax.axis_index("face")
+    rows = width // tiles
+    send = jnp.moveaxis(ends.reshape(slots, DEPTH, tiles, rows, chans), 2, 0)
+    got = lax.all_to_all(send, "tile", split_axis=0, concat_axis=0, tiled=True)
+    rims = jnp.concatenate([jnp.stack([got[0], got[tiles - 1]], axis=1), sides], axis=1)
+    strips = face_all(rims.reshape(slots * 4, DEPTH, rows, chans))
+    per_group = slots * 4
+    place = ((group - index // per_group) % groups) * per_group + index % per_group
+    picked = jnp.take(strips, place.reshape(-1), axis=0).reshape(slots, 4, DEPTH, rows, chans)
+    half = tiles // 2
+    back = jnp.stack([picked[:, 0]] * half + [picked[:, 1]] * (tiles - half))
+    back = lax.all_to_all(back, "tile", split_axis=0, concat_axis=0, tiled=True)
+    end_flip = jnp.where(tile == 0, flip[:, 0], flip[:, 1])[:, None, None, None]
+    new_ends = jnp.moveaxis(back, 0, 2).reshape(slots, DEPTH, width, chans)
+    new_ends = jnp.where(end_flip, new_ends[:, :, ::-1], new_ends)
+    mirrored = lax.ppermute(picked[:, 2:], "tile", [(t, tiles - 1 - t) for t in range(tiles)])
+    new_sides = jnp.where(flip[:, 2:, None, None, None], mirrored[:, :, :, ::-1], picked[:, 2:])
+    return new_ends, new_sides
+
+
+def halo(first, last):
+    tiles = lax.axis_size("tile")
+    above = lax.ppermute(last, "tile", [(t, t + 1) for t in range(tiles - 1)])
+    below = lax.ppermute(first, "tile", [(t + 1, t) for t in range(tiles - 1)])
+    return above, below
+
+
+def row_shards(
+    fields,
+    cotangent,
+    dw_kernel,
+    dw_bias,
+    norm_gain,
+    norm_bias,
+    proj_in,
+    bias_in,
+    proj_out,
+    bias_out,
+    layer_scale,
+    strip_source,
+    strip_flip,
+):
+    slots, rows, width, chans = fields.shape
+    tiles = lax.axis_size("tile")
+    tile = lax.axis_index("tile")
+    first_tile, last_tile = tile == 0, tile == tiles - 1
+    own_samples = lax.axis_index("face") * slots + jnp.arange(slots, dtype=jnp.int32)
+    source, mirror = reader_tables(own_samples, strip_source, strip_flip)
+    entries = jnp.arange(48, dtype=jnp.int32)
+    hits = strip_source[None, :] == entries[:, None]
+    reader_of = jnp.sum(jnp.where(hits, entries[None, :], 0), axis=1)
+    flip_of = jnp.sum(jnp.where(hits, strip_flip[None, :], 0), axis=1)
+    own_strips = (own_samples % 12)[:, None] * 4 + jnp.arange(4, dtype=jnp.int32)[None, :]
+    target = (own_samples // 12)[:, None] * 48 + reader_of[own_strips]
+    target_mirror = flip_of[own_strips] == 1
+
+    taps = jnp.concatenate([dw_kernel, dw_bias[:, None]], axis=1).T
+    taps = lax.all_to_all(
+        jnp.broadcast_to(taps[None], (tiles,) + taps.shape), "tile", split_axis=0, concat_axis=0, tiled=True
+    )
+    taps = jnp.moveaxis(taps, 0, 1).reshape(TAPS * TAPS + 1, chans)
+    taps = jnp.pad(taps, ((0, 6), (0, 0)))
+    weights = jnp.moveaxis(taps.reshape(-1, chans // LANES, LANES), 1, 0)
+    turned = jnp.pad(weights[:, TAPS * TAPS - 1 :: -1], ((0, 0), (0, 7), (0, 0)))
+
+    ends = jnp.where(first_tile, fields[:, :DEPTH], fields[:, : rows - DEPTH - 1 : -1])
+    side_pair = jnp.stack([fields[:, :, :DEPTH], fields[:, :, : width - DEPTH - 1 : -1]], axis=1)
+    sides = jnp.swapaxes(side_pair, 2, 3)
+    above, below = halo(fields[:, :DEPTH], fields[:, rows - DEPTH :])
+    new_ends, new_sides = exchange(ends, sides, source, mirror)
+    side_above, side_below = halo(new_sides[:, :, :, :DEPTH], new_sides[:, :, :, rows - DEPTH :])
+    tall = jnp.swapaxes(jnp.concatenate([side_above, new_sides, side_below], axis=3), 2, 3)
+    left = jnp.pad(tall[:, 0, :, ::-1], ((0, 0), (0, 0), (SUB - DEPTH, 0), (0, 0)))
+    right = jnp.pad(tall[:, 1], ((0, 0), (0, 0), (0, SUB - DEPTH), (0, 0)))
+    top = jnp.where(first_tile, new_ends[:, ::-1], above)
+    bot = jnp.where(last_tile, new_ends, below)
+    conv = conv_forward(fields, top, bot, left, right, weights)
+    vectors = jnp.stack([norm_gain, norm_bias, bias_out, layer_scale])
+    flat = (-1, chans)
+    section_out, dconv = cell_block(
+        conv.reshape(flat), fields.reshape(flat), cotangent.reshape(flat), vectors, bias_in[None], proj_in, proj_out
+    )
+    dconv = dconv.reshape(fields.shape)
+    above, below = halo(dconv[:, :DEPTH], dconv[:, rows - DEPTH :])
+    grad, left, right, top, bot = conv_backward(dconv, above, below, turned)
+    ends = jnp.where(first_tile, top, bot).astype(jnp.bfloat16)
+    sides = jnp.stack([left[:, :, : SUB - DEPTH - 1 : -1], right[:, :, :DEPTH]], axis=1).astype(jnp.bfloat16)
+    ends, sides = exchange(ends, jnp.swapaxes(sides, 2, 3), target, target_mirror)
+    top = jnp.where(first_tile, ends, 0)
+    bot = jnp.where(last_tile, ends[:, ::-1], 0)
+    sides = jnp.swapaxes(sides, 2, 3)
+    left = jnp.pad(sides[:, 0], ((0, 0), (0, 0), (0, SUB - DEPTH), (0, 0)))
+    right = jnp.pad(sides[:, 1, :, ::-1], ((0, 0), (0, 0), (SUB - DEPTH, 0), (0, 0)))
+    field_grad = join(grad, cotangent, top, bot, left, right)
+    return (section_out.reshape(fields.shape), field_grad)
+
+
+def block_of(fields, *rest):
+    rows, chans = fields.shape[1], fields.shape[3]
+    if rows % SUB == 0 and chans % LANES == 0 and fields.shape[2] % (2 * LANES // 2) == 0:
+        return row_shards(fields, *rest)
+    return shards(fields, *rest)
+
 
 def solution(mesh):
     placed = (
@@ -189,7 +553,7 @@
         P(),
     )
     return jax.shard_map(
-        shards,
+        block_of,
         mesh=mesh,
         in_specs=placed,
         out_specs=(P("face", "tile", None, None), P("face", "tile", None, None)),

time: 926 us -> 303 us (0.33); the launches traced: 908 us -> 302 us
  local copies, waits for them, and re-layouts: 408 us -> 35.1 us
  matrix products: 234 us -> 0 us
  Pallas kernels: 0 us -> 127 us
  other arithmetic: 85.1 us -> 12.3 us
  starting transfers between devices: 13.7 us -> 59.4 us
  blocking collectives: 43 us -> 0 us
  waiting for transfers between devices: 109 us -> 67.3 us
  between operations: 15 us -> 1.16 us
    conv_general_dilated x2 -> x0, matrix products: 181 us -> none  [grouped_conv(): lax.conv_general_dilated(planes_wide, taps.reshape(chans, 1, 7, 7), (1, 1...]
    pallas_call x0 -> x4, Pallas kernels: none -> 127 us  [the longest x1 48.5 us: conv_backward(): pl.pallas_call(conv_backward_kernel, grid=(slots,), in_specs=[by_slot(x.s...]
    conv_general_dilated x8 -> x0, local copies, waits for them, and re-layouts: 105 us -> none  [grouped_conv(): lax.conv_general_dilated(planes_wide, taps.reshape(chans, 1, 7, 7), (1, 1...]
    scatter-add x2 -> x0, local copies, waits for them, and re-layouts: 99.8 us -> none  [the longest x1 67.9 us: shards(): interior = interior.at[:, :, size - 3:, :].add(owned[:, 1][:, :, ::-1, :])]
    all_to_all x3 -> x5, waiting for transfers between devices: 81.2 us -> 19.7 us  [the longest x2 11.7 us: exchange(): got = lax.all_to_all(send, 'tile', split_axis=0, concat_axis=0, tiled=True)]
    dot_general x4 -> x0, matrix products: 53 us -> none  [the longest x1 25.1 us: shards(): lax.dot_general(dpre, proj_in, (((1,), (1,)), ((), ())), preferred_elemen...]
    ppermute x0 -> x14, waiting for transfers between devices: none -> 47.6 us  [the longest x6 45.4 us: face_all(): lax.ppermute(blocks, 'face', [(g, (g + step) % groups) for g in range(gro...]
    slice x5 -> x13, local copies, waits for them, and re-layouts: 51.8 us -> 5.11 us  [the longest x1 1.34 us: row_shards(): above, below = halo(dconv[:, :DEPTH], dconv[:, rows - DEPTH:])]
  transfers between devices with their start and end apart: 5 -> 19, of which waited for: 4 -> 9; matrix products, arithmetic and copies ran while one was open for 21% -> 12% of each run, Pallas kernels for 0% -> 0%
where the time goes in v1:
time: 303 us; the launch traced here: 302 us
  Pallas kernels  127 us (42%)
  waiting for transfers between devices  67.3 us (22%)
  starting transfers between devices  59.4 us (20%)
  local copies, waits for them, and re-layouts  35.1 us (12%)
  other arithmetic  12.3 us (4%)
    pallas_call x1, Pallas kernels, conv_backward(): pl.pallas_call(conv_backward_kernel, grid=(slots,), in_specs=[by_slot(x.s...  48.5 us
    ppermute x6, waiting for transfers between devices, face_all(): lax.ppermute(blocks, 'face', [(g, (g + step) % groups) for g in range(gro...  45.4 us
    pallas_call x1, Pallas kernels, cell_block(): pl.pallas_call(functools.partial(cell_kernel, chunk=chunk), grid=(cells /...  39.5 us
    pallas_call x1, Pallas kernels, conv_forward(): pl.pallas_call(conv_forward_kernel, grid=(slots,), in_specs=[by_slot(x.sh...  31.7 us
    all_to_all x2, starting transfers between devices, exchange(): got = lax.all_to_all(send, 'tile', split_axis=0, concat_axis=0, tiled=True)  19.6 us
    unnamed x50, local copies, waits for them, and re-layouts  13.7 us
    all_to_all x2, waiting for transfers between devices, exchange(): got = lax.all_to_all(send, 'tile', split_axis=0, concat_axis=0, tiled=True)  11.7 us
    ppermute x3, starting transfers between devices, halo(): above = lax.ppermute(last, 'tile', [(t, t + 1) for t in range(tiles - 1)])  11.5 us
  transfers between devices with their start and end apart: 19, of which 9 were waited for; matrix products, arithmetic and copies ran while one was open for 12% of the time, Pallas kernels for 0%

profile of v1, /device:TPU:0, one launch (start us, length us, event | category | flops | bytes accessed | tf_op | source)
XLA Modules:
  0.0 302.0 jit_solution(8427612795136207683)
XLA Ops:
  0.6 1.1 slice.101
  1.7 3.2 %collective-permute-start.3 = (bf16[3,3,128,256]{3,2,1,0:T(8,128)(2,1)S(1)}, bf16[3,3,128,256]{3,2,1,0:T(8,128)(2,1)}, u32[]{:S(2)}, u32[]{:S(2)}) collective-permute-start(bf16[3,3,128,256]{3,2,1,0:T(8,128)(2,1)S(1)} %slice.101), channel_id=1, source_target_pairs={{0,1},{1,2},{2,3},{3,4},{4,5},{5,6},{6,7},{8,9},{9,10},{10,11},{11... | collective-permute-start | bytes 1769480 | tf_op jit(solution)/shard_map/ppermute | solution.py:457
  4.9 1.3 reverse_select_fusion.2
  6.2 0.9 copy.103
  7.1 4.2 %all-to-all-start = ((bf16[8,3,3,16,256]{4,3,2,1,0:T(8,128)(2,1)}), bf16[8,3,3,16,256]{4,3,2,1,0:T(8,128)(2,1)S(1)}, u32[]{:S(2)}, u32[]{:S(2)}) async-start(bf16[8,3,3,16,256]{4,3,2,1,0:T(8,128)(2,1)} %bitcast.121), calls=%async_computation | async-start | bytes 1179648 | tf_op jit(solution)/shard_map/all_to_all | solution.py:438
  11.3 1.3 collective-permute-start.4
  12.9 0.7 gather_fusion.1
  13.5 0.7 gather_fusion
  14.2 0.7 gather_fusion.3
  15.2 1.1 fusion.27
  16.8 0.8 reshape.243
  17.6 4.1 %all-to-all-done = bf16[8,3,3,16,256]{4,3,2,1,0:T(8,128)(2,1)S(1)} async-done(((bf16[8,3,3,16,256]{4,3,2,1,0:T(8,128)(2,1)}), bf16[8,3,3,16,256]{4,3,2,1,0:T(8,128)(2,1)S(1)}, u32[]{:S(2)}, u32[]{:S(2)}) %all-to-all-start) | async-done | bytes 589856 | tf_op jit(solution)/shard_map/all_to_all | solution.py:438
  21.7 3.3 %all-to-all-start.2 = ((f32[8,1,1600]{2,1,0:T(1,128)}), f32[8,1,1600]{2,1,0:T(1,128)S(1)}, u32[]{:S(2)}, u32[]{:S(2)}) async-start(f32[8,1,1600]{2,1,0:T(1,128)} %reshape.243), calls=%async_computation.2 | async-start | bytes 106496 | tf_op jit(solution)/shard_map/all_to_all | solution.py:492
  25.1 3.8 %collective-permute-start.2 = (bf16[12,3,16,256]{3,2,1,0:T(8,128)(2,1)S(1)}, bf16[12,3,16,256]{3,2,1,0:T(8,128)(2,1)S(1)}, u32[]{:S(2)}, u32[]{:S(2)}) collective-permute-start(bf16[12,3,16,256]{3,2,1,0:T(8,128)(2,1)S(1)} %bitcast.156), channel_id=1, source_target_pairs={{0,24},{8,0},{16,8},{24,16},{1,25},{9,1},{17,9},{25,17},{2,26},{10... | collective-permute-start | bytes 884744 | tf_op jit(solution)/shard_map/ppermute | solution.py:428
  28.9 1.0 collective-permute-start
  30.4 5.9 %collective-permute-done.2 = bf16[12,3,16,256]{3,2,1,0:T(8,128)(2,1)S(1)} collective-permute-done((bf16[12,3,16,256]{3,2,1,0:T(8,128)(2,1)S(1)}, bf16[12,3,16,256]{3,2,1,0:T(8,128)(2,1)S(1)}, u32[]{:S(2)}, u32[]{:S(2)}) %collective-permute-start.2) | collective-permute-done | bytes 294944 | tf_op jit(solution)/shard_map/ppermute | solution.py:428
  36.3 18.3 %collective-permute-done.1 = bf16[12,3,16,256]{3,2,1,0:T(8,128)(2,1)S(1)} collective-permute-done((bf16[12,3,16,256]{3,2,1,0:T(8,128)(2,1)S(1)}, bf16[12,3,16,256]{3,2,1,0:T(8,128)(2,1)S(1)}, u32[]{:S(2)}, u32[]{:S(2)}) %collective-permute-start.1) | collective-permute-done | bytes 294944 | tf_op jit(solution)/shard_map/ppermute | solution.py:428
  54.6 1.1 pad_maximum_fusion
  56.4 0.6 fusion.3
  57.2 1.6 collective-permute-start.5
  60.0 0.6 fusion.4
  60.6 0.6 fusion.7
  61.3 0.6 fusion.6
  63.2 1.9 collective-permute-done.5
  65.3 3.7 %all-to-all-start.1 = ((bf16[8,3,3,16,256]{4,3,2,1,0:T(8,128)(2,1)}), bf16[8,3,3,16,256]{4,3,2,1,0:T(8,128)(2,1)S(1)}, u32[]{:S(2)}, u32[]{:S(2)}) async-start(bf16[8,3,3,16,256]{4,3,2,1,0:T(8,128)(2,1)} %fusion.8), calls=%async_computation.1 | async-start | bytes 1179648 | tf_op jit(solution)/shard_map/all_to_all | solution.py:446
  69.1 2.4 collective-permute-start.6
  71.5 1.3 collective-permute-start.7
  73.4 1.0 copy.76
  74.4 1.0 copy.75
  75.9 0.8 reduce.4
  76.9 0.7 copy.74
  78.3 0.8 pad.25.right_ref
  79.1 0.8 pad.24.left_ref
  79.9 0.7 rev.38
  80.7 2.1 broadcast_select_fusion.2
  82.7 1.0 reverse_select_fusion.1.top_ref
  83.7 31.7 %conv_forward.1 = f32[3,16,128,256]{3,2,1,0:T(8,128)} custom-call(bf16[3,16,128,256]{3,2,1,0:T(8,128)(2,1)} %x_ref.1, bf16[3,3,128,256]{3,2,1,0:T(8,128)(2,1)} %reverse_select_fusion.1.top_ref, bf16[3,3,128,256]{3,2,1,0:T(8,128)(2,1)} %get-tuple-element.23.bot_ref, bf16[3,22,8,256]{3,2,1,0:T(8,128)(2,1)} %pad.24.left_ref, ...), custom_call_target="tpu_custom_call" | custom-call | tf_op jit(solution)/shard_map/conv_forward/pallas_call | solution.py:355
  115.4 39.5 %cell_block.1 = (bf16[6144,256]{1,0:T(8,128)(2,1)}, bf16[6144,256]{1,0:T(8,128)(2,1)}) custom-call(f32[6144,256]{1,0:T(8,128)} %bitcast.125, bf16[6144,256]{1,0:T(8,128)(2,1)} %bitcast.126, bf16[6144,256]{1,0:T(8,128)(2,1)} %bitcast.127, f32[4,256]{1,0:T(4,128)} %pad_maximum_fusion.4.vec_ref, f32[1,1024]{1,0:T(1,128)} %bitcast.173, ...), custom_call_target="tpu_custom_call" | custom-call | tf_op jit(solution)/shard_map/cell_block/pallas_call | solution.py:399
  154.9 1.3 fusion.26
  156.3 1.4 collective-permute-start.9
  157.7 5.9 %collective-permute-start.8 = (bf16[3,3,128,256]{3,2,1,0:T(8,128)(2,1)S(1)}, bf16[3,3,128,256]{3,2,1,0:T(8,128)(2,1)S(1)}, u32[]{:S(2)}, u32[]{:S(2)}) collective-permute-start(bf16[3,3,128,256]{3,2,1,0:T(8,128)(2,1)S(1)} %get-tuple-element.28), channel_id=1, source_target_pairs={{0,1},{1,2},{2,3},{3,4},{4,5},{5,6},{6,7},{8,9},{9,10},{10,11},{11... | collective-permute-start | bytes 1769480 | tf_op jit(solution)/shard_map/ppermute | solution.py:457
  163.6 0.7 gather_fusion.2
  165.7 0.8 copy-done.5
  166.5 48.5 %conv_backward.1 = (f32[3,16,128,256]{3,2,1,0:T(8,128)}, f32[3,16,8,256]{3,2,1,0:T(8,128)}, f32[3,16,8,256]{3,2,1,0:T(8,128)}, f32[3,3,128,256]{3,2,1,0:T(8,128)}, f32[3,3,128,256]{3,2,1,0:T(8,128)}) custom-call(bf16[3,16,128,256]{3,2,1,0:T(8,128)(2,1)} %bitcast.129, bf16[3,3,128,256]{3,2,1,0:T(8,128)(2,1)} %copy-done.5, bf16[3,3,128,256]{3,2,1,0:T(8,128)(2,1)} %copy-done.4, ...), custom_call_target="tpu_custom_call" | custom-call | tf_op jit(solution)/shard_map/conv_backward/pallas_call | solution.py:379
  215.1 1.4 select_convert_fusion
  216.5 0.9 copy.102
  217.3 15.3 %all-to-all-start.3 = ((bf16[8,3,3,16,256]{4,3,2,1,0:T(8,128)(2,1)}), bf16[8,3,3,16,256]{4,3,2,1,0:T(8,128)(2,1)S(1)}, u32[]{:S(2)}, u32[]{:S(2)}) async-start(bf16[8,3,3,16,256]{4,3,2,1,0:T(8,128)(2,1)} %bitcast.120), calls=%async_computation.3 | async-start | bytes 1179648 | tf_op jit(solution)/shard_map/all_to_all | solution.py:438
  233.0 1.0 slice.121
  234.3 1.0 fusion
  235.5 7.6 %all-to-all-done.3 = bf16[8,3,3,16,256]{4,3,2,1,0:T(8,128)(2,1)S(1)} async-done(((bf16[8,3,3,16,256]{4,3,2,1,0:T(8,128)(2,1)}), bf16[8,3,3,16,256]{4,3,2,1,0:T(8,128)(2,1)S(1)}, u32[]{:S(2)}, u32[]{:S(2)}) %all-to-all-start.3) | async-done | bytes 589856 | tf_op jit(solution)/shard_map/all_to_all | solution.py:438
  243.7 2.9 collective-permute-start.11
  246.6 1.9 collective-permute-start.10
  248.6 3.2 %collective-permute-done.12 = bf16[12,3,16,256]{3,2,1,0:T(8,128)(2,1)S(1)} collective-permute-done((bf16[12,3,16,256]{3,2,1,0:T(8,128)(2,1)S(1)}, bf16[12,3,16,256]{3,2,1,0:T(8,128)(2,1)S(1)}, u32[]{:S(2)}, u32[]{:S(2)}) %collective-permute-start.12) | collective-permute-done | bytes 294944 | tf_op jit(solution)/shard_map/ppermute | solution.py:428
  251.7 18.1 %collective-permute-done.11 = bf16[12,3,16,256]{3,2,1,0:T(8,128)(2,1)S(1)} collective-permute-done((bf16[12,3,16,256]{3,2,1,0:T(8,128)(2,1)S(1)}, bf16[12,3,16,256]{3,2,1,0:T(8,128)(2,1)S(1)}, u32[]{:S(2)}, u32[]{:S(2)}) %collective-permute-start.11) | collective-permute-done | bytes 294944 | tf_op jit(solution)/shard_map/ppermute | solution.py:428
  270.6 0.6 fusion.11
  271.4 2.3 collective-permute-start.13
  278.1 3.7 %all-to-all-start.4 = ((bf16[8,3,3,16,256]{4,3,2,1,0:T(8,128)(2,1)}), bf16[8,3,3,16,256]{4,3,2,1,0:T(8,128)(2,1)S(1)}, u32[]{:S(2)}, u32[]{:S(2)}) async-start(bf16[8,3,3,16,256]{4,3,2,1,0:T(8,128)(2,1)} %fusion.16), calls=%async_computation.4 | async-start | bytes 1179648 | tf_op jit(solution)/shard_map/all_to_all | solution.py:446
  282.8 0.8 pad.29.right_ref
  283.6 0.7 pad.28.left_ref
  284.3 8.0 %all-to-all-done.4 = bf16[8,3,3,16,256]{4,3,2,1,0:T(8,128)(2,1)S(1)} async-done(((bf16[8,3,3,16,256]{4,3,2,1,0:T(8,128)(2,1)}), bf16[8,3,3,16,256]{4,3,2,1,0:T(8,128)(2,1)S(1)}, u32[]{:S(2)}, u32[]{:S(2)}) %all-to-all-start.4) | async-done | bytes 589856 | tf_op jit(solution)/shard_map/all_to_all | solution.py:446
  292.4 0.7 rev.44
  293.1 1.0 broadcast_select_fusion.3
  294.1 0.9 reverse_select_fusion.bot_ref
  295.0 7.0 %join.1 = bf16[3,16,128,256]{3,2,1,0:T(8,128)(2,1)} custom-call(f32[3,16,128,256]{3,2,1,0:T(8,128)} %get-tuple-element.12.grad_ref, bf16[3,16,128,256]{3,2,1,0:T(8,128)(2,1)} %cot_ref.1, bf16[3,3,128,256]{3,2,1,0:T(8,128)(2,1)} %get-tuple-element.19.top_ref, bf16[3,3,128,256]{3,2,1,0:T(8,128)(2,1)} %reverse_select_fusion.bot_ref, ...), custom_call_target="tpu_custom_call" | custom-call | tf_op jit(solution)/shard_map/join/pallas_call | solution.py:412
  (118 shorter events, 16.3 us)
Async XLA Ops:
  1.7 81.0 %collective-permute-start.3 = (bf16[3,3,128,256]{3,2,1,0:T(8,128)(2,1)S(1)}, bf16[3,3,128,256]{3,2,1,0:T(8,128)(2,1)}, u32[]{:S(2)}, u32[]{:S(2)}) collective-permute-start(bf16[3,3,128,256]{3,2,1,0:T(8,128)(2,1)S(1)} %slice.101), channel_id=1, source_target_pairs={{0,1},{1,2},{2,3},{3,4},{4,5},{5,6},{6,7},{8,9},{9,10},{10,11},{11... | collective-permute-start | bytes 1769480 | tf_op jit(solution)/shard_map/ppermute | solution.py:457
  6.2 6.6 %copy-start = (s32[48]{0:T(128)S(1)}, s32[48]{0:T(128)}, u32[]{:S(2)}) copy-start(s32[48]{0:T(128)} %param.26) | copy-start | bytes 580
  6.2 6.6 %copy-start.1 = (s32[48]{0:T(128)S(1)}, s32[48]{0:T(128)}, u32[]{:S(2)}) copy-start(s32[48]{0:T(128)} %param.27) | copy-start | bytes 580
  7.1 14.7 %all-to-all-start = ((bf16[8,3,3,16,256]{4,3,2,1,0:T(8,128)(2,1)}), bf16[8,3,3,16,256]{4,3,2,1,0:T(8,128)(2,1)S(1)}, u32[]{:S(2)}, u32[]{:S(2)}) async-start(bf16[8,3,3,16,256]{4,3,2,1,0:T(8,128)(2,1)} %bitcast.121), calls=%async_computation | async-start | bytes 1179648 | tf_op jit(solution)/shard_map/all_to_all | solution.py:438
  11.3 69.4 %collective-permute-start.4 = (bf16[3,3,128,256]{3,2,1,0:T(8,128)(2,1)S(1)}, bf16[3,3,128,256]{3,2,1,0:T(8,128)(2,1)}, u32[]{:S(2)}, u32[]{:S(2)}) collective-permute-start(bf16[3,3,128,256]{3,2,1,0:T(8,128)(2,1)S(1)} %get-tuple-element.30), channel_id=1, source_target_pairs={{1,0},{2,1},{3,2},{4,3},{5,4},{6,5},{7,6},{9,8},{10,9},{11,10},{12... | collective-permute-start | bytes 1769480 | tf_op jit(solution)/shard_map/ppermute | solution.py:458
  14.2 2.4 copy-start.12
  14.2 2.5 copy-start.7
  21.7 43.6 %all-to-all-start.2 = ((f32[8,1,1600]{2,1,0:T(1,128)}), f32[8,1,1600]{2,1,0:T(1,128)S(1)}, u32[]{:S(2)}, u32[]{:S(2)}) async-start(f32[8,1,1600]{2,1,0:T(1,128)} %reshape.243), calls=%async_computation.2 | async-start | bytes 106496 | tf_op jit(solution)/shard_map/all_to_all | solution.py:492
  25.1 11.2 %collective-permute-start.2 = (bf16[12,3,16,256]{3,2,1,0:T(8,128)(2,1)S(1)}, bf16[12,3,16,256]{3,2,1,0:T(8,128)(2,1)S(1)}, u32[]{:S(2)}, u32[]{:S(2)}) collective-permute-start(bf16[12,3,16,256]{3,2,1,0:T(8,128)(2,1)S(1)} %bitcast.156), channel_id=1, source_target_pairs={{0,24},{8,0},{16,8},{24,16},{1,25},{9,1},{17,9},{25,17},{2,26},{10... | collective-permute-start | bytes 884744 | tf_op jit(solution)/shard_map/ppermute | solution.py:428
  28.9 25.7 %collective-permute-start.1 = (bf16[12,3,16,256]{3,2,1,0:T(8,128)(2,1)S(1)}, bf16[12,3,16,256]{3,2,1,0:T(8,128)(2,1)S(1)}, u32[]{:S(2)}, u32[]{:S(2)}) collective-permute-start(bf16[12,3,16,256]{3,2,1,0:T(8,128)(2,1)S(1)} %bitcast.157), channel_id=1, source_target_pairs={{0,16},{8,24},{16,0},{24,8},{1,17},{9,25},{17,1},{25,9},{2,18},{10... | collective-permute-start | bytes 884744 | tf_op jit(solution)/shard_map/ppermute | solution.py:428
  28.9 25.7 %collective-permute-start = (bf16[12,3,16,256]{3,2,1,0:T(8,128)(2,1)S(1)}, bf16[12,3,16,256]{3,2,1,0:T(8,128)(2,1)}, u32[]{:S(2)}, u32[]{:S(2)}) collective-permute-start(bf16[12,3,16,256]{3,2,1,0:T(8,128)(2,1)S(1)} %bitcast.158), channel_id=1, source_target_pairs={{0,8},{8,16},{16,24},{24,0},{1,9},{9,17},{17,25},{25,1},{2,10},{10... | collective-permute-start | bytes 884744 | tf_op jit(solution)/shard_map/ppermute | solution.py:428
  57.2 7.9 %collective-permute-start.5 = (bf16[3,2,3,16,256]{4,2,3,0,1:T(4,128)(2,1)S(1)}, bf16[3,2,3,16,256]{4,2,3,0,1:T(4,128)(2,1)S(1)}, u32[]{:S(2)}, u32[]{:S(2)}) collective-permute-start(bf16[3,2,3,16,256]{4,2,3,0,1:T(4,128)(2,1)S(1)} %copy.90), channel_id=1, source_target_pairs={{0,7},{1,6},{2,5},{3,4},{4,3},{5,2},{6,1},{7,0},{8,15},{9,14},{10,... | collective-permute-start | bytes 442376 | tf_op jit(solution)/shard_map/ppermute | solution.py:450
  61.3 11.5 %copy-start.8 = (f32[256]{0:T(256)S(1)}, f32[256]{0:T(256)}, u32[]{:S(2)}) copy-start(f32[256]{0:T(256)} %param.25) | copy-start | bytes 3076
  61.3 11.5 %copy-start.9 = (f32[256]{0:T(256)S(1)}, f32[256]{0:T(256)}, u32[]{:S(2)}) copy-start(f32[256]{0:T(256)} %param.24) | copy-start | bytes 3076
  61.3 11.5 %copy-start.10 = (f32[256]{0:T(256)S(1)}, f32[256]{0:T(256)}, u32[]{:S(2)}) copy-start(f32[256]{0:T(256)} %param.20) | copy-start | bytes 3076
  61.3 11.5 %copy-start.11 = (f32[256]{0:T(256)S(1)}, f32[256]{0:T(256)}, u32[]{:S(2)}) copy-start(f32[256]{0:T(256)} %param.19) | copy-start | bytes 3076
  61.3 12.1 %copy-start.2 = (bf16[256,1024]{1,0:T(8,128)(2,1)S(1)}, bf16[256,1024]{1,0:T(8,128)(2,1)}, u32[]{:S(2)}) copy-start(bf16[256,1024]{1,0:T(8,128)(2,1)} %w_in_ref.1) | copy-start | bytes 1572868
  65.3 9.1 %copy-start.3 = (bf16[1024,256]{1,0:T(8,128)(2,1)S(1)}, bf16[1024,256]{1,0:T(8,128)(2,1)}, u32[]{:S(2)}) copy-start(bf16[1024,256]{1,0:T(8,128)(2,1)} %w_out_ref.1) | copy-start | bytes 1572868
  65.3 14.5 %all-to-all-start.1 = ((bf16[8,3,3,16,256]{4,3,2,1,0:T(8,128)(2,1)}), bf16[8,3,3,16,256]{4,3,2,1,0:T(8,128)(2,1)S(1)}, u32[]{:S(2)}, u32[]{:S(2)}) async-start(bf16[8,3,3,16,256]{4,3,2,1,0:T(8,128)(2,1)} %fusion.8), calls=%async_computation.1 | async-start | bytes 1179648 | tf_op jit(solution)/shard_map/all_to_all | solution.py:446
  69.1 8.6 %collective-permute-start.6 = (bf16[3,2,3,3,256]{4,2,3,0,1:T(4,128)(2,1)S(1)}, bf16[3,2,3,3,256]{4,2,3,0,1:T(4,128)(2,1)S(1)}, u32[]{:S(2)}, u32[]{:S(2)}) collective-permute-start(bf16[3,2,3,3,256]{4,2,3,0,1:T(4,128)(2,1)S(1)} %get-tuple-element.41), channel_id=1, source_target_pairs={{0,1},{1,2},{2,3},{3,4},{4,5},{5,6},{6,7},{8,9},{9,10},{10,11},{11... | collective-permute-start | bytes 82952 | tf_op jit(solution)/shard_map/ppermute | solution.py:457
  71.5 6.2 %collective-permute-start.7 = (bf16[3,2,3,3,256]{4,2,3,0,1:T(4,128)(2,1)S(1)}, bf16[3,2,3,3,256]{4,2,3,0,1:T(4,128)(2,1)S(1)}, u32[]{:S(2)}, u32[]{:S(2)}) collective-permute-start(bf16[3,2,3,3,256]{4,2,3,0,1:T(4,128)(2,1)S(1)} %get-tuple-element.42), channel_id=1, source_target_pairs={{1,0},{2,1},{3,2},{4,3},{5,4},{6,5},{7,6},{9,8},{10,9},{11,10},{12... | collective-permute-start | bytes 82952 | tf_op jit(solution)/shard_map/ppermute | solution.py:458
  156.3 8.0 %copy-start.6 = (f32[56,2,128]{2,0,1:T(8,128)S(1)}, f32[56,2,128]{2,0,1:T(8,128)}, u32[]{:S(2)}) copy-start(f32[56,2,128]{2,0,1:T(8,128)} %copy.74) | copy-start | bytes 172036
  156.3 8.6 %collective-permute-start.9 = (bf16[3,3,128,256]{3,2,1,0:T(8,128)(2,1)S(1)}, bf16[3,3,128,256]{3,2,1,0:T(8,128)(2,1)S(1)}, u32[]{:S(2)}, u32[]{:S(2)}) collective-permute-start(bf16[3,3,128,256]{3,2,1,0:T(8,128)(2,1)S(1)} %get-tuple-element.27), channel_id=1, source_target_pairs={{1,0},{2,1},{3,2},{4,3},{5,4},{6,5},{7,6},{9,8},{10,9},{11,10},{12... | collective-permute-start | bytes 1769480 | tf_op jit(solution)/shard_map/ppermute | solution.py:458
  157.7 7.5 %collective-permute-start.8 = (bf16[3,3,128,256]{3,2,1,0:T(8,128)(2,1)S(1)}, bf16[3,3,128,256]{3,2,1,0:T(8,128)(2,1)S(1)}, u32[]{:S(2)}, u32[]{:S(2)}) collective-permute-start(bf16[3,3,128,256]{3,2,1,0:T(8,128)(2,1)S(1)} %get-tuple-element.28), channel_id=1, source_target_pairs={{0,1},{1,2},{2,3},{3,4},{4,5},{5,6},{6,7},{8,9},{9,10},{10,11},{11... | collective-permute-start | bytes 1769480 | tf_op jit(solution)/shard_map/ppermute | solution.py:457
  164.9 0.8 copy-start.4
  165.7 0.8 copy-start.5
  217.3 25.8 %all-to-all-start.3 = ((bf16[8,3,3,16,256]{4,3,2,1,0:T(8,128)(2,1)}), bf16[8,3,3,16,256]{4,3,2,1,0:T(8,128)(2,1)S(1)}, u32[]{:S(2)}, u32[]{:S(2)}) async-start(bf16[8,3,3,16,256]{4,3,2,1,0:T(8,128)(2,1)} %bitcast.120), calls=%async_computation.3 | async-start | bytes 1179648 | tf_op jit(solution)/shard_map/all_to_all | solution.py:438
  243.6 8.1 %collective-permute-start.12 = (bf16[12,3,16,256]{3,2,1,0:T(8,128)(2,1)S(1)}, bf16[12,3,16,256]{3,2,1,0:T(8,128)(2,1)S(1)}, u32[]{:S(2)}, u32[]{:S(2)}) collective-permute-start(bf16[12,3,16,256]{3,2,1,0:T(8,128)(2,1)S(1)} %bitcast.160), channel_id=1, source_target_pairs={{0,24},{8,0},{16,8},{24,16},{1,25},{9,1},{17,9},{25,17},{2,26},{10... | collective-permute-start | bytes 884744 | tf_op jit(solution)/shard_map/ppermute | solution.py:428
  243.7 26.1 %collective-permute-start.11 = (bf16[12,3,16,256]{3,2,1,0:T(8,128)(2,1)S(1)}, bf16[12,3,16,256]{3,2,1,0:T(8,128)(2,1)S(1)}, u32[]{:S(2)}, u32[]{:S(2)}) collective-permute-start(bf16[12,3,16,256]{3,2,1,0:T(8,128)(2,1)S(1)} %bitcast.161), channel_id=1, source_target_pairs={{0,16},{8,24},{16,0},{24,8},{1,17},{9,25},{17,1},{25,9},{2,18},{10... | collective-permute-start | bytes 884744 | tf_op jit(solution)/shard_map/ppermute | solution.py:428
  246.6 23.2 %collective-permute-start.10 = (bf16[12,3,16,256]{3,2,1,0:T(8,128)(2,1)S(1)}, bf16[12,3,16,256]{3,2,1,0:T(8,128)(2,1)S(1)}, u32[]{:S(2)}, u32[]{:S(2)}) collective-permute-start(bf16[12,3,16,256]{3,2,1,0:T(8,128)(2,1)S(1)} %bitcast.162), channel_id=1, source_target_pairs={{0,8},{8,16},{16,24},{24,0},{1,9},{9,17},{17,25},{25,1},{2,10},{10... | collective-permute-start | bytes 884744 | tf_op jit(solution)/shard_map/ppermute | solution.py:428
  271.4 10.9 %collective-permute-start.13 = (bf16[3,2,3,16,256]{4,2,3,0,1:T(4,128)(2,1)S(1)}, bf16[3,2,3,16,256]{4,2,3,0,1:T(4,128)(2,1)S(1)}, u32[]{:S(2)}, u32[]{:S(2)}) collective-permute-start(bf16[3,2,3,16,256]{4,2,3,0,1:T(4,128)(2,1)S(1)} %copy.94), channel_id=1, source_target_pairs={{0,7},{1,6},{2,5},{3,4},{4,3},{5,2},{6,1},{7,0},{8,15},{9,14},{10,... | collective-permute-start | bytes 442376 | tf_op jit(solution)/shard_map/ppermute | solution.py:450
  278.1 14.2 %all-to-all-start.4 = ((bf16[8,3,3,16,256]{4,3,2,1,0:T(8,128)(2,1)}), bf16[8,3,3,16,256]{4,3,2,1,0:T(8,128)(2,1)S(1)}, u32[]{:S(2)}, u32[]{:S(2)}) async-start(bf16[8,3,3,16,256]{4,3,2,1,0:T(8,128)(2,1)} %fusion.16), calls=%async_computation.4 | async-start | bytes 1179648 | tf_op jit(solution)/shard_map/all_to_all | solution.py:446

commit v2 on v0

--- a/solution.py
+++ b/solution.py
@@ -1,6 +1,8 @@
 import jax
 import jax.numpy as jnp
 from jax import lax
+from jax.experimental import pallas as pl
+from jax.experimental.pallas import tpu as pltpu
 from jax.sharding import PartitionSpec as P
 
 EPSILON = 1e-06
@@ -171,6 +173,634 @@
     )
     return (section_out.reshape(fields.shape), field_grad)
 
+DEPTH = 3
+TAPS = 7
+SUB = 8
+LANES = 128
+SIDE = 16
+
+
+def load_taps(w, half, q):
+    return [w[half, pl.ds(TAPS * p + q, 1), :] for p in range(TAPS)]
+
+
+def plus(total, part):
+    return part if total is None else total + part
+
+
+def widen_rows(xs, at, ref, rows, lead):
+    width = ref.shape[2]
+    for half in range(ref.shape[3] // LANES):
+        lanes = pl.ds(half * LANES, LANES)
+
+        def one(row, carry):
+            xs[half, at + row, pl.ds(lead, width), :] = ref[0, row, :, lanes].astype(jnp.float32)
+            return carry
+
+        if rows > DEPTH:
+            lax.fori_loop(0, rows, one, 0)
+        else:
+            for row in range(rows):
+                one(row, 0)
+
+
+def clear_pads(xs, width):
+    halves, rows = xs.shape[:2]
+    for half in range(halves):
+        xs[half, :, pl.ds(0, SUB), :] = jnp.zeros((rows, SUB, LANES), jnp.float32)
+        xs[half, :, pl.ds(SUB + width, SUB), :] = jnp.zeros((rows, SUB, LANES), jnp.float32)
+
+
+def conv_partial_kernel(x_ref, w_ref, out_ref, xs):
+    rows, width, chans = x_ref.shape[1:]
+    clear_pads(xs, width)
+    widen_rows(xs, 0, x_ref, rows, SUB)
+    wide = 2
+    for half in range(chans // LANES):
+        lanes = pl.ds(half * LANES, LANES)
+
+        def one(block, carry):
+            start = pl.multiple_of(block * (SUB * wide), SUB * wide)
+            acc = [[None] * rows for _ in range(wide)]
+            for q in range(TAPS):
+                taps = load_taps(w_ref, half, q)
+                for row in range(rows):
+                    for b in range(wide):
+                        x = xs[half, row, pl.ds(start + SUB * (b + 1) - DEPTH + q, SUB), :]
+                        for p in range(TAPS):
+                            i = row + DEPTH - p
+                            if 0 <= i < rows:
+                                acc[b][i] = plus(acc[b][i], x * taps[p])
+            bias = w_ref[half, pl.ds(TAPS * TAPS, 1), :]
+            for b in range(wide):
+                for i in range(rows):
+                    out_ref[0, i, pl.ds(start + SUB * b, SUB), lanes] = acc[b][i] + bias
+            return carry
+
+        lax.fori_loop(0, width // (SUB * wide), one, 0)
+
+
+def row_parts(xh, w, half, col):
+    head = [None] * DEPTH
+    tail = [None] * DEPTH
+    for q in range(TAPS):
+        for h in range(DEPTH):
+            up = xh[half, h, pl.ds(col + SUB - DEPTH + q, SUB), :]
+            down = xh[half, DEPTH + h, pl.ds(col + SUB - DEPTH + q, SUB), :]
+            for i in range(h + 1):
+                head[i] = plus(head[i], up * w[half, pl.ds(TAPS * (h - i) + q, 1), :])
+            for k in range(DEPTH - h):
+                tail[k] = plus(tail[k], down * w[half, pl.ds(TAPS * (h + k + 4) + q, 1), :])
+    return head, tail
+
+
+def end_parts(xh, w, half, col, first):
+    out = [None] * DEPTH
+    for q in range(TAPS):
+        for h in range(DEPTH):
+            x = xh[half, jnp.where(first, h, 2 * DEPTH - 1 - h), pl.ds(col + SUB - DEPTH + q, SUB), :]
+            for d in range(h + 1):
+                p = jnp.where(first, h - d, TAPS - 1 - h + d)
+                out[d] = plus(out[d], x * w[half, pl.ds(TAPS * p + q, 1), :])
+    return out
+
+
+def column_parts(xc, w, half, starts):
+    rows = xc.shape[1] - 2 * DEPTH
+    acc = [None] * rows
+    for q, start in starts:
+        taps = load_taps(w, half, q)
+        for row in range(rows + 2 * DEPTH):
+            x = xc[half, row, pl.ds(start, SUB), :]
+            for p in range(TAPS):
+                if 0 <= row - p < rows:
+                    acc[row - p] = plus(acc[row - p], x * taps[p])
+    return acc
+
+
+def cells_of(cells, x, cot, vec, bias_in, w_in, w_out, w_out_t, w_in_t):
+    chans = cells.shape[1]
+    gain, shift, bias_out, scale = (vec[k : k + 1, :] for k in range(4))
+    hidden = w_in.shape[1]
+    piece = 256
+    cells = cells.astype(jnp.bfloat16).astype(jnp.float32)
+    mean = jnp.sum(cells, axis=-1, keepdims=True) * (1.0 / chans)
+    centred = cells - mean
+    inv = lax.rsqrt(jnp.sum(centred * centred, axis=-1, keepdims=True) * (1.0 / chans) + EPSILON)
+    nhat = centred * inv
+    normed = (nhat * gain + shift).astype(jnp.bfloat16)
+    dmix = (scale * cot.astype(jnp.float32)).astype(jnp.bfloat16)
+    mlp = None
+    dnorm = None
+    for first in range(0, hidden, piece):
+        cut = pl.ds(first, piece)
+        pre = jnp.dot(normed, w_in[:, cut], preferred_element_type=jnp.float32) + bias_in[0:1, cut]
+        dact = jnp.dot(dmix, w_out_t[:, cut], preferred_element_type=jnp.float32)
+        square = pre * pre
+        tanh_val = jnp.tanh(pre * (GELU_SCALE + (GELU_SCALE * GELU_CUBIC) * square))
+        lifted = 0.5 + 0.5 * tanh_val
+        act = (pre * lifted).astype(jnp.bfloat16)
+        bend = pre * ((0.5 * GELU_SCALE) + (1.5 * GELU_SCALE * GELU_CUBIC) * square)
+        slope = lifted + (1.0 - tanh_val * tanh_val) * bend
+        dpre = (dact * slope).astype(jnp.bfloat16)
+        mlp = plus(mlp, jnp.dot(act, w_out[cut, :], preferred_element_type=jnp.float32))
+        dnorm = plus(dnorm, jnp.dot(dpre, w_in_t[cut, :], preferred_element_type=jnp.float32))
+    section = (x.astype(jnp.float32) + scale * (mlp + bias_out)).astype(jnp.bfloat16)
+    dnorm = dnorm * gain
+    first_mean = jnp.sum(dnorm, axis=-1, keepdims=True) * (1.0 / chans)
+    second_mean = jnp.sum(dnorm * nhat, axis=-1, keepdims=True) * (1.0 / chans)
+    dconv = (inv * (dnorm - first_mean - nhat * second_mean)).astype(jnp.bfloat16)
+    return section, dconv
+
+
+def edge_kernel(
+    flags, cl, cr, ce, xl, xr, xe, gl, gr, ge, top, bot, left, right, w, wt, vec, bi, wi, wo, wot, wit,
+    sl, sr, se, dl, dr, de, tb, xh, xcl, xcr, lrs, ends,
+):
+    rows, chans = cl.shape[1], cl.shape[3]
+    width = top.shape[2]
+    inner = width - 2 * SIDE
+    mats = (vec, bi, wi, wo, wot, wit)
+    first = flags[0] == 1
+    clear_pads(xh, width)
+    widen_rows(xh, 0, top, DEPTH, SUB)
+    widen_rows(xh, DEPTH, bot, DEPTH, SUB)
+    for half in range(chans // LANES):
+        lanes = pl.ds(half * LANES, LANES)
+        xcl[half, :, pl.ds(0, SUB), :] = left[0, :, :, lanes].astype(jnp.float32)
+        xcl[half, :, pl.ds(SUB, SUB), :] = jnp.zeros((rows + 2 * DEPTH, SUB, LANES), jnp.float32)
+        xcr[half, :, pl.ds(0, SUB), :] = jnp.zeros((rows + 2 * DEPTH, SUB, LANES), jnp.float32)
+        xcr[half, :, pl.ds(SUB, SUB), :] = right[0, :, :, lanes].astype(jnp.float32)
+    lrs[0] = cl[0]
+    lrs[1] = cr[0]
+    for half in range(chans // LANES):
+        lanes = pl.ds(half * LANES, LANES)
+        near = column_parts(xcl, w, half, [(q, SUB - DEPTH + q) for q in range(DEPTH)])
+        far = column_parts(xcr, w, half, [(q, q - DEPTH) for q in range(4, TAPS)])
+        for i in range(rows):
+            lrs[0, i, pl.ds(0, SUB), lanes] += near[i]
+            lrs[1, i, pl.ds(SIDE - SUB, SUB), lanes] += far[i]
+        for side in range(2):
+            for b in range(0, SIDE, SUB):
+                head, tail = row_parts(xh, w, half, b + side * (width - SIDE))
+                for d in range(DEPTH):
+                    lrs[side, d, pl.ds(b, SUB), lanes] += head[d]
+                    lrs[side, rows - 1 - d, pl.ds(b, SUB), lanes] += tail[d]
+    flat = (2 * rows * SIDE, chans)
+    both = lambda a, b: jnp.stack([a[0], b[0]]).reshape(flat)
+    section, dconv = cells_of(lrs[...].reshape(flat), both(xl, xr), both(gl, gr), *mats)
+    section = section.reshape(2, rows, SIDE, chans)
+    dconv = dconv.reshape(2, rows, SIDE, chans)
+    sl[0] = section[0]
+    sr[0] = section[1]
+    dl[0] = dconv[0]
+    dr[0] = dconv[1]
+
+    @pl.when(flags[0] + flags[1] > 0)
+    def _():
+        at = [jnp.where(first, d, SUB - 1 - d) for d in range(DEPTH)]
+        whole_at = [jnp.where(first, d, rows - 1 - d) for d in range(DEPTH)]
+        mid = pl.ds(SIDE, inner)
+        for d in range(DEPTH):
+            ends[d] = ce[0, at[d], mid, :]
+        for half in range(chans // LANES):
+            lanes = pl.ds(half * LANES, LANES)
+
+            def one(block, carry):
+                start = pl.multiple_of(block * SUB, SUB)
+                parts = end_parts(xh, w, half, start + SIDE, first)
+                for d in range(DEPTH):
+                    ends[d, pl.ds(start, SUB), lanes] += parts[d]
+                return carry
+
+            lax.fori_loop(0, inner // SUB, one, 0)
+        rim = lambda ref: jnp.stack([ref[0, at[d], mid, :] for d in range(DEPTH)]).reshape(DEPTH * inner, chans)
+        section, dconv = cells_of(ends[...].reshape(DEPTH * inner, chans), rim(xe), rim(ge), *mats)
+        se[0] = section.reshape(DEPTH, inner, chans)
+        dconv = dconv.reshape(DEPTH, inner, chans)
+        de[0] = dconv
+        for half in range(chans // LANES):
+            lanes = pl.ds(half * LANES, LANES)
+            for d in range(DEPTH):
+                xh[half, d, pl.ds(SUB, SIDE), :] = dl[0, whole_at[d], :, lanes].astype(jnp.float32)
+                xh[half, d, pl.ds(SUB + SIDE, inner), :] = de[0, d, :, lanes].astype(jnp.float32)
+                xh[half, d, pl.ds(SUB + SIDE + inner, SIDE), :] = dr[0, whole_at[d], :, lanes].astype(jnp.float32)
+
+            def one_strip(block, carry):
+                start = pl.multiple_of(block * SUB, SUB)
+                out = [None] * DEPTH
+                for q in range(TAPS):
+                    for edge in range(DEPTH):
+                        x = xh[half, edge, pl.ds(start + SUB - DEPTH + q, SUB), :]
+                        for d in range(DEPTH - edge):
+                            p = jnp.where(first, edge + d + 4, 2 - edge - d)
+                            out[d] = plus(out[d], x * wt[half, pl.ds(TAPS * p + q, 1), :])
+                for d in range(DEPTH):
+                    xh[half, DEPTH + d, pl.ds(start + SUB, SUB), :] = out[d]
+                return carry
+
+            lax.fori_loop(0, width // SUB, one_strip, 0)
+            for d in range(DEPTH):
+                tb[0, d, :, lanes] = xh[half, DEPTH + d, pl.ds(SUB, width), :].astype(jnp.bfloat16)
+
+
+def strip_kernel(left, right, wt, near_ref, far_ref, xcl, xcr):
+    rows, chans = near_ref.shape[1], near_ref.shape[3]
+    for half in range(chans // LANES):
+        lanes = pl.ds(half * LANES, LANES)
+        zeros = jnp.zeros((rows + 2 * DEPTH, SUB, LANES), jnp.float32)
+        xcl[half, :, pl.ds(0, SUB), :] = zeros
+        xcl[half, :, pl.ds(SUB, SUB), :] = left[0, :, :, lanes].astype(jnp.float32)
+        xcr[half, :, pl.ds(0, SUB), :] = right[0, :, :, lanes].astype(jnp.float32)
+        xcr[half, :, pl.ds(SUB, SUB), :] = zeros
+    for half in range(chans // LANES):
+        lanes = pl.ds(half * LANES, LANES)
+        near = column_parts(xcl, wt, half, [(q, q - DEPTH) for q in range(4, TAPS)])
+        far = column_parts(xcr, wt, half, [(q, SUB - DEPTH + q) for q in range(DEPTH)])
+        for i in range(rows):
+            near_ref[0, i, :, lanes] = near[i]
+            far_ref[0, i, :, lanes] = far[i]
+
+
+def interior_kernel(
+    flags, conv, x, cot, top, bot, sl, sr, se, dl, dr, de, w, vec, bi, wi, wo, wot, wit, sec, dc, xh, cs
+):
+    rows, width, chans = conv.shape[1:]
+    inner = width - 2 * SIDE
+    mid = pl.ds(SIDE, inner)
+    mats = (vec, bi, wi, wo, wot, wit)
+    for full, near, far in ((sec, sl, sr), (dc, dl, dr)):
+        full[0, :, pl.ds(0, SIDE), :] = near[0]
+        full[0, :, pl.ds(width - SIDE, SIDE), :] = far[0]
+    clear_pads(xh, width)
+    widen_rows(xh, 0, top, DEPTH, SUB)
+    widen_rows(xh, DEPTH, bot, DEPTH, SUB)
+    last = rows - DEPTH
+    cs[pl.ds(0, DEPTH)] = conv[0, pl.ds(0, DEPTH), mid, :]
+    cs[pl.ds(DEPTH, DEPTH)] = conv[0, pl.ds(last, DEPTH), mid, :]
+    for half in range(chans // LANES):
+        lanes = pl.ds(half * LANES, LANES)
+
+        def one(block, carry):
+            start = pl.multiple_of(block * SUB, SUB)
+            head, tail = row_parts(xh, w, half, start + SIDE)
+            for d in range(DEPTH):
+                cs[d, pl.ds(start, SUB), lanes] += head[d]
+                cs[2 * DEPTH - 1 - d, pl.ds(start, SUB), lanes] += tail[d]
+            return carry
+
+        lax.fori_loop(0, inner // SUB, one, 0)
+
+    at_end = flags[0] + flags[1] > 0
+
+    @pl.when(jnp.logical_not(at_end))
+    def _():
+        flat = (2 * DEPTH * inner, chans)
+        pick = lambda ref: jnp.concatenate([ref[0, pl.ds(0, DEPTH), mid, :], ref[0, pl.ds(last, DEPTH), mid, :]]).reshape(flat)
+        section, dconv = cells_of(cs[...].reshape(flat), pick(x), pick(cot), *mats)
+        for full, value in ((sec, section), (dc, dconv)):
+            value = value.reshape(2 * DEPTH, inner, chans)
+            full[0, pl.ds(0, DEPTH), mid, :] = value[:DEPTH]
+            full[0, pl.ds(last, DEPTH), mid, :] = value[DEPTH:]
+
+    @pl.when(at_end)
+    def _():
+        flat = (DEPTH * inner, chans)
+        first = flags[0] == 1
+        base = jnp.where(first, last, 0)
+        rim = pl.ds(base, DEPTH)
+        section, dconv = cells_of(
+            cs[pl.ds(jnp.where(first, DEPTH, 0), DEPTH)].reshape(flat),
+            x[0, rim, mid, :].reshape(flat),
+            cot[0, rim, mid, :].reshape(flat),
+            *mats,
+        )
+        for full, value, done in ((sec, section, se), (dc, dconv, de)):
+            full[0, rim, mid, :] = value.reshape(DEPTH, inner, chans)
+            for d in range(DEPTH):
+                full[0, jnp.where(first, d, rows - 1 - d), mid, :] = done[0, d]
+
+    free = rows - 2 * DEPTH
+    step = free // 2
+
+    def some(block, carry):
+        flat = (step * inner, chans)
+        these = pl.ds(DEPTH + block * step, step)
+        section, dconv = cells_of(
+            conv[0, these, mid, :].reshape(flat), x[0, these, mid, :].reshape(flat), cot[0, these, mid, :].reshape(flat), *mats
+        )
+        sec[0, these, mid, :] = section.reshape(step, inner, chans)
+        dc[0, these, mid, :] = dconv.reshape(step, inner, chans)
+        return carry
+
+    lax.fori_loop(0, 2, some, 0)
+
+
+def join_kernel(grad, cot, above, below, top, bot, left, right, wt, out, xh, total):
+    rows, width, chans = grad.shape[1:]
+    clear_pads(xh, width)
+    widen_rows(xh, 0, above, DEPTH, SUB)
+    widen_rows(xh, DEPTH, below, DEPTH, SUB)
+    total[...] = grad[0]
+    for half in range(chans // LANES):
+        lanes = pl.ds(half * LANES, LANES)
+
+        def one(block, carry):
+            start = pl.multiple_of(block * SUB, SUB)
+            head, tail = row_parts(xh, wt, half, start)
+            for d in range(DEPTH):
+                total[d, pl.ds(start, SUB), lanes] += head[d]
+                total[rows - 1 - d, pl.ds(start, SUB), lanes] += tail[d]
+            return carry
+
+        lax.fori_loop(0, width // SUB, one, 0)
+    total[pl.ds(0, DEPTH)] += top[0].astype(jnp.float32)
+    total[pl.ds(rows - DEPTH, DEPTH)] += bot[0].astype(jnp.float32)
+    total[:, pl.ds(0, SUB), :] += left[0].astype(jnp.float32)
+    total[:, pl.ds(width - SUB, SUB), :] += right[0].astype(jnp.float32)
+
+    def finish(row, carry):
+        conv_grad = total[row].astype(jnp.bfloat16).astype(jnp.float32)
+        out[0, row] = (cot[0, row].astype(jnp.float32) + conv_grad).astype(jnp.bfloat16)
+        return carry
+
+    lax.fori_loop(0, rows, finish, 0)
+
+
+def by_slot(x, base=0):
+    return pl.BlockSpec((1,) + tuple(x.shape[1:]), lambda s, *_: (s + base if base else s,) + (0,) * (len(x.shape) - 1))
+
+
+def whole(x):
+    return pl.BlockSpec(tuple(x.shape), lambda s, *_: (0,) * len(x.shape))
+
+
+def run(kernel, name, span, ins, specs, outs, scratch, flags=None, micros=10, into=()):
+    base, slots = span
+    prefetch = () if flags is None else (flags,)
+    first = len(prefetch) + len(ins)
+
+    def body(*refs):
+        return kernel(*refs[:first], *refs[first + len(into) :])
+
+    return pl.pallas_call(
+        body,
+        grid_spec=pltpu.PrefetchScalarGridSpec(
+            num_scalar_prefetch=len(prefetch),
+            grid=(slots,),
+            in_specs=specs + [pl.BlockSpec(memory_space=pl.ANY)] * len(into),
+            out_specs=[by_slot(o, base) for o in outs],
+            scratch_shapes=[pltpu.VMEM(s, jnp.float32) for s in scratch],
+        ),
+        out_shape=list(outs),
+        input_output_aliases={first + k: k for k in range(len(into))},
+        compiler_params=pltpu.CompilerParams(vmem_limit_bytes=60 * 1024 * 1024),
+        cost_estimate=pl.CostEstimate(
+            flops=micros * 1_000_000_000, transcendentals=0, bytes_accessed=sum(o.size * 2 for o in outs)
+        ),
+        name=name,
+    )(*prefetch, *ins, *into)
+
+
+def conv_partial(x, weights, name, span, into=()):
+    slots, rows, width, chans = x.shape
+    out = jax.ShapeDtypeStruct(x.shape, jnp.float32)
+    pads = (chans // LANES, rows, width + 2 * SUB, LANES)
+    specs = [by_slot(x, span[0]), whole(weights)]
+    return run(conv_partial_kernel, name, span, (x, weights), specs, [out], [pads], micros=9 * span[1], into=into)[0]
+
+
+def face_all(blocks):
+    groups = lax.axis_size("face")
+    parts = [blocks]
+    for step in range(1, groups):
+        parts.append(lax.ppermute(blocks, "face", [(g, (g + step) % groups) for g in range(groups)]))
+    return jnp.stack(parts)
+
+
+def spread_ends(ends, rider=None):
+    slots, _, width, chans = ends.shape
+    tiles = lax.axis_size("tile")
+    rows = width // tiles
+    send = jnp.moveaxis(ends.reshape(slots, DEPTH, tiles, rows, chans), 2, 0).reshape(tiles, -1, chans)
+    if rider is not None:
+        send = jnp.concatenate([send, jnp.broadcast_to(rider[None], (tiles,) + rider.shape)], axis=1)
+    got = lax.all_to_all(send, "tile", split_axis=0, concat_axis=0, tiled=True)
+    count = slots * DEPTH * rows
+    found = jnp.stack([got[0, :count], got[tiles - 1, :count]]).reshape(2, slots, DEPTH, rows, chans)
+    return jnp.moveaxis(found, 0, 1), got[:, count:]
+
+
+def in_three(values):
+    parts = []
+    for _ in range(3):
+        part = lax.reduce_precision(values, 8, 7)
+        parts.append(part.astype(jnp.bfloat16))
+        values = values - part
+    return jnp.stack(parts)
+
+
+def pick(all_ends, all_sides, index):
+    groups, slots, _, _, rows, chans = all_ends.shape
+    flat = (groups * slots * 2, DEPTH, rows, chans)
+    strips = jnp.concatenate([all_ends.reshape(flat), all_sides.reshape(flat)])
+    group, slot, edge = index // (slots * 4), index // 4 % slots, index % 4
+    back = (lax.axis_index("face") - group) % groups
+    place = jnp.where(edge < 2, back, groups + back) * (slots * 2) + slot * 2 + edge % 2
+    return jnp.take(strips, place.reshape(-1), axis=0).reshape(slots, 4, DEPTH, rows, chans)
+
+
+def settle(picked, flip, reach):
+    slots, _, _, rows, chans = picked.shape
+    tiles = lax.axis_size("tile")
+    tile = lax.axis_index("tile")
+    half = tiles // 2
+    back = jnp.stack([picked[:, 0]] * half + [picked[:, 1]] * (tiles - half))
+    back = lax.all_to_all(back, "tile", split_axis=0, concat_axis=0, tiled=True)
+    end_flip = jnp.where(tile == 0, flip[:, 0], flip[:, 1])[:, None, None, None]
+    new_ends = jnp.moveaxis(back, 0, 2).reshape(slots, DEPTH, tiles * rows, chans)
+    new_ends = jnp.where(end_flip, new_ends[:, :, ::-1], new_ends)
+    side_flip = flip[:, 2:, None, None, None]
+    found = picked[:, 2:]
+    mirrored = lax.ppermute(found, "tile", [(t, tiles - 1 - t) for t in range(tiles)])
+    new_sides = jnp.where(side_flip, mirrored[:, :, :, ::-1], found)
+    if reach:
+        head, tail = found[:, :, :, :reach], found[:, :, :, rows - reach :]
+        above, below = halo(head, tail)
+        above_turned = lax.ppermute(head, "tile", [(t, tiles - t) for t in range(1, tiles)])
+        below_turned = lax.ppermute(tail, "tile", [(t, tiles - 2 - t) for t in range(tiles - 1)])
+        above = jnp.where(side_flip, above_turned[:, :, :, ::-1], above)
+        below = jnp.where(side_flip, below_turned[:, :, :, ::-1], below)
+        new_sides = jnp.concatenate([above, new_sides, below], axis=3)
+    return new_ends, new_sides
+
+
+def halo(first, last):
+    tiles = lax.axis_size("tile")
+    above = lax.ppermute(last, "tile", [(t, t + 1) for t in range(tiles - 1)])
+    below = lax.ppermute(first, "tile", [(t + 1, t) for t in range(tiles - 1)])
+    return above, below
+
+
+def row_shards(
+    fields,
+    cotangent,
+    dw_kernel,
+    dw_bias,
+    norm_gain,
+    norm_bias,
+    proj_in,
+    bias_in,
+    proj_out,
+    bias_out,
+    layer_scale,
+    strip_source,
+    strip_flip,
+):
+    slots, rows, width, chans = fields.shape
+    tiles = lax.axis_size("tile")
+    tile = lax.axis_index("tile")
+    first_tile, last_tile = tile == 0, tile == tiles - 1
+    flags = jnp.stack([first_tile, last_tile]).astype(jnp.int32)
+    own_samples = lax.axis_index("face") * slots + jnp.arange(slots, dtype=jnp.int32)
+    source, mirror = reader_tables(own_samples, strip_source, strip_flip)
+    entries = jnp.arange(48, dtype=jnp.int32)
+    hits = strip_source[None, :] == entries[:, None]
+    reader_of = jnp.sum(jnp.where(hits, entries[None, :], 0), axis=1)
+    flip_of = jnp.sum(jnp.where(hits, strip_flip[None, :], 0), axis=1)
+    own_strips = (own_samples % 12)[:, None] * 4 + jnp.arange(4, dtype=jnp.int32)[None, :]
+    target = (own_samples // 12)[:, None] * 48 + reader_of[own_strips]
+    target_mirror = flip_of[own_strips] == 1
+
+    own_taps = jnp.concatenate([dw_kernel, dw_bias[:, None]], axis=1).T
+    own_chans = own_taps.shape[1]
+    taps_count = TAPS * TAPS + 1
+    rider_rows = -(-3 * taps_count * own_chans // chans)
+    rider_rows += -rider_rows % 8
+    rider = in_three(own_taps).reshape(-1)
+    rider = jnp.pad(rider, (0, rider_rows * chans - rider.size)).reshape(rider_rows, chans)
+    ends = jnp.where(first_tile, fields[:, :DEPTH], fields[:, : rows - DEPTH - 1 : -1])
+    near_ends, riders = spread_ends(ends, rider)
+    riders = riders.reshape(tiles, -1)[:, : 3 * taps_count * own_chans].astype(jnp.float32)
+    riders = riders.reshape(tiles, 3, taps_count, own_chans)
+    taps = (riders[:, 0] + riders[:, 1]) + riders[:, 2]
+    taps = jnp.moveaxis(taps, 0, 1).reshape(taps_count, chans)
+    taps = jnp.pad(taps, ((0, 6), (0, 0)))
+    weights = jnp.moveaxis(taps.reshape(-1, chans // LANES, LANES), 1, 0)
+    turned = jnp.pad(weights[:, TAPS * TAPS - 1 :: -1], ((0, 0), (0, 7), (0, 0)))
+    vectors = jnp.stack([norm_gain, norm_bias, bias_out, layer_scale])
+    mats = (vectors, bias_in[None], proj_in, proj_out, proj_out.T, proj_in.T)
+
+    side_pair = jnp.stack([fields[:, :, :DEPTH], fields[:, :, : width - DEPTH - 1 : -1]], axis=1)
+    all_sides = face_all(jnp.swapaxes(side_pair, 2, 3))
+    above, below = halo(fields[:, :DEPTH], fields[:, rows - DEPTH :])
+    all_ends = face_all(near_ends)
+    early, near_ends, all_sides = lax.optimization_barrier((fields, near_ends, all_sides))
+    partial = conv_partial(early, weights, "conv_partial", (0, 2))
+    partial, all_ends, above, below = lax.optimization_barrier((partial, all_ends, above, below))
+    picked = pick(all_ends, all_sides, source)
+    late, picked = lax.optimization_barrier((fields, picked))
+    new_ends, sides = settle(picked, mirror, DEPTH)
+    partial = conv_partial(late, weights, "conv_partial_rest", (2, slots - 2), (partial,))
+    sides = jnp.swapaxes(sides, 2, 3)
+    left = jnp.pad(sides[:, 0, :, ::-1], ((0, 0), (0, 0), (SUB - DEPTH, 0), (0, 0)))
+    right = jnp.pad(sides[:, 1], ((0, 0), (0, 0), (0, SUB - DEPTH), (0, 0)))
+    top = jnp.where(first_tile, new_ends[:, ::-1], above)
+    bot = jnp.where(last_tile, new_ends, below)
+
+    near_spec = pl.BlockSpec((1, rows, SIDE, chans), lambda s, f: (s, 0, 0, 0))
+    far_spec = pl.BlockSpec((1, rows, SIDE, chans), lambda s, f: (s, 0, width // SIDE - 1, 0))
+    end_spec = pl.BlockSpec((1, SUB, width, chans), lambda s, f: (s, f[1] * (rows // SUB - 1), 0, 0))
+    side_out = jax.ShapeDtypeStruct((slots, rows, SIDE, chans), jnp.bfloat16)
+    end_out = jax.ShapeDtypeStruct((slots, DEPTH, width - 2 * SIDE, chans), jnp.bfloat16)
+    strip_out = jax.ShapeDtypeStruct((slots, DEPTH, width, chans), jnp.bfloat16)
+    halves = chans // LANES
+    halo_pads = (halves, 2 * DEPTH, width + 2 * SUB, LANES)
+    side_pads = (halves, rows + 2 * DEPTH, 2 * SUB, LANES)
+    extras = (top, bot, left, right)
+    sl, sr, se, dl, dr, de, tb = run(
+        edge_kernel,
+        "edge_cells",
+        (0, slots),
+        (partial,) * 3 + (fields,) * 3 + (cotangent,) * 3 + extras + (weights, turned) + mats,
+        [near_spec, far_spec, end_spec] * 3 + [by_slot(x) for x in extras] + [whole(x) for x in (weights, turned) + mats],
+        [side_out, side_out, end_out, side_out, side_out, end_out, strip_out],
+        [halo_pads, side_pads, side_pads, (2, rows, SIDE, chans), (DEPTH, width - 2 * SIDE, chans)],
+        flags,
+        micros=23,
+    )
+
+    outer = jnp.stack([dl[:, :, :SUB], dr[:, :, SIDE - SUB :]], axis=1)
+    outer_above, outer_below = halo(outer[:, :, :DEPTH], outer[:, :, rows - DEPTH :])
+    outer = jnp.concatenate([outer_above, outer, outer_below], axis=2)
+    strip = jax.ShapeDtypeStruct((slots, rows, SUB, chans), jnp.float32)
+    ins = (outer[:, 0], outer[:, 1])
+    near, far = run(
+        strip_kernel,
+        "side_strips",
+        (0, slots),
+        ins + (turned,),
+        [by_slot(x) for x in ins] + [whole(turned)],
+        [strip, strip],
+        [side_pads, side_pads],
+    )
+    side_pair = jnp.stack([near[:, :, : SUB - DEPTH - 1 : -1], far[:, :, :DEPTH]], axis=1).astype(jnp.bfloat16)
+    near_ends, _ = spread_ends(tb)
+    all_sides = face_all(jnp.swapaxes(side_pair, 2, 3))
+    all_ends = face_all(near_ends)
+
+    full = jax.ShapeDtypeStruct(fields.shape, jnp.bfloat16)
+    ins = (partial, fields, cotangent, top, bot, sl, sr, se, dl, dr, de)
+    done = ()
+    for span, sign in (((0, 1), near), ((1, slots - 1), (near_ends, all_sides))):
+        gated = lax.optimization_barrier((fields, sign))[0]
+        ins = (partial, gated, cotangent, top, bot, sl, sr, se, dl, dr, de)
+        done = run(
+            interior_kernel,
+            "interior_cells",
+            span,
+            ins + (weights,) + mats,
+            [by_slot(x, span[0]) for x in ins] + [whole(x) for x in (weights,) + mats],
+            [full, full],
+            [halo_pads, (2 * DEPTH, width - 2 * SIDE, chans)],
+            flags,
+            micros=9 * span[1],
+            into=done,
+        )
+    section_out, dconv = done
+    dconv, all_ends = lax.optimization_barrier((dconv, all_ends))
+    picked = pick(all_ends, all_sides, target)
+    ends, sides = settle(picked, target_mirror, 0)
+    above, below = halo(dconv[:, :DEPTH], dconv[:, rows - DEPTH :])
+    early, picked = lax.optimization_barrier((dconv, picked))
+    grad = conv_partial(early, turned, "conv_gradient", (0, 2))
+    late, above, below, ends = lax.optimization_barrier((dconv, above, below, ends))
+    grad = conv_partial(late, turned, "conv_gradient_rest", (2, slots - 2), (grad,))
+
+    top = jnp.where(first_tile, ends, 0)
+    bot = jnp.where(last_tile, ends[:, ::-1], 0)
+    sides = jnp.swapaxes(sides, 2, 3)
+    left = jnp.pad(sides[:, 0], ((0, 0), (0, 0), (0, SUB - DEPTH), (0, 0)))
+    right = jnp.pad(sides[:, 1, :, ::-1], ((0, 0), (0, 0), (SUB - DEPTH, 0), (0, 0)))
+    ins = (grad, cotangent, above, below, top, bot, left, right)
+    field_grad = run(
+        join_kernel,
+        "join",
+        (0, slots),
+        ins + (turned,),
+        [by_slot(x) for x in ins] + [whole(turned)],
+        [full],
+        [halo_pads, (rows, width, chans)],
+    )[0]
+    return (section_out, field_grad)
+
+
+def block_of(fields, *rest):
+    rows, width, chans = fields.shape[1:]
+    if rows % SUB == 0 and rows <= 16 and chans % LANES == 0 and width % SIDE == 0 and width > 4 * SIDE:
+        return row_shards(fields, *rest)
+    return shards(fields, *rest)
+
 
 def solution(mesh):
     placed = (
@@ -189,7 +819,7 @@
         P(),
     )
     return jax.shard_map(
-        shards,
+        block_of,
         mesh=mesh,
         in_specs=placed,
         out_specs=(P("face", "tile", None, None), P("face", "tile", None, None)),

time: 926 us -> 253 us (0.27); the launches traced: 908 us -> 252 us
  local copies, waits for them, and re-layouts: 408 us -> 38.2 us
  matrix products: 234 us -> 0 us
  Pallas kernels: 0 us -> 125 us
  waiting for transfers between devices: 109 us -> 6.53 us
  other arithmetic: 85.1 us -> 14.5 us
  starting transfers between devices: 13.7 us -> 66.6 us
  blocking collectives: 43 us -> 0 us
  between operations: 15 us -> 1.43 us
    conv_general_dilated x2 -> x0, matrix products: 181 us -> none  [grouped_conv(): lax.conv_general_dilated(planes_wide, taps.reshape(chans, 1, 7, 7), (1, 1...]
    pallas_call x0 -> x9, Pallas kernels: none -> 125 us  [run(): pl.pallas_call(body, grid_spec=pltpu.PrefetchScalarGridSpec(num_scalar_pr...]
    conv_general_dilated x8 -> x0, local copies, waits for them, and re-layouts: 105 us -> none  [grouped_conv(): lax.conv_general_dilated(planes_wide, taps.reshape(chans, 1, 7, 7), (1, 1...]
    scatter-add x2 -> x0, local copies, waits for them, and re-layouts: 99.8 us -> none  [the longest x1 67.9 us: shards(): interior = interior.at[:, :, size - 3:, :].add(owned[:, 1][:, :, ::-1, :])]
    all_to_all x3 -> x4, waiting for transfers between devices: 81.2 us -> 0.37 us  [the longest x2 0.36 us: spread_ends(): got = lax.all_to_all(send, 'tile', split_axis=0, concat_axis=0, tiled=True)]
    dot_general x4 -> x0, matrix products: 53 us -> none  [the longest x1 25.1 us: shards(): lax.dot_general(dpre, proj_in, (((1,), (1,)), ((), ())), preferred_elemen...]
    ppermute x0 -> x24, starting transfers between devices: none -> 48.1 us  [the longest x12 18.8 us: face_all(): lax.ppermute(blocks, 'face', [(g, (g + step) % groups) for g in range(gro...]
    slice x5 -> x14, local copies, waits for them, and re-layouts: 51.8 us -> 5.15 us  [the longest x1 1.33 us: row_shards(): above, below = halo(dconv[:, :DEPTH], dconv[:, rows - DEPTH:])]
  transfers between devices with their start and end apart: 5 -> 28, of which waited for: 4 -> 3; matrix products, arithmetic and copies ran while one was open for 21% -> 15% of each run, Pallas kernels for 0% -> 32%
where the time goes in v2:
time: 253 us; the launch traced here: 252 us
  Pallas kernels  125 us (49%)
  starting transfers between devices  66.6 us (26%)
  local copies, waits for them, and re-layouts  38.2 us (15%)
  other arithmetic  14.5 us (6%)
  waiting for transfers between devices  6.53 us (3%)
    pallas_call x9, Pallas kernels, run(): pl.pallas_call(body, grid_spec=pltpu.PrefetchScalarGridSpec(num_scalar_pr...  125 us
    ppermute x12, starting transfers between devices, face_all(): lax.ppermute(blocks, 'face', [(g, (g + step) % groups) for g in range(gro...  18.8 us
    ppermute x4, starting transfers between devices, halo(): above = lax.ppermute(last, 'tile', [(t, t + 1) for t in range(tiles - 1)])  15.1 us
    unnamed x40, local copies, waits for them, and re-layouts  13 us
    all_to_all x2, starting transfers between devices, settle(): back = lax.all_to_all(back, 'tile', split_axis=0, concat_axis=0, tiled=True)  10.4 us
    all_to_all x2, starting transfers between devices, spread_ends(): got = lax.all_to_all(send, 'tile', split_axis=0, concat_axis=0, tiled=True)  8.13 us
    ppermute x2, starting transfers between devices, settle(): lax.ppermute(found, 'tile', [(t, tiles - 1 - t) for t in range(tiles)])  5.17 us
    ppermute x4, starting transfers between devices, halo(): below = lax.ppermute(first, 'tile', [(t + 1, t) for t in range(tiles - 1)])  5.14 us
  transfers between devices with their start and end apart: 28, of which 3 were waited for; matrix products, arithmetic and copies ran while one was open for 15% of the time, Pallas kernels for 32%

profile of v2, /device:TPU:0, one launch (start us, length us, event | category | flops | bytes accessed | tf_op | source)
XLA Modules:
  0.0 251.9 jit_solution(17332320877966842031)
XLA Ops:
  0.6 1.1 fusion.38
  1.8 0.7 fusion.2
  2.5 5.0 %collective-permute-start.2 = (bf16[3,2,3,16,256]{4,3,2,1,0:T(8,128)(2,1)}, bf16[3,2,3,16,256]{4,3,2,1,0:T(8,128)(2,1)S(1)}, u32[]{:S(2)}, u32[]{:S(2)}) collective-permute-start(bf16[3,2,3,16,256]{4,3,2,1,0:T(8,128)(2,1)} %get-tuple-element.100), channel_id=1, source_target_pairs={{0,24},{8,0},{16,8},{24,16},{1,25},{9,1},{17,9},{25,17},{2,26},{10... | collective-permute-start | bytes 442376 | tf_op jit(solution)/shard_map/ppermute | solution.py:577
  7.5 1.0 collective-permute-start
  8.5 1.1 slice.132
  9.6 1.3 collective-permute-start.6
  11.0 0.7 copy.52
  11.7 0.8 fusion.21
  12.8 1.3 fusion.37
  14.1 0.9 pad_maximum_fusion.3
  15.0 4.6 %all-to-all-start = ((bf16[8,168,256]{2,1,0:T(8,128)(2,1)}), bf16[8,168,256]{2,1,0:T(8,128)(2,1)S(1)}, u32[]{:S(2)}, u32[]{:S(2)}) async-start(bf16[8,168,256]{2,1,0:T(8,128)(2,1)} %pad_maximum_fusion.3), calls=%async_computation | async-start | bytes 1376256 | tf_op jit(solution)/shard_map/all_to_all | solution.py:588
  19.6 1.3 collective-permute-start.7
  22.0 0.7 gather_fusion.1
  26.2 2.1 copy.67
  28.3 1.0 copy.68
  29.8 1.0 pad_maximum_fusion.4
  31.2 2.9 %collective-permute-start.5 = (bf16[3,2,3,16,256]{4,3,2,1,0:T(8,128)(2,1)S(1)}, bf16[3,2,3,16,256]{4,3,2,1,0:T(8,128)(2,1)}, u32[]{:S(2)}, u32[]{:S(2)}) collective-permute-start(bf16[3,2,3,16,256]{4,3,2,1,0:T(8,128)(2,1)S(1)} %bitcast.186), channel_id=1, source_target_pairs={{0,24},{8,0},{16,8},{24,16},{1,25},{9,1},{17,9},{25,17},{2,26},{10... | collective-permute-start | bytes 442376 | tf_op jit(solution)/shard_map/ppermute | solution.py:577
  34.1 1.1 collective-permute-start.4
  35.7 0.7 copy.59
  36.4 18.4 %conv_partial.1.refs_2_ = f32[3,16,128,256]{3,2,1,0:T(8,128)} custom-call(bf16[3,16,128,256]{3,2,1,0:T(8,128)(2,1)} %refs_2_.1, f32[2,56,128]{2,1,0:T(8,128)} %bitcast.209), custom_call_target="tpu_custom_call" | custom-call | flops 17999998976 | bytes 3145728 | tf_op jit(solution)/shard_map/conv_partial/pallas_call | solution.py:546
  55.5 1.1 pad_maximum_fusion.5
  56.6 0.8 copy-done.2
  59.8 1.3 collective-permute-start.12
  61.1 7.5 %collective-permute-start.9 = (bf16[3,2,3,3,256]{4,2,3,0,1:T(4,128)(2,1)S(1)}, bf16[3,2,3,3,256]{4,2,3,0,1:T(4,128)(2,1)S(1)}, u32[]{:S(2)}, u32[]{:S(2)}) collective-permute-start(bf16[3,2,3,3,256]{4,2,3,0,1:T(4,128)(2,1)S(1)} %get-tuple-element.87), channel_id=1, source_target_pairs={{0,1},{1,2},{2,3},{3,4},{4,5},{5,6},{6,7},{8,9},{9,10},{10,11},{11... | collective-permute-start | bytes 82952 | tf_op jit(solution)/shard_map/ppermute | solution.py:640
  68.5 3.2 %collective-permute-start.11 = (bf16[3,2,3,3,256]{4,2,3,0,1:T(4,128)(2,1)S(1)}, bf16[3,2,3,3,256]{4,2,3,0,1:T(4,128)(2,1)S(1)}, u32[]{:S(2)}, u32[]{:S(2)}) collective-permute-start(bf16[3,2,3,3,256]{4,2,3,0,1:T(4,128)(2,1)S(1)} %get-tuple-element.87), channel_id=1, source_target_pairs={{0,6},{1,5},{2,4},{3,3},{4,2},{5,1},{6,0},{8,14},{9,13},{10,12},{1... | collective-permute-start | bytes 82952 | tf_op jit(solution)/shard_map/ppermute | solution.py:631
  76.3 3.7 %all-to-all-start.1 = ((bf16[8,3,3,16,256]{4,3,2,1,0:T(8,128)(2,1)}), bf16[8,3,3,16,256]{4,3,2,1,0:T(8,128)(2,1)S(1)}, u32[]{:S(2)}, u32[]{:S(2)}) async-start(bf16[8,3,3,16,256]{4,3,2,1,0:T(8,128)(2,1)} %bitcast_dynamic-update-slice_fusion.3), calls=%async_computation.1 | async-start | bytes 1179648 | tf_op jit(solution)/shard_map/all_to_all | solution.py:619
  80.0 2.4 collective-permute-start.10
  82.4 10.4 %conv_partial_rest.1.refs_1_.refs_2_.refs_3_ = f32[3,16,128,256]{3,2,1,0:T(8,128)} custom-call(bf16[3,16,128,256]{3,2,1,0:T(8,128)(2,1)} %refs_2_.1, f32[2,56,128]{2,1,0:T(8,128)} %bitcast.210, f32[3,16,128,256]{3,2,1,0:T(8,128)} %conv_partial.1.refs_2_), custom_call_target="tpu_custom_call", output_to_operand_aliasing={{}: (2, {})} | custom-call | flops 8999999488 | bytes 3145728 | tf_op jit(solution)/shard_map/conv_partial_rest/pallas_call | solution.py:546
  92.9 1.0 collective-permute-done.10
  94.8 0.8 pad.30.refs_12_
  95.6 0.8 pad.31.refs_13_
  96.4 0.7 rev.44
  97.2 2.0 broadcast_select_fusion.2
  99.2 1.0 reverse_select_fusion.1.refs_10_.refs_4_
  100.2 23.1 %edge_cells.1 = (bf16[3,16,16,256]{3,2,1,0:T(8,128)(2,1)}, bf16[3,16,16,256]{3,2,1,0:T(8,128)(2,1)}, bf16[3,3,96,256]{3,2,1,0:T(8,128)(2,1)}, bf16[3,16,16,256]{...) custom-call(s32[2]{0:T(128)} %add_convert_fusion.refs_0_, ...), custom_call_target="tpu_custom_call" | custom-call | flops 23000000512 | bytes 3047424 | tf_op jit(solution)/shard_map/edge_cells/pallas_call | solution.py:546
  123.3 0.9 slice_bitcast_fusion.2
  124.3 0.9 slice_bitcast_fusion.3
  125.2 1.3 collective-permute-start.14
  126.5 3.0 %collective-permute-start.13 = (bf16[3,2,3,8,256]{4,3,2,0,1:T(8,128)(2,1)S(1)}, bf16[3,2,3,8,256]{4,3,2,0,1:T(8,128)(2,1)S(1)}, u32[]{:S(2)}, u32[]{:S(2)}) collective-permute-start(bf16[3,2,3,8,256]{4,3,2,0,1:T(8,128)(2,1)S(1)} %get-tuple-element.85), channel_id=1, source_target_pairs={{0,1},{1,2},{2,3},{3,4},{4,5},{5,6},{6,7},{8,9},{9,10},{10,11},{11... | collective-permute-start | bytes 221192 | tf_op jit(solution)/shard_map/ppermute | solution.py:640
  129.6 2.0 copy.69
  131.6 3.5 %all-to-all-start.2 = ((bf16[8,144,256]{2,1,0:T(8,128)(2,1)}), bf16[8,144,256]{2,1,0:T(8,128)(2,1)S(1)}, u32[]{:S(2)}, u32[]{:S(2)}) async-start(bf16[8,144,256]{2,1,0:T(8,128)(2,1)} %bitcast.47), calls=%async_computation.2 | async-start | bytes 1179648 | tf_op jit(solution)/shard_map/all_to_all | solution.py:588
  135.2 0.9 slice_bitcast_fusion
  136.1 3.4 %side_strips.1 = (f32[3,16,8,256]{3,2,1,0:T(8,128)}, f32[3,16,8,256]{3,2,1,0:T(8,128)}) custom-call(bf16[3,22,8,256]{3,2,1,0:T(8,128)(2,1)} %get-tuple-element.84.refs_0_, bf16[3,22,8,256]{3,2,1,0:T(8,128)(2,1)} %get-tuple-element.83.refs_1_, f32[2,56,128]{2,1,0:T(8,128)} %pad.32.refs_15_.refs_2_.refs_1_.refs_8_), custom_call_target="tpu_custom_call" | custom-call | flops 10000000000 | bytes 393216 | tf_op jit(solution)/shard_map/side_strips/pallas_call | solution.py:546
  139.5 1.0 fusion.1
  140.5 1.0 slice.161
  142.0 3.9 %collective-permute-start.17 = (bf16[3,2,3,16,256]{4,2,3,0,1:T(4,128)(2,1)S(1)}, bf16[3,2,3,16,256]{4,2,3,0,1:T(4,128)(2,1)S(1)}, u32[]{:S(2)}, u32[]{:S(2)}) collective-permute-start(bf16[3,2,3,16,256]{4,2,3,0,1:T(4,128)(2,1)S(1)} %get-tuple-element.94), channel_id=1, source_target_pairs={{0,24},{8,0},{16,8},{24,16},{1,25},{9,1},{17,9},{25,17},{2,26},{10... | collective-permute-start | bytes 442376 | tf_op jit(solution)/shard_map/ppermute | solution.py:577
  146.5 12.0 %interior_cells.2 = (bf16[3,16,128,256]{3,2,1,0:T(8,128)(2,1)}, bf16[3,16,128,256]{3,2,1,0:T(8,128)(2,1)}) custom-call(s32[2]{0:T(128)} %add_convert_fusion.refs_0_, f32[3,16,128,256]{3,2,1,0:T(8,128)} %conv_partial_rest.1.refs_1_.refs_2_.refs_3_, bf16[3,16,128,256]{3,2,1,0:T(8,128)(2,1)} %refs_2_.1, bf16[3,16,128,256]{3,2,1,0:T(8,128)(2,1)} %refs_1_.1, ...), custom_call_target="tpu_custom_call" | custom-call | flops 8999999488 | bytes 6291456 | tf_op jit(solution)/shard_map/interior_cells/pallas_call | solution.py:546
  158.6 5.1 %collective-permute-done.16 = bf16[3,2,3,16,256]{4,2,3,0,1:T(4,128)(2,1)S(1)} collective-permute-done((bf16[3,2,3,16,256]{4,2,3,0,1:T(4,128)(2,1)S(1)}, bf16[3,2,3,16,256]{4,2,3,0,1:T(4,128)(2,1)S(1)}, u32[]{:S(2)}, u32[]{:S(2)}) %collective-permute-start.16) | collective-permute-done | bytes 147488 | tf_op jit(solution)/shard_map/ppermute | solution.py:577
  163.7 0.7 pad_maximum_fusion.2
  164.6 2.2 collective-permute-start.19
  166.8 1.9 collective-permute-start.18
  168.8 19.2 %interior_cells.3 = (bf16[3,16,128,256]{3,2,1,0:T(8,128)(2,1)}, bf16[3,16,128,256]{3,2,1,0:T(8,128)(2,1)}) custom-call(s32[2]{0:T(128)} %add_convert_fusion.refs_0_, f32[3,16,128,256]{3,2,1,0:T(8,128)} %conv_partial_rest.1.refs_1_.refs_2_.refs_3_, bf16[3,16,128,256]{3,2,1,0:T(8,128)(2,1)} %refs_2_.1, ...), custom_call_target="tpu_custom_call", output_to_operand_aliasing={{0}: (19, {}), {1}: (20, {})} | custom-call | flops 17999998976 | bytes 6291456 | tf_op jit(solution)/shard_map/interior_cells/pallas_call | solution.py:546
  188.1 1.3 fusion.36
  190.8 3.2 %collective-permute-start.21 = (bf16[3,3,128,256]{3,2,1,0:T(8,128)(2,1)S(1)}, bf16[3,3,128,256]{3,2,1,0:T(8,128)(2,1)}, u32[]{:S(2)}, u32[]{:S(2)}) collective-permute-start(bf16[3,3,128,256]{3,2,1,0:T(8,128)(2,1)S(1)} %get-tuple-element.72), channel_id=1, source_target_pairs={{0,1},{1,2},{2,3},{3,4},{4,5},{5,6},{6,7},{8,9},{9,10},{10,11},{11... | collective-permute-start | bytes 1769480 | tf_op jit(solution)/shard_map/ppermute | solution.py:640
  194.1 1.3 collective-permute-start.22
  199.8 6.7 %all-to-all-start.3 = ((bf16[8,3,3,16,256]{4,3,2,1,0:T(8,128)(2,1)}), bf16[8,3,3,16,256]{4,3,2,1,0:T(8,128)(2,1)S(1)}, u32[]{:S(2)}, u32[]{:S(2)}) async-start(bf16[8,3,3,16,256]{4,3,2,1,0:T(8,128)(2,1)} %fusion.17), calls=%async_computation.3 | async-start | bytes 1179648 | tf_op jit(solution)/shard_map/all_to_all | solution.py:619
  206.6 2.7 %collective-permute-start.23 = (bf16[3,2,3,16,256]{4,2,3,0,1:T(4,128)(2,1)S(1)}, bf16[3,2,3,16,256]{4,2,3,0,1:T(4,128)(2,1)S(1)}, u32[]{:S(2)}, u32[]{:S(2)}) collective-permute-start(bf16[3,2,3,16,256]{4,2,3,0,1:T(4,128)(2,1)S(1)} %copy.81), channel_id=1, source_target_pairs={{0,7},{1,6},{2,5},{3,4},{4,3},{5,2},{6,1},{7,0},{8,15},{9,14},{10,... | collective-permute-start | bytes 442376 | tf_op jit(solution)/shard_map/ppermute | solution.py:625
  209.3 18.2 %conv_gradient.1.refs_2_ = f32[3,16,128,256]{3,2,1,0:T(8,128)} custom-call(bf16[3,16,128,256]{3,2,1,0:T(8,128)(2,1)} %get-tuple-element.59.refs_0_, f32[2,56,128]{2,1,0:T(8,128)} %pad.32.refs_15_.refs_2_.refs_1_.refs_8_), custom_call_target="tpu_custom_call" | custom-call | flops 17999998976 | bytes 3145728 | tf_op jit(solution)/shard_map/conv_gradient/pallas_call | solution.py:546
  227.9 0.7 pad.33.refs_6_
  228.8 0.7 pad.34.refs_7_
  229.6 0.7 rev.52
  230.5 1.3 reverse_select_fusion
  231.9 10.4 %conv_gradient_rest.1.refs_0_ = f32[3,16,128,256]{3,2,1,0:T(8,128)} custom-call(bf16[3,16,128,256]{3,2,1,0:T(8,128)(2,1)} %get-tuple-element.59.refs_0_, f32[2,56,128]{2,1,0:T(8,128)} %pad.32.refs_15_.refs_2_.refs_1_.refs_8_, f32[3,16,128,256]{3,2,1,0:T(8,128)} %conv_gradient.1.refs_2_), custom_call_target="tpu_custom_call", output_to_operand_aliasing={{}: (2, {})} | custom-call | flops 8999999488 | bytes 3145728 | tf_op jit(solution)/shard_map/conv_gradient_rest/pallas_call | solution.py:546
  242.2 9.7 %join.1 = bf16[3,16,128,256]{3,2,1,0:T(8,128)(2,1)} custom-call(f32[3,16,128,256]{3,2,1,0:T(8,128)} %conv_gradient_rest.1.refs_0_, bf16[3,16,128,256]{3,2,1,0:T(8,128)(2,1)} %refs_1_.1, bf16[3,3,128,256]{3,2,1,0:T(8,128)(2,1)} %collective-permute-done.21.refs_2_, bf16[3,3,128,256]{3,2,1,0:T(8,128)(2,1)} %collective-permute-done.22.refs_3_, ...), custom_call_target="tpu_custom_call" | custom-call | flops 10000000000 | bytes 3145728 | tf_op jit(solution)/shard_map/join/pallas_call | solution.py:546
  (148 shorter events, 22.8 us)
Async XLA Ops:
  2.5 27.3 %collective-permute-start.2 = (bf16[3,2,3,16,256]{4,3,2,1,0:T(8,128)(2,1)}, bf16[3,2,3,16,256]{4,3,2,1,0:T(8,128)(2,1)S(1)}, u32[]{:S(2)}, u32[]{:S(2)}) collective-permute-start(bf16[3,2,3,16,256]{4,3,2,1,0:T(8,128)(2,1)} %get-tuple-element.100), channel_id=1, source_target_pairs={{0,24},{8,0},{16,8},{24,16},{1,25},{9,1},{17,9},{25,17},{2,26},{10... | collective-permute-start | bytes 442376 | tf_op jit(solution)/shard_map/ppermute | solution.py:577
  7.5 22.2 %collective-permute-start.1 = (bf16[3,2,3,16,256]{4,3,2,1,0:T(8,128)(2,1)}, bf16[3,2,3,16,256]{4,3,2,1,0:T(8,128)(2,1)S(1)}, u32[]{:S(2)}, u32[]{:S(2)}) collective-permute-start(bf16[3,2,3,16,256]{4,3,2,1,0:T(8,128)(2,1)} %get-tuple-element.100), channel_id=1, source_target_pairs={{0,16},{8,24},{16,0},{24,8},{1,17},{9,25},{17,1},{25,9},{2,18},{10... | collective-permute-start | bytes 442376 | tf_op jit(solution)/shard_map/ppermute | solution.py:577
  7.5 22.3 %collective-permute-start = (bf16[3,2,3,16,256]{4,3,2,1,0:T(8,128)(2,1)}, bf16[3,2,3,16,256]{4,3,2,1,0:T(8,128)(2,1)}, u32[]{:S(2)}, u32[]{:S(2)}) collective-permute-start(bf16[3,2,3,16,256]{4,3,2,1,0:T(8,128)(2,1)} %get-tuple-element.100), channel_id=1, source_target_pairs={{0,8},{8,16},{16,24},{24,0},{1,9},{9,17},{17,25},{25,1},{2,10},{10... | collective-permute-start | bytes 442376 | tf_op jit(solution)/shard_map/ppermute | solution.py:577
  9.6 47.0 %collective-permute-start.6 = (bf16[3,3,128,256]{3,2,1,0:T(8,128)(2,1)S(1)}, bf16[3,3,128,256]{3,2,1,0:T(8,128)(2,1)S(1)}, u32[]{:S(2)}, u32[]{:S(2)}) collective-permute-start(bf16[3,3,128,256]{3,2,1,0:T(8,128)(2,1)S(1)} %slice.132), channel_id=1, source_target_pairs={{0,1},{1,2},{2,3},{3,4},{4,5},{5,6},{6,7},{8,9},{9,10},{10,11},{11... | collective-permute-start | bytes 1769480 | tf_op jit(solution)/shard_map/ppermute | solution.py:640
  12.8 8.3 %copy-start = (s32[48]{0:T(128)S(1)}, s32[48]{0:T(128)}, u32[]{:S(2)}) copy-start(s32[48]{0:T(128)} %param.26) | copy-start | bytes 580
  12.8 8.3 %copy-start.1 = (s32[48]{0:T(128)S(1)}, s32[48]{0:T(128)}, u32[]{:S(2)}) copy-start(s32[48]{0:T(128)} %param.27) | copy-start | bytes 580
  15.0 16.1 %all-to-all-start = ((bf16[8,168,256]{2,1,0:T(8,128)(2,1)}), bf16[8,168,256]{2,1,0:T(8,128)(2,1)S(1)}, u32[]{:S(2)}, u32[]{:S(2)}) async-start(bf16[8,168,256]{2,1,0:T(8,128)(2,1)} %pad_maximum_fusion.3), calls=%async_computation | async-start | bytes 1376256 | tf_op jit(solution)/shard_map/all_to_all | solution.py:588
  19.6 37.0 %collective-permute-start.7 = (bf16[3,3,128,256]{3,2,1,0:T(8,128)(2,1)S(1)}, bf16[3,3,128,256]{3,2,1,0:T(8,128)(2,1)}, u32[]{:S(2)}, u32[]{:S(2)}) collective-permute-start(bf16[3,3,128,256]{3,2,1,0:T(8,128)(2,1)S(1)} %get-tuple-element.73), channel_id=1, source_target_pairs={{1,0},{2,1},{3,2},{4,3},{5,4},{6,5},{7,6},{9,8},{10,9},{11,10},{12... | collective-permute-start | bytes 1769480 | tf_op jit(solution)/shard_map/ppermute | solution.py:641
  21.2 2.8 %copy-start.6 = (f32[256]{0:T(256)S(1)}, f32[256]{0:T(256)}, u32[]{:S(2)}) copy-start(f32[256]{0:T(256)} %param.25) | copy-start | bytes 3076
  21.3 2.8 %copy-start.7 = (f32[256]{0:T(256)S(1)}, f32[256]{0:T(256)}, u32[]{:S(2)}) copy-start(f32[256]{0:T(256)} %param.24) | copy-start | bytes 3076
  21.3 2.8 %copy-start.8 = (f32[256]{0:T(256)S(1)}, f32[256]{0:T(256)}, u32[]{:S(2)}) copy-start(f32[256]{0:T(256)} %param.20) | copy-start | bytes 3076
  21.3 2.8 %copy-start.9 = (f32[256]{0:T(256)S(1)}, f32[256]{0:T(256)}, u32[]{:S(2)}) copy-start(f32[256]{0:T(256)} %param.19) | copy-start | bytes 3076
  22.6 5.7 %copy-start.4 = (bf16[256,1024]{1,0:T(8,128)(2,1)S(1)}, bf16[256,1024]{1,0:T(8,128)(2,1)}, u32[]{:S(2)}) copy-start(bf16[256,1024]{1,0:T(8,128)(2,1)} %refs_15_.3) | copy-start | bytes 1572868
  31.2 24.3 %collective-permute-start.5 = (bf16[3,2,3,16,256]{4,3,2,1,0:T(8,128)(2,1)S(1)}, bf16[3,2,3,16,256]{4,3,2,1,0:T(8,128)(2,1)}, u32[]{:S(2)}, u32[]{:S(2)}) collective-permute-start(bf16[3,2,3,16,256]{4,3,2,1,0:T(8,128)(2,1)S(1)} %bitcast.186), channel_id=1, source_target_pairs={{0,24},{8,0},{16,8},{24,16},{1,25},{9,1},{17,9},{25,17},{2,26},{10... | collective-permute-start | bytes 442376 | tf_op jit(solution)/shard_map/ppermute | solution.py:577
  34.1 21.4 %collective-permute-start.4 = (bf16[3,2,3,16,256]{4,3,2,1,0:T(8,128)(2,1)S(1)}, bf16[3,2,3,16,256]{4,3,2,1,0:T(8,128)(2,1)}, u32[]{:S(2)}, u32[]{:S(2)}) collective-permute-start(bf16[3,2,3,16,256]{4,3,2,1,0:T(8,128)(2,1)S(1)} %bitcast.187), channel_id=1, source_target_pairs={{0,16},{8,24},{16,0},{24,8},{1,17},{9,25},{17,1},{25,9},{2,18},{10... | collective-permute-start | bytes 442376 | tf_op jit(solution)/shard_map/ppermute | solution.py:577
  35.2 20.3 %collective-permute-start.3 = (bf16[3,2,3,16,256]{4,3,2,1,0:T(8,128)(2,1)S(1)}, bf16[3,2,3,16,256]{4,3,2,1,0:T(8,128)(2,1)}, u32[]{:S(2)}, u32[]{:S(2)}) collective-permute-start(bf16[3,2,3,16,256]{4,3,2,1,0:T(8,128)(2,1)S(1)} %bitcast.188), channel_id=1, source_target_pairs={{0,8},{8,16},{16,24},{24,0},{1,9},{9,17},{17,25},{25,1},{2,10},{10... | collective-permute-start | bytes 442376 | tf_op jit(solution)/shard_map/ppermute | solution.py:577
  36.4 18.4 %copy-start.5 = (f32[56,2,128]{2,0,1:T(8,128)S(1)}, f32[56,2,128]{2,0,1:T(8,128)}, u32[]{:S(2)}) copy-start(f32[56,2,128]{2,0,1:T(8,128)} %copy.59) | copy-start | bytes 172036
  56.6 0.8 copy-start.2
  59.1 33.7 %collective-permute-start.8 = (bf16[3,2,3,3,256]{4,2,3,0,1:T(4,128)(2,1)S(1)}, bf16[3,2,3,3,256]{4,2,3,0,1:T(4,128)(2,1)S(1)}, u32[]{:S(2)}, u32[]{:S(2)}) collective-permute-start(bf16[3,2,3,3,256]{4,2,3,0,1:T(4,128)(2,1)S(1)} %get-tuple-element.88), channel_id=1, source_target_pairs={{1,7},{2,6},{3,5},{4,4},{5,3},{6,2},{7,1},{9,15},{10,14},{11,13},{... | collective-permute-start | bytes 82952 | tf_op jit(solution)/shard_map/ppermute | solution.py:630
  59.8 33.1 %collective-permute-start.12 = (bf16[3,2,3,3,256]{4,2,3,0,1:T(4,128)(2,1)S(1)}, bf16[3,2,3,3,256]{4,2,3,0,1:T(4,128)(2,1)S(1)}, u32[]{:S(2)}, u32[]{:S(2)}) collective-permute-start(bf16[3,2,3,3,256]{4,2,3,0,1:T(4,128)(2,1)S(1)} %get-tuple-element.88), channel_id=1, source_target_pairs={{1,0},{2,1},{3,2},{4,3},{5,4},{6,5},{7,6},{9,8},{10,9},{11,10},{12... | collective-permute-start | bytes 82952 | tf_op jit(solution)/shard_map/ppermute | solution.py:641
  61.1 31.8 %collective-permute-start.9 = (bf16[3,2,3,3,256]{4,2,3,0,1:T(4,128)(2,1)S(1)}, bf16[3,2,3,3,256]{4,2,3,0,1:T(4,128)(2,1)S(1)}, u32[]{:S(2)}, u32[]{:S(2)}) collective-permute-start(bf16[3,2,3,3,256]{4,2,3,0,1:T(4,128)(2,1)S(1)} %get-tuple-element.87), channel_id=1, source_target_pairs={{0,1},{1,2},{2,3},{3,4},{4,5},{5,6},{6,7},{8,9},{9,10},{10,11},{11... | collective-permute-start | bytes 82952 | tf_op jit(solution)/shard_map/ppermute | solution.py:640
  68.5 24.3 %collective-permute-start.11 = (bf16[3,2,3,3,256]{4,2,3,0,1:T(4,128)(2,1)S(1)}, bf16[3,2,3,3,256]{4,2,3,0,1:T(4,128)(2,1)S(1)}, u32[]{:S(2)}, u32[]{:S(2)}) collective-permute-start(bf16[3,2,3,3,256]{4,2,3,0,1:T(4,128)(2,1)S(1)} %get-tuple-element.87), channel_id=1, source_target_pairs={{0,6},{1,5},{2,4},{3,3},{4,2},{5,1},{6,0},{8,14},{9,13},{10,12},{1... | collective-permute-start | bytes 82952 | tf_op jit(solution)/shard_map/ppermute | solution.py:631
  76.3 20.1 %all-to-all-start.1 = ((bf16[8,3,3,16,256]{4,3,2,1,0:T(8,128)(2,1)}), bf16[8,3,3,16,256]{4,3,2,1,0:T(8,128)(2,1)S(1)}, u32[]{:S(2)}, u32[]{:S(2)}) async-start(bf16[8,3,3,16,256]{4,3,2,1,0:T(8,128)(2,1)} %bitcast_dynamic-update-slice_fusion.3), calls=%async_computation.1 | async-start | bytes 1179648 | tf_op jit(solution)/shard_map/all_to_all | solution.py:619
  80.0 13.9 %collective-permute-start.10 = (bf16[3,2,3,16,256]{4,2,3,0,1:T(4,128)(2,1)S(1)}, bf16[3,2,3,16,256]{4,2,3,0,1:T(4,128)(2,1)S(1)}, u32[]{:S(2)}, u32[]{:S(2)}) collective-permute-start(bf16[3,2,3,16,256]{4,2,3,0,1:T(4,128)(2,1)S(1)} %slice.195), channel_id=1, source_target_pairs={{0,7},{1,6},{2,5},{3,4},{4,3},{5,2},{6,1},{7,0},{8,15},{9,14},{10,... | collective-permute-start | bytes 442376 | tf_op jit(solution)/shard_map/ppermute | solution.py:625
  94.4 4.8 %copy-start.3 = (bf16[3,3,128,256]{3,2,1,0:T(8,128)(2,1)S(1)}, bf16[3,3,128,256]{3,2,1,0:T(8,128)(2,1)}, u32[]{:S(2)}) copy-start(bf16[3,3,128,256]{3,2,1,0:T(8,128)(2,1)} %copy-done.2) | copy-start | bytes 1769476
  125.2 9.9 %collective-permute-start.14 = (bf16[3,2,3,8,256]{4,3,2,0,1:T(8,128)(2,1)S(1)}, bf16[3,2,3,8,256]{4,3,2,0,1:T(8,128)(2,1)S(1)}, u32[]{:S(2)}, u32[]{:S(2)}) collective-permute-start(bf16[3,2,3,8,256]{4,3,2,0,1:T(8,128)(2,1)S(1)} %get-tuple-element.86), channel_id=1, source_target_pairs={{1,0},{2,1},{3,2},{4,3},{5,4},{6,5},{7,6},{9,8},{10,9},{11,10},{12... | collective-permute-start | bytes 221192 | tf_op jit(solution)/shard_map/ppermute | solution.py:641
  126.5 8.6 %collective-permute-start.13 = (bf16[3,2,3,8,256]{4,3,2,0,1:T(8,128)(2,1)S(1)}, bf16[3,2,3,8,256]{4,3,2,0,1:T(8,128)(2,1)S(1)}, u32[]{:S(2)}, u32[]{:S(2)}) collective-permute-start(bf16[3,2,3,8,256]{4,3,2,0,1:T(8,128)(2,1)S(1)} %get-tuple-element.85), channel_id=1, source_target_pairs={{0,1},{1,2},{2,3},{3,4},{4,5},{5,6},{6,7},{8,9},{9,10},{10,11},{11... | collective-permute-start | bytes 221192 | tf_op jit(solution)/shard_map/ppermute | solution.py:640
  131.6 32.9 %all-to-all-start.2 = ((bf16[8,144,256]{2,1,0:T(8,128)(2,1)}), bf16[8,144,256]{2,1,0:T(8,128)(2,1)S(1)}, u32[]{:S(2)}, u32[]{:S(2)}) async-start(bf16[8,144,256]{2,1,0:T(8,128)(2,1)} %bitcast.47), calls=%async_computation.2 | async-start | bytes 1179648 | tf_op jit(solution)/shard_map/all_to_all | solution.py:588
  142.0 16.6 %collective-permute-start.17 = (bf16[3,2,3,16,256]{4,2,3,0,1:T(4,128)(2,1)S(1)}, bf16[3,2,3,16,256]{4,2,3,0,1:T(4,128)(2,1)S(1)}, u32[]{:S(2)}, u32[]{:S(2)}) collective-permute-start(bf16[3,2,3,16,256]{4,2,3,0,1:T(4,128)(2,1)S(1)} %get-tuple-element.94), channel_id=1, source_target_pairs={{0,24},{8,0},{16,8},{24,16},{1,25},{9,1},{17,9},{25,17},{2,26},{10... | collective-permute-start | bytes 442376 | tf_op jit(solution)/shard_map/ppermute | solution.py:577
  145.9 17.8 %collective-permute-start.16 = (bf16[3,2,3,16,256]{4,2,3,0,1:T(4,128)(2,1)S(1)}, bf16[3,2,3,16,256]{4,2,3,0,1:T(4,128)(2,1)S(1)}, u32[]{:S(2)}, u32[]{:S(2)}) collective-permute-start(bf16[3,2,3,16,256]{4,2,3,0,1:T(4,128)(2,1)S(1)} %get-tuple-element.94), channel_id=1, source_target_pairs={{0,16},{8,24},{16,0},{24,8},{1,17},{9,25},{17,1},{25,9},{2,18},{10... | collective-permute-start | bytes 442376 | tf_op jit(solution)/shard_map/ppermute | solution.py:577
  145.9 17.8 %collective-permute-start.15 = (bf16[3,2,3,16,256]{4,2,3,0,1:T(4,128)(2,1)S(1)}, bf16[3,2,3,16,256]{4,2,3,0,1:T(4,128)(2,1)S(1)}, u32[]{:S(2)}, u32[]{:S(2)}) collective-permute-start(bf16[3,2,3,16,256]{4,2,3,0,1:T(4,128)(2,1)S(1)} %get-tuple-element.94), channel_id=1, source_target_pairs={{0,8},{8,16},{16,24},{24,0},{1,9},{9,17},{17,25},{25,1},{2,10},{10... | collective-permute-start | bytes 442376 | tf_op jit(solution)/shard_map/ppermute | solution.py:577
  164.6 23.4 %collective-permute-start.20 = (bf16[3,2,3,16,256]{4,3,2,1,0:T(8,128)(2,1)S(1)}, bf16[3,2,3,16,256]{4,3,2,1,0:T(8,128)(2,1)S(1)}, u32[]{:S(2)}, u32[]{:S(2)}) collective-permute-start(bf16[3,2,3,16,256]{4,3,2,1,0:T(8,128)(2,1)S(1)} %bitcast.190), channel_id=1, source_target_pairs={{0,24},{8,0},{16,8},{24,16},{1,25},{9,1},{17,9},{25,17},{2,26},{10... | collective-permute-start | bytes 442376 | tf_op jit(solution)/shard_map/ppermute | solution.py:577
  164.6 23.3 %collective-permute-start.19 = (bf16[3,2,3,16,256]{4,3,2,1,0:T(8,128)(2,1)S(1)}, bf16[3,2,3,16,256]{4,3,2,1,0:T(8,128)(2,1)S(1)}, u32[]{:S(2)}, u32[]{:S(2)}) collective-permute-start(bf16[3,2,3,16,256]{4,3,2,1,0:T(8,128)(2,1)S(1)} %bitcast.191), channel_id=1, source_target_pairs={{0,16},{8,24},{16,0},{24,8},{1,17},{9,25},{17,1},{25,9},{2,18},{10... | collective-permute-start | bytes 442376 | tf_op jit(solution)/shard_map/ppermute | solution.py:577
  166.8 21.1 %collective-permute-start.18 = (bf16[3,2,3,16,256]{4,3,2,1,0:T(8,128)(2,1)S(1)}, bf16[3,2,3,16,256]{4,3,2,1,0:T(8,128)(2,1)S(1)}, u32[]{:S(2)}, u32[]{:S(2)}) collective-permute-start(bf16[3,2,3,16,256]{4,3,2,1,0:T(8,128)(2,1)S(1)} %bitcast.192), channel_id=1, source_target_pairs={{0,8},{8,16},{16,24},{24,0},{1,9},{9,17},{17,25},{25,1},{2,10},{10... | collective-permute-start | bytes 442376 | tf_op jit(solution)/shard_map/ppermute | solution.py:577
  190.8 39.7 %collective-permute-start.21 = (bf16[3,3,128,256]{3,2,1,0:T(8,128)(2,1)S(1)}, bf16[3,3,128,256]{3,2,1,0:T(8,128)(2,1)}, u32[]{:S(2)}, u32[]{:S(2)}) collective-permute-start(bf16[3,3,128,256]{3,2,1,0:T(8,128)(2,1)S(1)} %get-tuple-element.72), channel_id=1, source_target_pairs={{0,1},{1,2},{2,3},{3,4},{4,5},{5,6},{6,7},{8,9},{9,10},{10,11},{11... | collective-permute-start | bytes 1769480 | tf_op jit(solution)/shard_map/ppermute | solution.py:640
  194.1 36.4 %collective-permute-start.22 = (bf16[3,3,128,256]{3,2,1,0:T(8,128)(2,1)S(1)}, bf16[3,3,128,256]{3,2,1,0:T(8,128)(2,1)}, u32[]{:S(2)}, u32[]{:S(2)}) collective-permute-start(bf16[3,3,128,256]{3,2,1,0:T(8,128)(2,1)S(1)} %get-tuple-element.71), channel_id=1, source_target_pairs={{1,0},{2,1},{3,2},{4,3},{5,4},{6,5},{7,6},{9,8},{10,9},{11,10},{12... | collective-permute-start | bytes 1769480 | tf_op jit(solution)/shard_map/ppermute | solution.py:641
  199.8 29.8 %all-to-all-start.3 = ((bf16[8,3,3,16,256]{4,3,2,1,0:T(8,128)(2,1)}), bf16[8,3,3,16,256]{4,3,2,1,0:T(8,128)(2,1)S(1)}, u32[]{:S(2)}, u32[]{:S(2)}) async-start(bf16[8,3,3,16,256]{4,3,2,1,0:T(8,128)(2,1)} %fusion.17), calls=%async_computation.3 | async-start | bytes 1179648 | tf_op jit(solution)/shard_map/all_to_all | solution.py:619
  206.6 21.0 %collective-permute-start.23 = (bf16[3,2,3,16,256]{4,2,3,0,1:T(4,128)(2,1)S(1)}, bf16[3,2,3,16,256]{4,2,3,0,1:T(4,128)(2,1)S(1)}, u32[]{:S(2)}, u32[]{:S(2)}) collective-permute-start(bf16[3,2,3,16,256]{4,2,3,0,1:T(4,128)(2,1)S(1)} %copy.81), channel_id=1, source_target_pairs={{0,7},{1,6},{2,5},{3,4},{4,3},{5,2},{6,1},{7,0},{8,15},{9,14},{10,... | collective-permute-start | bytes 442376 | tf_op jit(solution)/shard_map/ppermute | solution.py:625

commit v3 on v2

--- a/solution.py
+++ b/solution.py
@@ -570,21 +570,46 @@
     return run(conv_partial_kernel, name, span, (x, weights), specs, [out], [pads], micros=9 * span[1], into=into)[0]
 
 
-def face_all(blocks):
+def face_all(own):
     groups = lax.axis_size("face")
-    parts = [blocks]
-    for step in range(1, groups):
-        parts.append(lax.ppermute(blocks, "face", [(g, (g + step) % groups) for g in range(groups)]))
-    return jnp.stack(parts)
-
-
-def spread_ends(ends, rider=None):
+    send = jnp.broadcast_to(own[None], (groups,) + own.shape)
+    return lax.all_to_all(send, "face", split_axis=0, concat_axis=0, tiled=True)
+
+
+def turn_sides(sides, flip):
+    tiles = lax.axis_size("tile")
+    mirrored = lax.ppermute(sides, "tile", [(t, tiles - 1 - t) for t in range(tiles)])
+    return jnp.where(flip[:, :, None, None, None], mirrored[:, :, :, ::-1], sides)
+
+
+def turn_ends(ends, flip):
+    here = jnp.where(lax.axis_index("tile") == 0, flip[:, 0], flip[:, 1])
+    return jnp.where(here[:, None, None, None], ends[:, :, ::-1], ends)
+
+
+def to_neighbours(head, tail):
+    tiles, chans = lax.axis_size("tile"), head.shape[-1]
+    after = jnp.arange(tiles, dtype=jnp.int32) == lax.axis_index("tile") + 1
+    rows = jnp.where(after[:, None, None], tail.reshape(1, -1, chans), head.reshape(1, -1, chans))
+    return jnp.pad(rows, ((0, 0), (0, -rows.shape[1] % 8), (0, 0)))
+
+
+def from_neighbours(got, shape):
+    tiles, tile = lax.axis_size("tile"), lax.axis_index("tile")
+    count = 1
+    for extent in shape[:-1]:
+        count *= extent
+    above = lax.dynamic_index_in_dim(got, jnp.maximum(tile - 1, 0), 0, False)[:count].reshape(shape)
+    below = lax.dynamic_index_in_dim(got, jnp.minimum(tile + 1, tiles - 1), 0, False)[:count].reshape(shape)
+    return jnp.where(tile == 0, 0, above), jnp.where(tile == tiles - 1, 0, below)
+
+
+def spread_ends(ends, rider):
     slots, _, width, chans = ends.shape
     tiles = lax.axis_size("tile")
     rows = width // tiles
     send = jnp.moveaxis(ends.reshape(slots, DEPTH, tiles, rows, chans), 2, 0).reshape(tiles, -1, chans)
-    if rider is not None:
-        send = jnp.concatenate([send, jnp.broadcast_to(rider[None], (tiles,) + rider.shape)], axis=1)
+    send = jnp.concatenate([send, rider], axis=1)
     got = lax.all_to_all(send, "tile", split_axis=0, concat_axis=0, tiled=True)
     count = slots * DEPTH * rows
     found = jnp.stack([got[0, :count], got[tiles - 1, :count]]).reshape(2, slots, DEPTH, rows, chans)
@@ -600,39 +625,23 @@
     return jnp.stack(parts)
 
 
-def pick(all_ends, all_sides, index):
-    groups, slots, _, _, rows, chans = all_ends.shape
-    flat = (groups * slots * 2, DEPTH, rows, chans)
-    strips = jnp.concatenate([all_ends.reshape(flat), all_sides.reshape(flat)])
-    group, slot, edge = index // (slots * 4), index // 4 % slots, index % 4
-    back = (lax.axis_index("face") - group) % groups
-    place = jnp.where(edge < 2, back, groups + back) * (slots * 2) + slot * 2 + edge % 2
-    return jnp.take(strips, place.reshape(-1), axis=0).reshape(slots, 4, DEPTH, rows, chans)
-
-
-def settle(picked, flip, reach):
-    slots, _, _, rows, chans = picked.shape
+def pick(found, index):
+    groups, slots, _, _, rows, chans = found.shape
+    strips = found.reshape(groups * slots * 4, DEPTH, rows, chans)
+    return jnp.take(strips, index.reshape(-1), axis=0).reshape(slots, 4, DEPTH, rows, chans)
+
+
+def gather_ends(found, rider=None):
+    slots, _, _, rows, chans = found.shape
     tiles = lax.axis_size("tile")
-    tile = lax.axis_index("tile")
     half = tiles // 2
-    back = jnp.stack([picked[:, 0]] * half + [picked[:, 1]] * (tiles - half))
-    back = lax.all_to_all(back, "tile", split_axis=0, concat_axis=0, tiled=True)
-    end_flip = jnp.where(tile == 0, flip[:, 0], flip[:, 1])[:, None, None, None]
-    new_ends = jnp.moveaxis(back, 0, 2).reshape(slots, DEPTH, tiles * rows, chans)
-    new_ends = jnp.where(end_flip, new_ends[:, :, ::-1], new_ends)
-    side_flip = flip[:, 2:, None, None, None]
-    found = picked[:, 2:]
-    mirrored = lax.ppermute(found, "tile", [(t, tiles - 1 - t) for t in range(tiles)])
-    new_sides = jnp.where(side_flip, mirrored[:, :, :, ::-1], found)
-    if reach:
-        head, tail = found[:, :, :, :reach], found[:, :, :, rows - reach :]
-        above, below = halo(head, tail)
-        above_turned = lax.ppermute(head, "tile", [(t, tiles - t) for t in range(1, tiles)])
-        below_turned = lax.ppermute(tail, "tile", [(t, tiles - 2 - t) for t in range(tiles - 1)])
-        above = jnp.where(side_flip, above_turned[:, :, :, ::-1], above)
-        below = jnp.where(side_flip, below_turned[:, :, :, ::-1], below)
-        new_sides = jnp.concatenate([above, new_sides, below], axis=3)
-    return new_ends, new_sides
+    send = jnp.stack([found[:, 0]] * half + [found[:, 1]] * (tiles - half)).reshape(tiles, -1, chans)
+    count = send.shape[1]
+    if rider is not None:
+        send = jnp.concatenate([send, rider], axis=1)
+    got = lax.all_to_all(send, "tile", split_axis=0, concat_axis=0, tiled=True)
+    ends = got[:, :count].reshape(tiles, slots, DEPTH, rows, chans)
+    return jnp.moveaxis(ends, 0, 2).reshape(slots, DEPTH, tiles * rows, chans), got[:, count:]
 
 
 def halo(first, last):
@@ -680,7 +689,8 @@
     rider = in_three(own_taps).reshape(-1)
     rider = jnp.pad(rider, (0, rider_rows * chans - rider.size)).reshape(rider_rows, chans)
     ends = jnp.where(first_tile, fields[:, :DEPTH], fields[:, : rows - DEPTH - 1 : -1])
-    near_ends, riders = spread_ends(ends, rider)
+    ends = turn_ends(ends, target_mirror[:, :2])
+    near_ends, riders = spread_ends(ends, jnp.broadcast_to(rider[None], (tiles,) + rider.shape))
     riders = riders.reshape(tiles, -1)[:, : 3 * taps_count * own_chans].astype(jnp.float32)
     riders = riders.reshape(tiles, 3, taps_count, own_chans)
     taps = (riders[:, 0] + riders[:, 1]) + riders[:, 2]
@@ -692,15 +702,20 @@
     mats = (vectors, bias_in[None], proj_in, proj_out, proj_out.T, proj_in.T)
 
     side_pair = jnp.stack([fields[:, :, :DEPTH], fields[:, :, : width - DEPTH - 1 : -1]], axis=1)
-    all_sides = face_all(jnp.swapaxes(side_pair, 2, 3))
-    above, below = halo(fields[:, :DEPTH], fields[:, rows - DEPTH :])
-    all_ends = face_all(near_ends)
-    early, near_ends, all_sides = lax.optimization_barrier((fields, near_ends, all_sides))
+    sides = turn_sides(jnp.swapaxes(side_pair, 2, 3), target_mirror[:, 2:])
+    own = jnp.concatenate([near_ends, sides], axis=1)
+    found = face_all(own)
+    early, own = lax.optimization_barrier((fields, own))
+    above, below = halo(early[:, :DEPTH], early[:, rows - DEPTH :])
     partial = conv_partial(early, weights, "conv_partial", (0, 2))
-    partial, all_ends, above, below = lax.optimization_barrier((partial, all_ends, above, below))
-    picked = pick(all_ends, all_sides, source)
+    partial, found, above, below = lax.optimization_barrier((partial, found, above, below))
+    picked = pick(found, source)
     late, picked = lax.optimization_barrier((fields, picked))
-    new_ends, sides = settle(picked, mirror, DEPTH)
+    sides = picked[:, 2:]
+    rider = to_neighbours(sides[:, :, :, :DEPTH], sides[:, :, :, rows - DEPTH :])
+    new_ends, riders = gather_ends(picked[:, :2], rider)
+    side_above, side_below = from_neighbours(riders, (slots, 2, DEPTH, DEPTH, chans))
+    sides = jnp.concatenate([side_above, sides, side_below], axis=3)
     partial = conv_partial(late, weights, "conv_partial_rest", (2, slots - 2), (partial,))
     sides = jnp.swapaxes(sides, 2, 3)
     left = jnp.pad(sides[:, 0, :, ::-1], ((0, 0), (0, 0), (SUB - DEPTH, 0), (0, 0)))
@@ -731,8 +746,15 @@
     )
 
     outer = jnp.stack([dl[:, :, :SUB], dr[:, :, SIDE - SUB :]], axis=1)
-    outer_above, outer_below = halo(outer[:, :, :DEPTH], outer[:, :, rows - DEPTH :])
-    outer = jnp.concatenate([outer_above, outer, outer_below], axis=2)
+    rims = jnp.stack([outer[:, 0, :, :DEPTH], outer[:, 1, :, SUB - DEPTH :]], axis=1)
+    near_ends, riders = spread_ends(tb, to_neighbours(rims[:, :, :DEPTH], rims[:, :, rows - DEPTH :]))
+    shown = []
+    for rim in from_neighbours(riders, (slots, 2, DEPTH, DEPTH, chans)):
+        blank = jnp.zeros((slots, DEPTH, SUB - DEPTH, chans), rim.dtype)
+        shown.append(
+            jnp.stack([jnp.concatenate([rim[:, 0], blank], axis=2), jnp.concatenate([blank, rim[:, 1]], axis=2)], axis=1)
+        )
+    outer = jnp.concatenate([shown[0], outer, shown[1]], axis=2)
     strip = jax.ShapeDtypeStruct((slots, rows, SUB, chans), jnp.float32)
     ins = (outer[:, 0], outer[:, 1])
     near, far = run(
@@ -745,14 +767,13 @@
         [side_pads, side_pads],
     )
     side_pair = jnp.stack([near[:, :, : SUB - DEPTH - 1 : -1], far[:, :, :DEPTH]], axis=1).astype(jnp.bfloat16)
-    near_ends, _ = spread_ends(tb)
-    all_sides = face_all(jnp.swapaxes(side_pair, 2, 3))
-    all_ends = face_all(near_ends)
+    own = jnp.concatenate([near_ends, jnp.swapaxes(side_pair, 2, 3)], axis=1)
+    found = face_all(own)
 
     full = jax.ShapeDtypeStruct(fields.shape, jnp.bfloat16)
     ins = (partial, fields, cotangent, top, bot, sl, sr, se, dl, dr, de)
     done = ()
-    for span, sign in (((0, 1), near), ((1, slots - 1), (near_ends, all_sides))):
+    for span, sign in (((0, 1), tb), ((1, slots - 1), own)):
         gated = lax.optimization_barrier((fields, sign))[0]
         ins = (partial, gated, cotangent, top, bot, sl, sr, se, dl, dr, de)
         done = run(
@@ -764,18 +785,18 @@
             [full, full],
             [halo_pads, (2 * DEPTH, width - 2 * SIDE, chans)],
             flags,
-            micros=9 * span[1],
+            micros=10 * span[1],
             into=done,
         )
     section_out, dconv = done
-    dconv, all_ends = lax.optimization_barrier((dconv, all_ends))
-    picked = pick(all_ends, all_sides, target)
-    ends, sides = settle(picked, target_mirror, 0)
     above, below = halo(dconv[:, :DEPTH], dconv[:, rows - DEPTH :])
-    early, picked = lax.optimization_barrier((dconv, picked))
-    grad = conv_partial(early, turned, "conv_gradient", (0, 2))
-    late, above, below, ends = lax.optimization_barrier((dconv, above, below, ends))
-    grad = conv_partial(late, turned, "conv_gradient_rest", (2, slots - 2), (grad,))
+    grad = conv_partial(dconv, turned, "conv_gradient", (0, 1))
+    grad, found = lax.optimization_barrier((grad, found))
+    picked = pick(found, target)
+    late, picked = lax.optimization_barrier((dconv, picked))
+    sides = turn_sides(picked[:, 2:], target_mirror[:, 2:])
+    ends = turn_ends(gather_ends(picked[:, :2])[0], target_mirror[:, :2])
+    grad = conv_partial(late, turned, "conv_gradient_rest", (1, slots - 1), (grad,))
 
     top = jnp.where(first_tile, ends, 0)
     bot = jnp.where(last_tile, ends[:, ::-1], 0)

time: 253 us -> 228 us (0.901)
  starting transfers between devices: 66.6 us -> 39.9 us
  waiting for transfers between devices: 6.53 us -> 14.6 us
  local copies, waits for them, and re-layouts: 38.2 us -> 33.1 us
    ppermute x16 -> x2, starting transfers between devices: 27.8 us -> 6.03 us  [turn_sides(): lax.ppermute(sides, 'tile', [(t, tiles - 1 - t) for t in range(tiles)])]
    all_to_all x2 -> x4, waiting for transfers between devices: 0.01 us -> 8.18 us  [the longest x2 5.9 us: face_all(): return lax.all_to_all(send, 'face', split_axis=0, concat_axis=0, tiled=True)]
    ppermute x4 -> x2, starting transfers between devices: 15.1 us -> 6.93 us  [halo(): above = lax.ppermute(last, 'tile', [(t, t + 1) for t in range(tiles - 1)])]
    unnamed x40 -> x42, local copies, waits for them, and re-layouts: 13 us -> 7.07 us
    all_to_all x2 -> x4, starting transfers between devices: 10.4 us -> 15.7 us  [the longest x2 8.4 us: face_all(): return lax.all_to_all(send, 'face', split_axis=0, concat_axis=0, tiled=True)]
    another operation x6 -> x0, other arithmetic: 3.75 us -> none  [face_all(): return jnp.stack(parts)]
    ppermute x4 -> x2, starting transfers between devices: 5.14 us -> 2.57 us  [halo(): below = lax.ppermute(first, 'tile', [(t + 1, t) for t in range(tiles - 1)])]
    ppermute x16 -> x2, waiting for transfers between devices: 6.15 us -> 5.6 us  [turn_sides(): lax.ppermute(sides, 'tile', [(t, tiles - 1 - t) for t in range(tiles)])]
  transfers between devices with their start and end apart: 28 -> 12, of which waited for: 3 -> 4; matrix products, arithmetic and copies ran while one was open for 15% -> 9% of each run, Pallas kernels for 32% -> 39%
where the time goes in v3:
time: 228 us; the launch traced here: 226 us
  Pallas kernels  124 us (54%)
  starting transfers between devices  39.9 us (18%)
  local copies, waits for them, and re-layouts  33.1 us (15%)
  waiting for transfers between devices  14.6 us (6%)
  other arithmetic  12.5 us (5%)
    pallas_call x9, Pallas kernels, run(): pl.pallas_call(body, grid_spec=pltpu.PrefetchScalarGridSpec(num_scalar_pr...  124 us
    all_to_all x2, starting transfers between devices, spread_ends(): got = lax.all_to_all(send, 'tile', split_axis=0, concat_axis=0, tiled=True)  8.72 us
    all_to_all x2, starting transfers between devices, face_all(): return lax.all_to_all(send, 'face', split_axis=0, concat_axis=0, tiled=True)  8.4 us
    all_to_all x2, starting transfers between devices, gather_ends(): got = lax.all_to_all(send, 'tile', split_axis=0, concat_axis=0, tiled=True)  7.27 us
    unnamed x42, local copies, waits for them, and re-layouts  7.07 us
    ppermute x2, starting transfers between devices, halo(): above = lax.ppermute(last, 'tile', [(t, t + 1) for t in range(tiles - 1)])  6.93 us
    ppermute x2, starting transfers between devices, turn_sides(): lax.ppermute(sides, 'tile', [(t, tiles - 1 - t) for t in range(tiles)])  6.03 us
    all_to_all x2, waiting for transfers between devices, face_all(): return lax.all_to_all(send, 'face', split_axis=0, concat_axis=0, tiled=True)  5.9 us
  transfers between devices with their start and end apart: 12, of which 4 were waited for; matrix products, arithmetic and copies ran while one was open for 9% of the time, Pallas kernels for 39%

profile of v3, /device:TPU:0, one launch (start us, length us, event | category | flops | bytes accessed | tf_op | source)
XLA Modules:
  0.0 226.2 jit_solution(2705931978856078797)
XLA Ops:
  0.8 0.8 select_reduce_fusion
  1.6 0.7 gather_fusion
  2.7 1.2 reverse_select_fusion.2
  3.9 0.7 rev.37
  5.8 0.9 pad_maximum_fusion
  6.7 5.2 %all-to-all-start = ((bf16[8,168,256]{2,1,0:T(8,128)(2,1)}), bf16[8,168,256]{2,1,0:T(8,128)(2,1)S(1)}, u32[]{:S(2)}, u32[]{:S(2)}) async-start(bf16[8,168,256]{2,1,0:T(8,128)(2,1)} %pad_maximum_fusion), calls=%async_computation | async-start | bytes 1376256 | tf_op jit(solution)/shard_map/all_to_all | solution.py:613
  11.8 1.1 slice_bitcast_fusion.7
  13.4 2.7 %collective-permute-start = (bf16[3,2,3,16,256]{4,2,3,0,1:T(4,128)(2,1)S(1)}, bf16[3,2,3,16,256]{4,2,3,0,1:T(4,128)(2,1)S(1)}, u32[]{:S(2)}, u32[]{:S(2)}) collective-permute-start(bf16[3,2,3,16,256]{4,2,3,0,1:T(4,128)(2,1)S(1)} %maximum_bitcast_fusion.1), channel_id=1, source_target_pairs={{0,7},{1,6},{2,5},{3,4},{4,3},{5,2},{6,1},{7,0},{8,15},{9,14},{10,... | collective-permute-start | bytes 442376 | tf_op jit(solution)/shard_map/ppermute | solution.py:581
  16.1 0.7 gather_fusion.1
  16.8 0.7 gather_fusion.2
  18.0 0.7 add_convert_fusion.refs_0_
  18.8 1.0 copy.64
  19.8 1.0 copy.65
  21.5 5.6 %collective-permute-done = bf16[3,2,3,16,256]{4,2,3,0,1:T(4,128)(2,1)S(1)} collective-permute-done((bf16[3,2,3,16,256]{4,2,3,0,1:T(4,128)(2,1)S(1)}, bf16[3,2,3,16,256]{4,2,3,0,1:T(4,128)(2,1)S(1)}, u32[]{:S(2)}, u32[]{:S(2)}) %collective-permute-start) | collective-permute-done | bytes 147488 | tf_op jit(solution)/shard_map/ppermute | solution.py:581
  28.0 2.4 %fusion.15 = (bf16[3,3,128,256]{3,2,1,0:T(8,128)(2,1)}, bf16[3,3,128,256]{3,2,1,0:T(8,128)(2,1)}) fusion(bf16[3,16,128,256]{3,2,1,0:T(8,128)(2,1)} %refs_2_.1), kind=kLoop, calls=%fused_computation.115 | loop fusion | bytes 2359296 | tf_op jit(solution)/shard_map/slice | solution.py:709
  30.5 1.1 broadcast_in_dim.157
  31.6 4.9 %all-to-all-start.1 = ((bf16[4,3,4,3,16,256]{5,4,3,2,1,0:T(8,128)(2,1)}), bf16[4,3,4,3,16,256]{5,4,3,2,1,0:T(8,128)(2,1)S(1)}, u32[]{:S(2)}, u32[]{:S(2)}) async-start(bf16[4,3,4,3,16,256]{5,4,3,2,1,0:T(8,128)(2,1)} %broadcast_in_dim.157), calls=%async_computation.1 | async-start | bytes 2359296 | tf_op jit(solution)/shard_map/all_to_all | solution.py:576
  36.6 0.7 copy.58
  37.4 1.9 collective-permute-start.1
  39.3 1.3 collective-permute-start.2
  40.6 18.3 %conv_partial.1.refs_2_ = f32[3,16,128,256]{3,2,1,0:T(8,128)} custom-call(bf16[3,16,128,256]{3,2,1,0:T(8,128)(2,1)} %refs_2_.1, f32[2,56,128]{2,1,0:T(8,128)} %bitcast.177), custom_call_target="tpu_custom_call" | custom-call | flops 17999998976 | bytes 3145728 | tf_op jit(solution)/shard_map/conv_partial/pallas_call | solution.py:546
  59.6 5.9 %all-to-all-done.1 = bf16[4,3,4,3,16,256]{5,4,3,2,1,0:T(8,128)(2,1)S(1)} async-done(((bf16[4,3,4,3,16,256]{5,4,3,2,1,0:T(8,128)(2,1)}), bf16[4,3,4,3,16,256]{5,4,3,2,1,0:T(8,128)(2,1)S(1)}, u32[]{:S(2)}, u32[]{:S(2)}) %all-to-all-start.1) | async-done | bytes 1179680 | tf_op jit(solution)/shard_map/all_to_all | solution.py:576
  66.7 0.9 fusion.2
  67.6 3.7 %all-to-all-start.2 = ((bf16[8,200,256]{2,1,0:T(8,128)(2,1)}), bf16[8,200,256]{2,1,0:T(8,128)(2,1)S(1)}, u32[]{:S(2)}, u32[]{:S(2)}) async-start(bf16[8,200,256]{2,1,0:T(8,128)(2,1)} %fusion.2), calls=%async_computation.2 | async-start | bytes 1638400 | tf_op jit(solution)/shard_map/all_to_all | solution.py:642
  71.4 10.4 %conv_partial_rest.1.refs_1_.refs_2_.refs_3_ = f32[3,16,128,256]{3,2,1,0:T(8,128)} custom-call(bf16[3,16,128,256]{3,2,1,0:T(8,128)(2,1)} %refs_2_.1, f32[2,56,128]{2,1,0:T(8,128)} %bitcast.178, f32[3,16,128,256]{3,2,1,0:T(8,128)} %conv_partial.1.refs_2_), custom_call_target="tpu_custom_call", output_to_operand_aliasing={{}: (2, {})} | custom-call | flops 8999999488 | bytes 3145728 | tf_op jit(solution)/shard_map/conv_partial_rest/pallas_call | solution.py:546
  81.8 2.3 %all-to-all-done.2 = bf16[8,200,256]{2,1,0:T(8,128)(2,1)S(1)} async-done(((bf16[8,200,256]{2,1,0:T(8,128)(2,1)}), bf16[8,200,256]{2,1,0:T(8,128)(2,1)S(1)}, u32[]{:S(2)}, u32[]{:S(2)}) %all-to-all-start.2) | async-done | bytes 819232 | tf_op jit(solution)/shard_map/all_to_all | solution.py:642
  84.9 0.8 pad.42.refs_12_
  85.7 0.8 pad.43.refs_13_
  86.5 1.0 broadcast_select_fusion.2.refs_11_.refs_5_
  87.5 1.0 reverse_select_fusion.1.refs_10_.refs_4_
  88.5 23.0 %edge_cells.1 = (bf16[3,16,16,256]{3,2,1,0:T(8,128)(2,1)}, bf16[3,16,16,256]{3,2,1,0:T(8,128)(2,1)}, bf16[3,3,96,256]{3,2,1,0:T(8,128)(2,1)}, bf16[3,16,16,256]{...) custom-call(s32[2]{0:T(128)} %add_convert_fusion.refs_0_, ...), custom_call_target="tpu_custom_call" | custom-call | flops 23000000512 | bytes 3047424 | tf_op jit(solution)/shard_map/edge_cells/pallas_call | solution.py:546
  111.5 1.0 slice_bitcast_fusion.3
  112.6 0.9 slice_bitcast_fusion.2
  113.9 1.0 fusion.3
  114.9 3.5 %all-to-all-start.3 = ((bf16[8,200,256]{2,1,0:T(8,128)(2,1)}), bf16[8,200,256]{2,1,0:T(8,128)(2,1)S(1)}, u32[]{:S(2)}, u32[]{:S(2)}) async-start(bf16[8,200,256]{2,1,0:T(8,128)(2,1)} %fusion.3), calls=%async_computation.3 | async-start | bytes 1638400 | tf_op jit(solution)/shard_map/all_to_all | solution.py:613
  118.4 12.0 %interior_cells.2 = (bf16[3,16,128,256]{3,2,1,0:T(8,128)(2,1)}, bf16[3,16,128,256]{3,2,1,0:T(8,128)(2,1)}) custom-call(s32[2]{0:T(128)} %add_convert_fusion.refs_0_, f32[3,16,128,256]{3,2,1,0:T(8,128)} %conv_partial_rest.1.refs_1_.refs_2_.refs_3_, bf16[3,16,128,256]{3,2,1,0:T(8,128)(2,1)} %refs_2_.1, bf16[3,16,128,256]{3,2,1,0:T(8,128)(2,1)} %refs_1_.1, ...), custom_call_target="tpu_custom_call" | custom-call | flops 10000000000 | bytes 6291456 | tf_op jit(solution)/shard_map/interior_cells/pallas_call | solution.py:546
  130.5 0.8 all-to-all-done.3
  131.7 0.9 slice_bitcast_fusion
  132.6 3.4 %side_strips.1 = (f32[3,16,8,256]{3,2,1,0:T(8,128)}, f32[3,16,8,256]{3,2,1,0:T(8,128)}) custom-call(bf16[3,22,8,256]{3,2,1,0:T(8,128)(2,1)} %get-tuple-element.70.refs_0_, bf16[3,22,8,256]{3,2,1,0:T(8,128)(2,1)} %get-tuple-element.69.refs_1_, f32[2,56,128]{2,1,0:T(8,128)} %pad.44.refs_15_.refs_2_.refs_1_.refs_8_), custom_call_target="tpu_custom_call" | custom-call | flops 10000000000 | bytes 393216 | tf_op jit(solution)/shard_map/side_strips/pallas_call | solution.py:546
  136.0 1.0 slice.227
  137.3 1.0 fusion.5
  138.8 1.2 broadcast_in_dim.169
  140.0 3.5 %all-to-all-start.4 = ((bf16[4,3,4,3,16,256]{5,4,3,2,1,0:T(8,128)(2,1)}), bf16[4,3,4,3,16,256]{5,4,3,2,1,0:T(8,128)(2,1)S(1)}, u32[]{:S(2)}, u32[]{:S(2)}) async-start(bf16[4,3,4,3,16,256]{5,4,3,2,1,0:T(8,128)(2,1)} %broadcast_in_dim.169), calls=%async_computation.4 | async-start | bytes 2359296 | tf_op jit(solution)/shard_map/all_to_all | solution.py:576
  143.5 19.2 %interior_cells.3 = (bf16[3,16,128,256]{3,2,1,0:T(8,128)(2,1)}, bf16[3,16,128,256]{3,2,1,0:T(8,128)(2,1)}) custom-call(s32[2]{0:T(128)} %add_convert_fusion.refs_0_, f32[3,16,128,256]{3,2,1,0:T(8,128)} %conv_partial_rest.1.refs_1_.refs_2_.refs_3_, bf16[3,16,128,256]{3,2,1,0:T(8,128)(2,1)} %refs_2_.1, ...), custom_call_target="tpu_custom_call", output_to_operand_aliasing={{0}: (19, {}), {1}: (20, {})} | custom-call | flops 20000000000 | bytes 6291456 | tf_op jit(solution)/shard_map/interior_cells/pallas_call | solution.py:546
  162.7 1.3 fusion.14
  164.0 5.0 %collective-permute-start.3 = (bf16[3,3,128,256]{3,2,1,0:T(8,128)(2,1)S(1)}, bf16[3,3,128,256]{3,2,1,0:T(8,128)(2,1)}, u32[]{:S(2)}, u32[]{:S(2)}) collective-permute-start(bf16[3,3,128,256]{3,2,1,0:T(8,128)(2,1)S(1)} %get-tuple-element.60), channel_id=1, source_target_pairs={{0,1},{1,2},{2,3},{3,4},{4,5},{5,6},{6,7},{8,9},{9,10},{10,11},{11... | collective-permute-start | bytes 1769480 | tf_op jit(solution)/shard_map/ppermute | solution.py:649
  169.0 1.3 collective-permute-start.4
  170.3 10.4 %conv_gradient.1.refs_2_ = f32[3,16,128,256]{3,2,1,0:T(8,128)} custom-call(bf16[3,16,128,256]{3,2,1,0:T(8,128)(2,1)} %get-tuple-element.52.refs_0_, f32[2,56,128]{2,1,0:T(8,128)} %pad.44.refs_15_.refs_2_.refs_1_.refs_8_), custom_call_target="tpu_custom_call" | custom-call | flops 8999999488 | bytes 3145728 | tf_op jit(solution)/shard_map/conv_gradient/pallas_call | solution.py:546
  181.6 3.3 %collective-permute-start.5 = (bf16[3,2,3,16,256]{4,2,3,0,1:T(4,128)(2,1)S(1)}, bf16[3,2,3,16,256]{4,2,3,0,1:T(4,128)(2,1)S(1)}, u32[]{:S(2)}, u32[]{:S(2)}) collective-permute-start(bf16[3,2,3,16,256]{4,2,3,0,1:T(4,128)(2,1)S(1)} %slice.271), channel_id=1, source_target_pairs={{0,7},{1,6},{2,5},{3,4},{4,3},{5,2},{6,1},{7,0},{8,15},{9,14},{10,... | collective-permute-start | bytes 442376 | tf_op jit(solution)/shard_map/ppermute | solution.py:581
  184.9 0.6 constant_dynamic-update-slice_fusion.15
  185.6 0.6 constant_dynamic-update-slice_fusion.14
  186.8 0.6 constant_dynamic-update-slice_fusion.12
  187.5 0.6 constant_dynamic-update-slice_fusion.11
  188.1 0.6 constant_dynamic-update-slice_fusion.10
  188.7 0.6 constant_dynamic-update-slice_fusion.9
  189.4 0.6 constant_dynamic-update-slice_fusion.8
  190.0 3.5 %all-to-all-start.5 = ((bf16[8,144,256]{2,1,0:T(8,128)(2,1)}), bf16[8,144,256]{2,1,0:T(8,128)(2,1)S(1)}, u32[]{:S(2)}, u32[]{:S(2)}) async-start(bf16[8,144,256]{2,1,0:T(8,128)(2,1)} %constant_dynamic-update-slice_fusion.8), calls=%async_computation.5 | async-start | bytes 1179648 | tf_op jit(solution)/shard_map/all_to_all | solution.py:642
  193.5 18.2 %conv_gradient_rest.1.refs_0_ = f32[3,16,128,256]{3,2,1,0:T(8,128)} custom-call(bf16[3,16,128,256]{3,2,1,0:T(8,128)(2,1)} %get-tuple-element.52.refs_0_, f32[2,56,128]{2,1,0:T(8,128)} %pad.44.refs_15_.refs_2_.refs_1_.refs_8_, f32[3,16,128,256]{3,2,1,0:T(8,128)} %conv_gradient.1.refs_2_), custom_call_target="tpu_custom_call", output_to_operand_aliasing={{}: (2, {})} | custom-call | flops 17999998976 | bytes 3145728 | tf_op jit(solution)/shard_map/conv_gradient_rest/pallas_call | solution.py:546
  212.3 0.8 pad.47.refs_7_
  213.1 0.7 pad.46.refs_6_
  213.9 0.7 rev.44
  214.6 1.0 broadcast_select_fusion.3
  215.6 0.9 reverse_select_fusion.refs_5_
  216.6 9.7 %join.1 = bf16[3,16,128,256]{3,2,1,0:T(8,128)(2,1)} custom-call(f32[3,16,128,256]{3,2,1,0:T(8,128)} %conv_gradient_rest.1.refs_0_, bf16[3,16,128,256]{3,2,1,0:T(8,128)(2,1)} %refs_1_.1, bf16[3,3,128,256]{3,2,1,0:T(8,128)(2,1)} %collective-permute-done.3.refs_2_, bf16[3,3,128,256]{3,2,1,0:T(8,128)(2,1)} %collective-permute-done.4.refs_3_, ...), custom_call_target="tpu_custom_call" | custom-call | flops 10000000000 | bytes 3145728 | tf_op jit(solution)/shard_map/join/pallas_call | solution.py:546
  (148 shorter events, 10.6 us)
Async XLA Ops:
  1.6 1.1 slice-start
  4.6 0.7 copy-start.11
  4.6 0.7 copy-start.6
  5.7 10.4 %copy-start = (s32[48]{0:T(128)S(1)}, s32[48]{0:T(128)}, u32[]{:S(2)}) copy-start(s32[48]{0:T(128)} %param.26) | copy-start | bytes 580
  6.7 20.6 %all-to-all-start = ((bf16[8,168,256]{2,1,0:T(8,128)(2,1)}), bf16[8,168,256]{2,1,0:T(8,128)(2,1)S(1)}, u32[]{:S(2)}, u32[]{:S(2)}) async-start(bf16[8,168,256]{2,1,0:T(8,128)(2,1)} %pad_maximum_fusion), calls=%async_computation | async-start | bytes 1376256 | tf_op jit(solution)/shard_map/all_to_all | solution.py:613
  13.4 5.5 %copy-start.4 = (bf16[1024,256]{1,0:T(8,128)(2,1)S(1)}, bf16[1024,256]{1,0:T(8,128)(2,1)}, u32[]{:S(2)}) copy-start(bf16[1024,256]{1,0:T(8,128)(2,1)} %refs_16_.3) | copy-start | bytes 1572868
  13.4 13.7 %collective-permute-start = (bf16[3,2,3,16,256]{4,2,3,0,1:T(4,128)(2,1)S(1)}, bf16[3,2,3,16,256]{4,2,3,0,1:T(4,128)(2,1)S(1)}, u32[]{:S(2)}, u32[]{:S(2)}) collective-permute-start(bf16[3,2,3,16,256]{4,2,3,0,1:T(4,128)(2,1)S(1)} %maximum_bitcast_fusion.1), channel_id=1, source_target_pairs={{0,7},{1,6},{2,5},{3,4},{4,3},{5,2},{6,1},{7,0},{8,15},{9,14},{10,... | collective-permute-start | bytes 442376 | tf_op jit(solution)/shard_map/ppermute | solution.py:581
  16.8 3.1 %copy-start.3 = (bf16[256,1024]{1,0:T(8,128)(2,1)S(1)}, bf16[256,1024]{1,0:T(8,128)(2,1)}, u32[]{:S(2)}) copy-start(bf16[256,1024]{1,0:T(8,128)(2,1)} %refs_15_.3) | copy-start | bytes 1572868
  16.8 4.1 %copy-start.7 = (f32[256]{0:T(256)S(1)}, f32[256]{0:T(256)}, u32[]{:S(2)}) copy-start(f32[256]{0:T(256)} %param.25) | copy-start | bytes 3076
  16.8 4.1 %copy-start.8 = (f32[256]{0:T(256)S(1)}, f32[256]{0:T(256)}, u32[]{:S(2)}) copy-start(f32[256]{0:T(256)} %param.24) | copy-start | bytes 3076
  16.8 4.0 %copy-start.9 = (f32[256]{0:T(256)S(1)}, f32[256]{0:T(256)}, u32[]{:S(2)}) copy-start(f32[256]{0:T(256)} %param.20) | copy-start | bytes 3076
  16.8 4.0 %copy-start.10 = (f32[256]{0:T(256)S(1)}, f32[256]{0:T(256)}, u32[]{:S(2)}) copy-start(f32[256]{0:T(256)} %param.19) | copy-start | bytes 3076
  31.6 33.9 %all-to-all-start.1 = ((bf16[4,3,4,3,16,256]{5,4,3,2,1,0:T(8,128)(2,1)}), bf16[4,3,4,3,16,256]{5,4,3,2,1,0:T(8,128)(2,1)S(1)}, u32[]{:S(2)}, u32[]{:S(2)}) async-start(bf16[4,3,4,3,16,256]{5,4,3,2,1,0:T(8,128)(2,1)} %broadcast_in_dim.157), calls=%async_computation.1 | async-start | bytes 2359296 | tf_op jit(solution)/shard_map/all_to_all | solution.py:576
  37.4 22.2 %collective-permute-start.1 = (bf16[3,3,128,256]{3,2,1,0:T(8,128)(2,1)}, bf16[3,3,128,256]{3,2,1,0:T(8,128)(2,1)S(1)}, u32[]{:S(2)}, u32[]{:S(2)}) collective-permute-start(bf16[3,3,128,256]{3,2,1,0:T(8,128)(2,1)} %get-tuple-element.62), channel_id=1, source_target_pairs={{0,1},{1,2},{2,3},{3,4},{4,5},{5,6},{6,7},{8,9},{9,10},{10,11},{11... | collective-permute-start | bytes 1769480 | tf_op jit(solution)/shard_map/ppermute | solution.py:649
  39.3 20.2 %collective-permute-start.2 = (bf16[3,3,128,256]{3,2,1,0:T(8,128)(2,1)}, bf16[3,3,128,256]{3,2,1,0:T(8,128)(2,1)S(1)}, u32[]{:S(2)}, u32[]{:S(2)}) collective-permute-start(bf16[3,3,128,256]{3,2,1,0:T(8,128)(2,1)} %get-tuple-element.61), channel_id=1, source_target_pairs={{1,0},{2,1},{3,2},{4,3},{5,4},{6,5},{7,6},{9,8},{10,9},{11,10},{12... | collective-permute-start | bytes 1769480 | tf_op jit(solution)/shard_map/ppermute | solution.py:650
  40.6 18.3 %copy-start.5 = (f32[56,2,128]{2,0,1:T(8,128)S(1)}, f32[56,2,128]{2,0,1:T(8,128)}, u32[]{:S(2)}) copy-start(f32[56,2,128]{2,0,1:T(8,128)} %copy.58) | copy-start | bytes 172036
  66.4 5.0 %copy-start.1 = (bf16[3,4,3,16,256]{4,2,3,0,1:T(4,128)(2,1)}, bf16[3,4,3,16,256]{4,2,3,0,1:T(4,128)(2,1)S(1)}, u32[]{:S(2)}) copy-start(bf16[3,4,3,16,256]{4,2,3,0,1:T(4,128)(2,1)S(1)} %copy.61) | copy-start | bytes 884740
  67.6 16.4 %all-to-all-start.2 = ((bf16[8,200,256]{2,1,0:T(8,128)(2,1)}), bf16[8,200,256]{2,1,0:T(8,128)(2,1)S(1)}, u32[]{:S(2)}, u32[]{:S(2)}) async-start(bf16[8,200,256]{2,1,0:T(8,128)(2,1)} %fusion.2), calls=%async_computation.2 | async-start | bytes 1638400 | tf_op jit(solution)/shard_map/all_to_all | solution.py:642
  71.4 12.8 %slice-start.1 = ((bf16[3,4,3,16,256]{4,2,3,0,1:T(4,128)(2,1)}), bf16[3,2,3,16,256]{4,2,3,0,1:T(4,128)(2,1)S(1)}, s32[]{:S(2)}) async-start(bf16[3,4,3,16,256]{4,2,3,0,1:T(4,128)(2,1)} %copy-done.1), calls=%async_computation.7 | async-start | bytes 393216 | tf_op jit(solution)/shard_map/slice | solution.py:714
  111.5 2.2 copy-start.2
  114.9 16.4 %all-to-all-start.3 = ((bf16[8,200,256]{2,1,0:T(8,128)(2,1)}), bf16[8,200,256]{2,1,0:T(8,128)(2,1)S(1)}, u32[]{:S(2)}, u32[]{:S(2)}) async-start(bf16[8,200,256]{2,1,0:T(8,128)(2,1)} %fusion.3), calls=%async_computation.3 | async-start | bytes 1638400 | tf_op jit(solution)/shard_map/all_to_all | solution.py:613
  140.0 40.7 %all-to-all-start.4 = ((bf16[4,3,4,3,16,256]{5,4,3,2,1,0:T(8,128)(2,1)}), bf16[4,3,4,3,16,256]{5,4,3,2,1,0:T(8,128)(2,1)S(1)}, u32[]{:S(2)}, u32[]{:S(2)}) async-start(bf16[4,3,4,3,16,256]{5,4,3,2,1,0:T(8,128)(2,1)} %broadcast_in_dim.169), calls=%async_computation.4 | async-start | bytes 2359296 | tf_op jit(solution)/shard_map/all_to_all | solution.py:576
  164.0 52.5 %collective-permute-start.3 = (bf16[3,3,128,256]{3,2,1,0:T(8,128)(2,1)S(1)}, bf16[3,3,128,256]{3,2,1,0:T(8,128)(2,1)}, u32[]{:S(2)}, u32[]{:S(2)}) collective-permute-start(bf16[3,3,128,256]{3,2,1,0:T(8,128)(2,1)S(1)} %get-tuple-element.60), channel_id=1, source_target_pairs={{0,1},{1,2},{2,3},{3,4},{4,5},{5,6},{6,7},{8,9},{9,10},{10,11},{11... | collective-permute-start | bytes 1769480 | tf_op jit(solution)/shard_map/ppermute | solution.py:649
  169.0 47.6 %collective-permute-start.4 = (bf16[3,3,128,256]{3,2,1,0:T(8,128)(2,1)S(1)}, bf16[3,3,128,256]{3,2,1,0:T(8,128)(2,1)}, u32[]{:S(2)}, u32[]{:S(2)}) collective-permute-start(bf16[3,3,128,256]{3,2,1,0:T(8,128)(2,1)S(1)} %get-tuple-element.59), channel_id=1, source_target_pairs={{1,0},{2,1},{3,2},{4,3},{5,4},{6,5},{7,6},{9,8},{10,9},{11,10},{12... | collective-permute-start | bytes 1769480 | tf_op jit(solution)/shard_map/ppermute | solution.py:650
  181.6 30.2 %collective-permute-start.5 = (bf16[3,2,3,16,256]{4,2,3,0,1:T(4,128)(2,1)S(1)}, bf16[3,2,3,16,256]{4,2,3,0,1:T(4,128)(2,1)S(1)}, u32[]{:S(2)}, u32[]{:S(2)}) collective-permute-start(bf16[3,2,3,16,256]{4,2,3,0,1:T(4,128)(2,1)S(1)} %slice.271), channel_id=1, source_target_pairs={{0,7},{1,6},{2,5},{3,4},{4,3},{5,2},{6,1},{7,0},{8,15},{9,14},{10,... | collective-permute-start | bytes 442376 | tf_op jit(solution)/shard_map/ppermute | solution.py:581
  190.0 23.8 %all-to-all-start.5 = ((bf16[8,144,256]{2,1,0:T(8,128)(2,1)}), bf16[8,144,256]{2,1,0:T(8,128)(2,1)S(1)}, u32[]{:S(2)}, u32[]{:S(2)}) async-start(bf16[8,144,256]{2,1,0:T(8,128)(2,1)} %constant_dynamic-update-slice_fusion.8), calls=%async_computation.5 | async-start | bytes 1179648 | tf_op jit(solution)/shard_map/all_to_all | solution.py:642

commit v4 on v3

--- a/solution.py
+++ b/solution.py
@@ -211,30 +211,71 @@
         xs[half, :, pl.ds(SUB + width, SUB), :] = jnp.zeros((rows, SUB, LANES), jnp.float32)
 
 
+EVEN = (TAPS + 1) // 2
+ODD = TAPS // 2
+SHARED = 2 * EVEN + ODD
+
+
+def shared_taps(taps):
+    chans = taps.shape[1]
+    kernel = taps[: TAPS * TAPS].reshape(TAPS, TAPS, chans)
+    even, odd = kernel[0::2], kernel[1::2]
+    both = even + jnp.pad(odd, ((0, EVEN - ODD), (0, 0), (0, 0)))
+    rows = jnp.moveaxis(jnp.concatenate([both, even, odd]), 0, 1).reshape(TAPS * SHARED, chans)
+    rows = jnp.concatenate([rows, taps[TAPS * TAPS :]])
+    rows = jnp.pad(rows, ((0, -rows.shape[0] % SUB), (0, 0)))
+    return jnp.moveaxis(rows.reshape(-1, chans // LANES, LANES), 1, 0)
+
+
 def conv_partial_kernel(x_ref, w_ref, out_ref, xs):
     rows, width, chans = x_ref.shape[1:]
+    pairs = rows // 2
+    before, after = pairs, 2 * pairs + 1
+    mid = pl.ds(SUB, width)
     clear_pads(xs, width)
-    widen_rows(xs, 0, x_ref, rows, SUB)
+    for half in range(chans // LANES):
+        lanes = pl.ds(half * LANES, LANES)
+
+        def upper(k, carry):
+            o = x_ref[0, 2 * k, :, lanes].astype(jnp.float32)
+            xs[half, k, mid, :] = o
+            xs[half, after + k, mid, :] = x_ref[0, 2 * k + 1, :, lanes].astype(jnp.float32) - o
+            return carry
+
+        def lower(k, carry):
+            xs[half, before + k, mid, :] = x_ref[0, 2 * k - 1, :, lanes].astype(jnp.float32) - xs[half, k, mid, :]
+            return carry
+
+        lax.fori_loop(0, pairs, upper, 0)
+        xs[half, before, mid, :] = -xs[half, 0, mid, :]
+        lax.fori_loop(1, pairs, lower, 0)
+        xs[half, before + pairs, mid, :] = x_ref[0, rows - 1, :, lanes].astype(jnp.float32)
+    groups = ((0, pairs, 0, EVEN), (before, pairs + 1, EVEN, EVEN), (after, pairs, 2 * EVEN, ODD))
     wide = 2
     for half in range(chans // LANES):
         lanes = pl.ds(half * LANES, LANES)
 
         def one(block, carry):
             start = pl.multiple_of(block * (SUB * wide), SUB * wide)
-            acc = [[None] * rows for _ in range(wide)]
+            acc = [[[None] * pairs for _ in groups] for _ in range(wide)]
             for q in range(TAPS):
-                taps = load_taps(w_ref, half, q)
-                for row in range(rows):
-                    for b in range(wide):
-                        x = xs[half, row, pl.ds(start + SUB * (b + 1) - DEPTH + q, SUB), :]
-                        for p in range(TAPS):
-                            i = row + DEPTH - p
-                            if 0 <= i < rows:
-                                acc[b][i] = plus(acc[b][i], x * taps[p])
-            bias = w_ref[half, pl.ds(TAPS * TAPS, 1), :]
-            for b in range(wide):
-                for i in range(rows):
-                    out_ref[0, i, pl.ds(start + SUB * b, SUB), lanes] = acc[b][i] + bias
+                for kind, (first, count, tap, many) in enumerate(groups):
+                    taps = [w_ref[half, pl.ds(SHARED * q + tap + b, 1), :] for b in range(many)]
+                    for row in range(count):
+                        for part in range(wide):
+                            x = xs[half, first + row, pl.ds(start + SUB * (part + 1) - DEPTH + q, SUB), :]
+                            sums = acc[part][kind]
+                            for b in range(many):
+                                a = row + 1 - b
+                                if 0 <= a < pairs:
+                                    sums[a] = plus(sums[a], x * taps[b])
+            bias = w_ref[half, pl.ds(SHARED * TAPS, 1), :]
+            for part in range(wide):
+                at = pl.ds(start + SUB * part, SUB)
+                for a in range(pairs):
+                    base = acc[part][0][a] + bias
+                    out_ref[0, 2 * a, at, lanes] = base + acc[part][1][a]
+                    out_ref[0, 2 * a + 1, at, lanes] = base + acc[part][2][a]
             return carry
 
         lax.fori_loop(0, width // (SUB * wide), one, 0)
@@ -254,14 +295,13 @@
     return head, tail
 
 
-def end_parts(xh, w, half, col, first):
+def end_parts(xe, w, half, col):
     out = [None] * DEPTH
     for q in range(TAPS):
         for h in range(DEPTH):
-            x = xh[half, jnp.where(first, h, 2 * DEPTH - 1 - h), pl.ds(col + SUB - DEPTH + q, SUB), :]
+            x = xe[half, h, pl.ds(col + SUB - DEPTH + q, SUB), :]
             for d in range(h + 1):
-                p = jnp.where(first, h - d, TAPS - 1 - h + d)
-                out[d] = plus(out[d], x * w[half, pl.ds(TAPS * p + q, 1), :])
+                out[d] = plus(out[d], x * w[half, pl.ds(TAPS * (h - d) + q, 1), :])
     return out
 
 
@@ -278,11 +318,12 @@
     return acc
 
 
-def cells_of(cells, x, cot, vec, bias_in, w_in, w_out, w_out_t, w_in_t):
-    chans = cells.shape[1]
-    gain, shift, bias_out, scale = (vec[k : k + 1, :] for k in range(4))
+def cells_of(cells, x, cot, vec, bias_in, w_in, w_out, w_out_t, w_in_t, acts, dpres):
+    count, chans = cells.shape
+    gain, shift, bias_twice, scale_half, scale, gain_half = (vec[k : k + 1, :] for k in range(6))
     hidden = w_in.shape[1]
     piece = 256
+    here = pl.ds(0, count)
     cells = cells.astype(jnp.bfloat16).astype(jnp.float32)
     mean = jnp.sum(cells, axis=-1, keepdims=True) * (1.0 / chans)
     centred = cells - mean
@@ -290,23 +331,19 @@
     nhat = centred * inv
     normed = (nhat * gain + shift).astype(jnp.bfloat16)
     dmix = (scale * cot.astype(jnp.float32)).astype(jnp.bfloat16)
-    mlp = None
-    dnorm = None
     for first in range(0, hidden, piece):
         cut = pl.ds(first, piece)
         pre = jnp.dot(normed, w_in[:, cut], preferred_element_type=jnp.float32) + bias_in[0:1, cut]
         dact = jnp.dot(dmix, w_out_t[:, cut], preferred_element_type=jnp.float32)
         square = pre * pre
         tanh_val = jnp.tanh(pre * (GELU_SCALE + (GELU_SCALE * GELU_CUBIC) * square))
-        lifted = 0.5 + 0.5 * tanh_val
-        act = (pre * lifted).astype(jnp.bfloat16)
-        bend = pre * ((0.5 * GELU_SCALE) + (1.5 * GELU_SCALE * GELU_CUBIC) * square)
-        slope = lifted + (1.0 - tanh_val * tanh_val) * bend
-        dpre = (dact * slope).astype(jnp.bfloat16)
-        mlp = plus(mlp, jnp.dot(act, w_out[cut, :], preferred_element_type=jnp.float32))
-        dnorm = plus(dnorm, jnp.dot(dpre, w_in_t[cut, :], preferred_element_type=jnp.float32))
-    section = (x.astype(jnp.float32) + scale * (mlp + bias_out)).astype(jnp.bfloat16)
-    dnorm = dnorm * gain
+        lifted = 1.0 + tanh_val
+        bend = pre * (GELU_SCALE + (3.0 * GELU_SCALE * GELU_CUBIC) * square)
+        acts[here, cut] = (pre * lifted).astype(jnp.bfloat16)
+        dpres[here, cut] = (dact * (lifted * (1.0 + (1.0 - tanh_val) * bend))).astype(jnp.bfloat16)
+    mlp = jnp.dot(acts[here, :], w_out[...], preferred_element_type=jnp.float32)
+    dnorm = jnp.dot(dpres[here, :], w_in_t[...], preferred_element_type=jnp.float32) * gain_half
+    section = (x.astype(jnp.float32) + scale_half * (mlp + bias_twice)).astype(jnp.bfloat16)
     first_mean = jnp.sum(dnorm, axis=-1, keepdims=True) * (1.0 / chans)
     second_mean = jnp.sum(dnorm * nhat, axis=-1, keepdims=True) * (1.0 / chans)
     dconv = (inv * (dnorm - first_mean - nhat * second_mean)).astype(jnp.bfloat16)
@@ -314,13 +351,13 @@
 
 
 def edge_kernel(
-    flags, cl, cr, ce, xl, xr, xe, gl, gr, ge, top, bot, left, right, w, wt, vec, bi, wi, wo, wot, wit,
-    sl, sr, se, dl, dr, de, tb, xh, xcl, xcr, lrs, ends,
+    flags, cl, cr, ce, xl, xr, xe, gl, gr, ge, top, bot, left, right, strip, w, wt, vec, bi, wi, wo, wot, wit,
+    sl, sr, dl, dr, tb, xh, xcl, xcr, lrs, ends, we, wte, dends, acts, dpres,
 ):
     rows, chans = cl.shape[1], cl.shape[3]
     width = top.shape[2]
     inner = width - 2 * SIDE
-    mats = (vec, bi, wi, wo, wot, wit)
+    mats = (vec, bi, wi, wo, wot, wit, acts, dpres)
     first = flags[0] == 1
     clear_pads(xh, width)
     widen_rows(xh, 0, top, DEPTH, SUB)
@@ -363,43 +400,48 @@
         mid = pl.ds(SIDE, inner)
         for d in range(DEPTH):
             ends[d] = ce[0, at[d], mid, :]
+        widen_rows(xh, 0, strip, DEPTH, SUB)
+        for half in range(chans // LANES):
+            for p in range(TAPS):
+                given = pl.ds(TAPS * jnp.where(first, p, TAPS - 1 - p), TAPS)
+                we[half, pl.ds(TAPS * p, TAPS), :] = w[half, given, :]
+                wte[half, pl.ds(TAPS * p, TAPS), :] = wt[half, given, :]
         for half in range(chans // LANES):
             lanes = pl.ds(half * LANES, LANES)
 
             def one(block, carry):
-                start = pl.multiple_of(block * SUB, SUB)
-                parts = end_parts(xh, w, half, start + SIDE, first)
-                for d in range(DEPTH):
-                    ends[d, pl.ds(start, SUB), lanes] += parts[d]
+                for k in range(2):
+                    start = pl.multiple_of((2 * block + k) * SUB, SUB)
+                    parts = end_parts(xh, we, half, start + SIDE)
+                    for d in range(DEPTH):
+                        ends[d, pl.ds(start, SUB), lanes] += parts[d]
                 return carry
 
-            lax.fori_loop(0, inner // SUB, one, 0)
+            lax.fori_loop(0, inner // (2 * SUB), one, 0)
         rim = lambda ref: jnp.stack([ref[0, at[d], mid, :] for d in range(DEPTH)]).reshape(DEPTH * inner, chans)
-        section, dconv = cells_of(ends[...].reshape(DEPTH * inner, chans), rim(xe), rim(ge), *mats)
-        se[0] = section.reshape(DEPTH, inner, chans)
-        dconv = dconv.reshape(DEPTH, inner, chans)
-        de[0] = dconv
+        dconv = cells_of(ends[...].reshape(DEPTH * inner, chans), rim(xe), rim(ge), *mats)[1]
+        dends[...] = dconv.reshape(DEPTH, inner, chans)
         for half in range(chans // LANES):
             lanes = pl.ds(half * LANES, LANES)
             for d in range(DEPTH):
                 xh[half, d, pl.ds(SUB, SIDE), :] = dl[0, whole_at[d], :, lanes].astype(jnp.float32)
-                xh[half, d, pl.ds(SUB + SIDE, inner), :] = de[0, d, :, lanes].astype(jnp.float32)
+                xh[half, d, pl.ds(SUB + SIDE, inner), :] = dends[d, :, lanes].astype(jnp.float32)
                 xh[half, d, pl.ds(SUB + SIDE + inner, SIDE), :] = dr[0, whole_at[d], :, lanes].astype(jnp.float32)
 
             def one_strip(block, carry):
-                start = pl.multiple_of(block * SUB, SUB)
-                out = [None] * DEPTH
-                for q in range(TAPS):
-                    for edge in range(DEPTH):
-                        x = xh[half, edge, pl.ds(start + SUB - DEPTH + q, SUB), :]
-                        for d in range(DEPTH - edge):
-                            p = jnp.where(first, edge + d + 4, 2 - edge - d)
-                            out[d] = plus(out[d], x * wt[half, pl.ds(TAPS * p + q, 1), :])
-                for d in range(DEPTH):
-                    xh[half, DEPTH + d, pl.ds(start + SUB, SUB), :] = out[d]
+                for k in range(2):
+                    start = pl.multiple_of((2 * block + k) * SUB, SUB)
+                    out = [None] * DEPTH
+                    for q in range(TAPS):
+                        for edge in range(DEPTH):
+                            x = xh[half, edge, pl.ds(start + SUB - DEPTH + q, SUB), :]
+                            for d in range(DEPTH - edge):
+                                out[d] = plus(out[d], x * wte[half, pl.ds(TAPS * (edge + d + 4) + q, 1), :])
+                    for d in range(DEPTH):
+                        xh[half, DEPTH + d, pl.ds(start + SUB, SUB), :] = out[d]
                 return carry
 
-            lax.fori_loop(0, width // SUB, one_strip, 0)
+            lax.fori_loop(0, width // (2 * SUB), one_strip, 0)
             for d in range(DEPTH):
                 tb[0, d, :, lanes] = xh[half, DEPTH + d, pl.ds(SUB, width), :].astype(jnp.bfloat16)
 
@@ -423,21 +465,19 @@
 
 
 def interior_kernel(
-    flags, conv, x, cot, top, bot, sl, sr, se, dl, dr, de, w, vec, bi, wi, wo, wot, wit, sec, dc, xh, cs
+    conv, x, cot, top, bot, sl, sr, dl, dr, w, vec, bi, wi, wo, wot, wit, sec, dc, xh, cs, acts, dpres
 ):
     rows, width, chans = conv.shape[1:]
     inner = width - 2 * SIDE
     mid = pl.ds(SIDE, inner)
-    mats = (vec, bi, wi, wo, wot, wit)
+    mats = (vec, bi, wi, wo, wot, wit, acts, dpres)
     for full, near, far in ((sec, sl, sr), (dc, dl, dr)):
         full[0, :, pl.ds(0, SIDE), :] = near[0]
         full[0, :, pl.ds(width - SIDE, SIDE), :] = far[0]
     clear_pads(xh, width)
     widen_rows(xh, 0, top, DEPTH, SUB)
     widen_rows(xh, DEPTH, bot, DEPTH, SUB)
-    last = rows - DEPTH
-    cs[pl.ds(0, DEPTH)] = conv[0, pl.ds(0, DEPTH), mid, :]
-    cs[pl.ds(DEPTH, DEPTH)] = conv[0, pl.ds(last, DEPTH), mid, :]
+    cs[...] = conv[0, :, mid, :]
     for half in range(chans // LANES):
         lanes = pl.ds(half * LANES, LANES)
 
@@ -446,54 +486,23 @@
             head, tail = row_parts(xh, w, half, start + SIDE)
             for d in range(DEPTH):
                 cs[d, pl.ds(start, SUB), lanes] += head[d]
-                cs[2 * DEPTH - 1 - d, pl.ds(start, SUB), lanes] += tail[d]
+                cs[rows - 1 - d, pl.ds(start, SUB), lanes] += tail[d]
             return carry
 
         lax.fori_loop(0, inner // SUB, one, 0)
-
-    at_end = flags[0] + flags[1] > 0
-
-    @pl.when(jnp.logical_not(at_end))
-    def _():
-        flat = (2 * DEPTH * inner, chans)
-        pick = lambda ref: jnp.concatenate([ref[0, pl.ds(0, DEPTH), mid, :], ref[0, pl.ds(last, DEPTH), mid, :]]).reshape(flat)
-        section, dconv = cells_of(cs[...].reshape(flat), pick(x), pick(cot), *mats)
-        for full, value in ((sec, section), (dc, dconv)):
-            value = value.reshape(2 * DEPTH, inner, chans)
-            full[0, pl.ds(0, DEPTH), mid, :] = value[:DEPTH]
-            full[0, pl.ds(last, DEPTH), mid, :] = value[DEPTH:]
-
-    @pl.when(at_end)
-    def _():
-        flat = (DEPTH * inner, chans)
-        first = flags[0] == 1
-        base = jnp.where(first, last, 0)
-        rim = pl.ds(base, DEPTH)
-        section, dconv = cells_of(
-            cs[pl.ds(jnp.where(first, DEPTH, 0), DEPTH)].reshape(flat),
-            x[0, rim, mid, :].reshape(flat),
-            cot[0, rim, mid, :].reshape(flat),
-            *mats,
-        )
-        for full, value, done in ((sec, section, se), (dc, dconv, de)):
-            full[0, rim, mid, :] = value.reshape(DEPTH, inner, chans)
-            for d in range(DEPTH):
-                full[0, jnp.where(first, d, rows - 1 - d), mid, :] = done[0, d]
-
-    free = rows - 2 * DEPTH
-    step = free // 2
+    step = SUB
 
     def some(block, carry):
         flat = (step * inner, chans)
-        these = pl.ds(DEPTH + block * step, step)
+        these = pl.ds(block * step, step)
         section, dconv = cells_of(
-            conv[0, these, mid, :].reshape(flat), x[0, these, mid, :].reshape(flat), cot[0, these, mid, :].reshape(flat), *mats
+            cs[these].reshape(flat), x[0, these, mid, :].reshape(flat), cot[0, these, mid, :].reshape(flat), *mats
         )
         sec[0, these, mid, :] = section.reshape(step, inner, chans)
         dc[0, these, mid, :] = dconv.reshape(step, inner, chans)
         return carry
 
-    lax.fori_loop(0, 2, some, 0)
+    lax.fori_loop(0, rows // step, some, 0)
 
 
 def join_kernel(grad, cot, above, below, top, bot, left, right, wt, out, xh, total):
@@ -501,7 +510,8 @@
     clear_pads(xh, width)
     widen_rows(xh, 0, above, DEPTH, SUB)
     widen_rows(xh, DEPTH, below, DEPTH, SUB)
-    total[...] = grad[0]
+    total[pl.ds(0, DEPTH)] = grad[0, pl.ds(0, DEPTH)] + top[0].astype(jnp.float32)
+    total[pl.ds(DEPTH, DEPTH)] = grad[0, pl.ds(rows - DEPTH, DEPTH)] + bot[0].astype(jnp.float32)
     for half in range(chans // LANES):
         lanes = pl.ds(half * LANES, LANES)
 
@@ -510,21 +520,30 @@
             head, tail = row_parts(xh, wt, half, start)
             for d in range(DEPTH):
                 total[d, pl.ds(start, SUB), lanes] += head[d]
-                total[rows - 1 - d, pl.ds(start, SUB), lanes] += tail[d]
+                total[2 * DEPTH - 1 - d, pl.ds(start, SUB), lanes] += tail[d]
             return carry
 
         lax.fori_loop(0, width // SUB, one, 0)
-    total[pl.ds(0, DEPTH)] += top[0].astype(jnp.float32)
-    total[pl.ds(rows - DEPTH, DEPTH)] += bot[0].astype(jnp.float32)
-    total[:, pl.ds(0, SUB), :] += left[0].astype(jnp.float32)
-    total[:, pl.ds(width - SUB, SUB), :] += right[0].astype(jnp.float32)
-
-    def finish(row, carry):
-        conv_grad = total[row].astype(jnp.bfloat16).astype(jnp.float32)
-        out[0, row] = (cot[0, row].astype(jnp.float32) + conv_grad).astype(jnp.bfloat16)
+
+    def finish(row, sums):
+        def store(at, values):
+            conv_grad = values.astype(jnp.bfloat16).astype(jnp.float32)
+            out[0, row, at, :] = (cot[0, row, at, :].astype(jnp.float32) + conv_grad).astype(jnp.bfloat16)
+
+        near, far = pl.ds(0, SIDE), pl.ds(width - SIDE, SIDE)
+        mid = pl.ds(SIDE, width - 2 * SIDE)
+        store(mid, sums(mid))
+        store(near, sums(near) + left[0, row].astype(jnp.float32))
+        store(far, sums(far) + right[0, row].astype(jnp.float32))
+
+    def free(row, carry):
+        finish(row, lambda at: grad[0, row, at, :])
         return carry
 
-    lax.fori_loop(0, rows, finish, 0)
+    lax.fori_loop(DEPTH, rows - DEPTH, free, 0)
+    for d in range(DEPTH):
+        finish(d, lambda at: total[d, at, :])
+        finish(rows - DEPTH + d, lambda at: total[DEPTH + d, at, :])
 
 
 def by_slot(x, base=0):
@@ -535,7 +554,7 @@
     return pl.BlockSpec(tuple(x.shape), lambda s, *_: (0,) * len(x.shape))
 
 
-def run(kernel, name, span, ins, specs, outs, scratch, flags=None, micros=10, into=()):
+def run(kernel, name, span, ins, specs, outs, scratch, flags=None, micros=10, into=(), halves=()):
     base, slots = span
     prefetch = () if flags is None else (flags,)
     first = len(prefetch) + len(ins)
@@ -550,7 +569,7 @@
             grid=(slots,),
             in_specs=specs + [pl.BlockSpec(memory_space=pl.ANY)] * len(into),
             out_specs=[by_slot(o, base) for o in outs],
-            scratch_shapes=[pltpu.VMEM(s, jnp.float32) for s in scratch],
+            scratch_shapes=[pltpu.VMEM(s, jnp.float32) for s in scratch] + [pltpu.VMEM(s, jnp.bfloat16) for s in halves],
         ),
         out_shape=list(outs),
         input_output_aliases={first + k: k for k in range(len(into))},
@@ -565,7 +584,7 @@
 def conv_partial(x, weights, name, span, into=()):
     slots, rows, width, chans = x.shape
     out = jax.ShapeDtypeStruct(x.shape, jnp.float32)
-    pads = (chans // LANES, rows, width + 2 * SUB, LANES)
+    pads = (chans // LANES, 3 * (rows // 2) + 1, width + 2 * SUB, LANES)
     specs = [by_slot(x, span[0]), whole(weights)]
     return run(conv_partial_kernel, name, span, (x, weights), specs, [out], [pads], micros=9 * span[1], into=into)[0]
 
@@ -698,7 +717,9 @@
     taps = jnp.pad(taps, ((0, 6), (0, 0)))
     weights = jnp.moveaxis(taps.reshape(-1, chans // LANES, LANES), 1, 0)
     turned = jnp.pad(weights[:, TAPS * TAPS - 1 :: -1], ((0, 0), (0, 7), (0, 0)))
-    vectors = jnp.stack([norm_gain, norm_bias, bias_out, layer_scale])
+    shared = shared_taps(taps[: taps_count])
+    shared_turned = shared_taps(jnp.pad(taps[TAPS * TAPS - 1 :: -1], ((0, 1), (0, 0))))
+    vectors = jnp.stack([norm_gain, norm_bias, 2.0 * bias_out, 0.5 * layer_scale, layer_scale, 0.5 * norm_gain])
     mats = (vectors, bias_in[None], proj_in, proj_out, proj_out.T, proj_in.T)
 
     side_pair = jnp.stack([fields[:, :, :DEPTH], fields[:, :, : width - DEPTH - 1 : -1]], axis=1)
@@ -707,7 +728,7 @@
     found = face_all(own)
     early, own = lax.optimization_barrier((fields, own))
     above, below = halo(early[:, :DEPTH], early[:, rows - DEPTH :])
-    partial = conv_partial(early, weights, "conv_partial", (0, 2))
+    partial = conv_partial(early, shared, "conv_partial", (0, 2))
     partial, found, above, below = lax.optimization_barrier((partial, found, above, below))
     picked = pick(found, source)
     late, picked = lax.optimization_barrier((fields, picked))
@@ -716,7 +737,7 @@
     new_ends, riders = gather_ends(picked[:, :2], rider)
     side_above, side_below = from_neighbours(riders, (slots, 2, DEPTH, DEPTH, chans))
     sides = jnp.concatenate([side_above, sides, side_below], axis=3)
-    partial = conv_partial(late, weights, "conv_partial_rest", (2, slots - 2), (partial,))
+    partial = conv_partial(late, shared, "conv_partial_rest", (2, slots - 2), (partial,))
     sides = jnp.swapaxes(sides, 2, 3)
     left = jnp.pad(sides[:, 0, :, ::-1], ((0, 0), (0, 0), (SUB - DEPTH, 0), (0, 0)))
     right = jnp.pad(sides[:, 1], ((0, 0), (0, 0), (0, SUB - DEPTH), (0, 0)))
@@ -727,22 +748,24 @@
     far_spec = pl.BlockSpec((1, rows, SIDE, chans), lambda s, f: (s, 0, width // SIDE - 1, 0))
     end_spec = pl.BlockSpec((1, SUB, width, chans), lambda s, f: (s, f[1] * (rows // SUB - 1), 0, 0))
     side_out = jax.ShapeDtypeStruct((slots, rows, SIDE, chans), jnp.bfloat16)
-    end_out = jax.ShapeDtypeStruct((slots, DEPTH, width - 2 * SIDE, chans), jnp.bfloat16)
     strip_out = jax.ShapeDtypeStruct((slots, DEPTH, width, chans), jnp.bfloat16)
     halves = chans // LANES
     halo_pads = (halves, 2 * DEPTH, width + 2 * SUB, LANES)
     side_pads = (halves, rows + 2 * DEPTH, 2 * SUB, LANES)
-    extras = (top, bot, left, right)
-    sl, sr, se, dl, dr, de, tb = run(
+    extras = (top, bot, left, right, new_ends[:, ::-1])
+    hidden = proj_in.shape[1]
+    sl, sr, dl, dr, tb = run(
         edge_kernel,
         "edge_cells",
         (0, slots),
         (partial,) * 3 + (fields,) * 3 + (cotangent,) * 3 + extras + (weights, turned) + mats,
         [near_spec, far_spec, end_spec] * 3 + [by_slot(x) for x in extras] + [whole(x) for x in (weights, turned) + mats],
-        [side_out, side_out, end_out, side_out, side_out, end_out, strip_out],
-        [halo_pads, side_pads, side_pads, (2, rows, SIDE, chans), (DEPTH, width - 2 * SIDE, chans)],
+        [side_out, side_out, side_out, side_out, strip_out],
+        [halo_pads, side_pads, side_pads, (2, rows, SIDE, chans), (DEPTH, width - 2 * SIDE, chans)]
+        + [weights.shape] * 2,
         flags,
         micros=23,
+        halves=[(DEPTH, width - 2 * SIDE, chans)] + [(2 * rows * SIDE, hidden)] * 2,
     )
 
     outer = jnp.stack([dl[:, :, :SUB], dr[:, :, SIDE - SUB :]], axis=1)
@@ -771,11 +794,10 @@
     found = face_all(own)
 
     full = jax.ShapeDtypeStruct(fields.shape, jnp.bfloat16)
-    ins = (partial, fields, cotangent, top, bot, sl, sr, se, dl, dr, de)
     done = ()
     for span, sign in (((0, 1), tb), ((1, slots - 1), own)):
         gated = lax.optimization_barrier((fields, sign))[0]
-        ins = (partial, gated, cotangent, top, bot, sl, sr, se, dl, dr, de)
+        ins = (partial, gated, cotangent, top, bot, sl, sr, dl, dr)
         done = run(
             interior_kernel,
             "interior_cells",
@@ -783,26 +805,26 @@
             ins + (weights,) + mats,
             [by_slot(x, span[0]) for x in ins] + [whole(x) for x in (weights,) + mats],
             [full, full],
-            [halo_pads, (2 * DEPTH, width - 2 * SIDE, chans)],
-            flags,
-            micros=10 * span[1],
+            [halo_pads, (rows, width - 2 * SIDE, chans)],
+            micros=8 * span[1],
             into=done,
+            halves=[(SUB * (width - 2 * SIDE), hidden)] * 2,
         )
     section_out, dconv = done
     above, below = halo(dconv[:, :DEPTH], dconv[:, rows - DEPTH :])
-    grad = conv_partial(dconv, turned, "conv_gradient", (0, 1))
+    grad = conv_partial(dconv, shared_turned, "conv_gradient", (0, 1))
     grad, found = lax.optimization_barrier((grad, found))
     picked = pick(found, target)
     late, picked = lax.optimization_barrier((dconv, picked))
     sides = turn_sides(picked[:, 2:], target_mirror[:, 2:])
     ends = turn_ends(gather_ends(picked[:, :2])[0], target_mirror[:, :2])
-    grad = conv_partial(late, turned, "conv_gradient_rest", (1, slots - 1), (grad,))
+    grad = conv_partial(late, shared_turned, "conv_gradient_rest", (1, slots - 1), (grad,))
 
     top = jnp.where(first_tile, ends, 0)
     bot = jnp.where(last_tile, ends[:, ::-1], 0)
     sides = jnp.swapaxes(sides, 2, 3)
-    left = jnp.pad(sides[:, 0], ((0, 0), (0, 0), (0, SUB - DEPTH), (0, 0)))
-    right = jnp.pad(sides[:, 1, :, ::-1], ((0, 0), (0, 0), (SUB - DEPTH, 0), (0, 0)))
+    left = jnp.pad(sides[:, 0], ((0, 0), (0, 0), (0, SIDE - DEPTH), (0, 0)))
+    right = jnp.pad(sides[:, 1, :, ::-1], ((0, 0), (0, 0), (SIDE - DEPTH, 0), (0, 0)))
     ins = (grad, cotangent, above, below, top, bot, left, right)
     field_grad = run(
         join_kernel,
@@ -811,7 +833,7 @@
         ins + (turned,),
         [by_slot(x) for x in ins] + [whole(turned)],
         [full],
-        [halo_pads, (rows, width, chans)],
+        [halo_pads, (2 * DEPTH, width, chans)],
     )[0]
     return (section_out, field_grad)
 

time: 228 us -> 223 us (0.978)
  Pallas kernels: 124 us -> 112 us
  waiting for transfers between devices: 14.6 us -> 22.7 us
  starting transfers between devices: 39.9 us -> 36.9 us
  local copies, waits for them, and re-layouts: 33.1 us -> 36 us
    pallas_call x9, Pallas kernels: 124 us -> 112 us  [run(): pl.pallas_call(body, grid_spec=pltpu.PrefetchScalarGridSpec(num_scalar_pr...]
    all_to_all x2, waiting for transfers between devices: 5.9 us -> 11.8 us  [face_all(): return lax.all_to_all(send, 'face', split_axis=0, concat_axis=0, tiled=True)]
    ppermute x2, starting transfers between devices: 6.93 us -> 3.55 us  [halo(): above = lax.ppermute(last, 'tile', [(t, t + 1) for t in range(tiles - 1)])]
    unnamed x42 -> x48, local copies, waits for them, and re-layouts: 7.07 us -> 7.88 us
  transfers between devices with their start and end apart: 12 -> 12, of which waited for: 4 -> 4; matrix products, arithmetic and copies ran while one was open for 9% -> 10% of each run, Pallas kernels for 39% -> 35%
where the time goes in v4:
time: 223 us; the launch traced here: 222 us
  Pallas kernels  112 us (50%)
  starting transfers between devices  36.9 us (17%)
  local copies, waits for them, and re-layouts  36 us (16%)
  waiting for transfers between devices  22.7 us (10%)
  other arithmetic  12.6 us (6%)
    pallas_call x9, Pallas kernels, run(): pl.pallas_call(body, grid_spec=pltpu.PrefetchScalarGridSpec(num_scalar_pr...  112 us
    all_to_all x2, waiting for transfers between devices, face_all(): return lax.all_to_all(send, 'face', split_axis=0, concat_axis=0, tiled=True)  11.8 us
    all_to_all x2, starting transfers between devices, spread_ends(): got = lax.all_to_all(send, 'tile', split_axis=0, concat_axis=0, tiled=True)  8.94 us
    all_to_all x2, starting transfers between devices, face_all(): return lax.all_to_all(send, 'face', split_axis=0, concat_axis=0, tiled=True)  8.4 us
    unnamed x48, local copies, waits for them, and re-layouts  7.88 us
    all_to_all x2, starting transfers between devices, gather_ends(): got = lax.all_to_all(send, 'tile', split_axis=0, concat_axis=0, tiled=True)  7.35 us
    ppermute x2, starting transfers between devices, turn_sides(): lax.ppermute(sides, 'tile', [(t, tiles - 1 - t) for t in range(tiles)])  6.03 us
    ppermute x2, waiting for transfers between devices, turn_sides(): lax.ppermute(sides, 'tile', [(t, tiles - 1 - t) for t in range(tiles)])  5.54 us
  transfers between devices with their start and end apart: 12, of which 4 were waited for; matrix products, arithmetic and copies ran while one was open for 10% of the time, Pallas kernels for 35%

profile of v4, /device:TPU:0, one launch (start us, length us, event | category | flops | bytes accessed | tf_op | source)
XLA Modules:
  0.0 221.6 jit_solution(651036865650269080)
XLA Ops:
  0.8 0.8 select_reduce_fusion
  1.6 0.7 gather_fusion
  2.7 1.2 reverse_select_fusion.1
  3.9 0.7 rev.41
  5.8 0.9 pad_maximum_fusion
  6.7 5.2 %all-to-all-start = ((bf16[8,168,256]{2,1,0:T(8,128)(2,1)}), bf16[8,168,256]{2,1,0:T(8,128)(2,1)S(1)}, u32[]{:S(2)}, u32[]{:S(2)}) async-start(bf16[8,168,256]{2,1,0:T(8,128)(2,1)} %pad_maximum_fusion), calls=%async_computation | async-start | bytes 1376256 | tf_op jit(solution)/shard_map/all_to_all | solution.py:632
  11.8 1.1 slice_bitcast_fusion.7
  13.4 2.7 %collective-permute-start = (bf16[3,2,3,16,256]{4,2,3,0,1:T(4,128)(2,1)S(1)}, bf16[3,2,3,16,256]{4,2,3,0,1:T(4,128)(2,1)S(1)}, u32[]{:S(2)}, u32[]{:S(2)}) collective-permute-start(bf16[3,2,3,16,256]{4,2,3,0,1:T(4,128)(2,1)S(1)} %maximum_bitcast_fusion.1), channel_id=1, source_target_pairs={{0,7},{1,6},{2,5},{3,4},{4,3},{5,2},{6,1},{7,0},{8,15},{9,14},{10,... | collective-permute-start | bytes 442376 | tf_op jit(solution)/shard_map/ppermute | solution.py:600
  16.1 0.7 gather_fusion.1
  16.8 0.7 gather_fusion.2
  18.0 0.7 add_convert_fusion.refs_0_
  18.9 1.0 copy.107
  19.9 1.0 copy.108
  21.5 5.5 %collective-permute-done = bf16[3,2,3,16,256]{4,2,3,0,1:T(4,128)(2,1)S(1)} collective-permute-done((bf16[3,2,3,16,256]{4,2,3,0,1:T(4,128)(2,1)S(1)}, bf16[3,2,3,16,256]{4,2,3,0,1:T(4,128)(2,1)S(1)}, u32[]{:S(2)}, u32[]{:S(2)}) %collective-permute-start) | collective-permute-done | bytes 147488 | tf_op jit(solution)/shard_map/ppermute | solution.py:600
  28.5 2.2 fusion.16
  30.6 2.2 %collective-permute-start.1 = (bf16[3,3,128,256]{3,2,1,0:T(8,128)(2,1)}, bf16[3,3,128,256]{3,2,1,0:T(8,128)(2,1)S(1)}, u32[]{:S(2)}, u32[]{:S(2)}) collective-permute-start(bf16[3,3,128,256]{3,2,1,0:T(8,128)(2,1)} %get-tuple-element.58), channel_id=1, source_target_pairs={{0,1},{1,2},{2,3},{3,4},{4,5},{5,6},{6,7},{8,9},{9,10},{10,11},{11... | collective-permute-start | bytes 1769480 | tf_op jit(solution)/shard_map/ppermute | solution.py:668
  32.9 1.3 collective-permute-start.2
  34.2 1.1 broadcast_in_dim.157
  35.3 4.9 %all-to-all-start.1 = ((bf16[4,3,4,3,16,256]{5,4,3,2,1,0:T(8,128)(2,1)}), bf16[4,3,4,3,16,256]{5,4,3,2,1,0:T(8,128)(2,1)S(1)}, u32[]{:S(2)}, u32[]{:S(2)}) async-start(bf16[4,3,4,3,16,256]{5,4,3,2,1,0:T(8,128)(2,1)} %broadcast_in_dim.157), calls=%async_computation.1 | async-start | bytes 2359296 | tf_op jit(solution)/shard_map/all_to_all | solution.py:595
  40.2 0.6 bitcast_bitcast_fusion.1.refs_1_
  40.8 15.3 %conv_partial.1.refs_2_ = f32[3,16,128,256]{3,2,1,0:T(8,128)} custom-call(bf16[3,16,128,256]{3,2,1,0:T(8,128)(2,1)} %refs_1_.2, f32[2,80,128]{2,1,0:T(8,128)} %bitcast_bitcast_fusion.1.refs_1_), custom_call_target="tpu_custom_call" | custom-call | flops 17999998976 | bytes 3145728 | tf_op jit(solution)/shard_map/conv_partial/pallas_call | solution.py:565
  57.6 0.6 bitcast_bitcast_fusion.refs_1_
  58.2 11.8 %all-to-all-done.1 = bf16[4,3,4,3,16,256]{5,4,3,2,1,0:T(8,128)(2,1)S(1)} async-done(((bf16[4,3,4,3,16,256]{5,4,3,2,1,0:T(8,128)(2,1)}), bf16[4,3,4,3,16,256]{5,4,3,2,1,0:T(8,128)(2,1)S(1)}, u32[]{:S(2)}, u32[]{:S(2)}) %all-to-all-start.1) | async-done | bytes 1179680 | tf_op jit(solution)/shard_map/all_to_all | solution.py:595
  71.2 0.9 fusion.2
  72.2 3.7 %all-to-all-start.2 = ((bf16[8,200,256]{2,1,0:T(8,128)(2,1)}), bf16[8,200,256]{2,1,0:T(8,128)(2,1)S(1)}, u32[]{:S(2)}, u32[]{:S(2)}) async-start(bf16[8,200,256]{2,1,0:T(8,128)(2,1)} %fusion.2), calls=%async_computation.2 | async-start | bytes 1638400 | tf_op jit(solution)/shard_map/all_to_all | solution.py:661
  75.9 9.0 %conv_partial_rest.1.refs_1_.refs_2_.refs_3_.refs_0_ = f32[3,16,128,256]{3,2,1,0:T(8,128)} custom-call(bf16[3,16,128,256]{3,2,1,0:T(8,128)(2,1)} %refs_1_.2, f32[2,80,128]{2,1,0:T(8,128)} %bitcast_bitcast_fusion.1.refs_1_, f32[3,16,128,256]{3,2,1,0:T(8,128)} %conv_partial.1.refs_2_), custom_call_target="tpu_custom_call", output_to_operand_aliasing={{}: (2, {})} | custom-call | flops 8999999488 | bytes 3145728 | tf_op jit(solution)/shard_map/conv_partial_rest/pallas_call | solution.py:565
  84.9 3.7 %all-to-all-done.2 = bf16[8,200,256]{2,1,0:T(8,128)(2,1)S(1)} async-done(((bf16[8,200,256]{2,1,0:T(8,128)(2,1)}), bf16[8,200,256]{2,1,0:T(8,128)(2,1)S(1)}, u32[]{:S(2)}, u32[]{:S(2)}) %all-to-all-start.2) | async-done | bytes 819232 | tf_op jit(solution)/shard_map/all_to_all | solution.py:661
  89.4 0.8 pad.60.refs_12_
  90.2 0.8 pad.61.refs_13_
  91.1 1.0 broadcast_select_fusion.2.refs_11_.refs_4_
  92.0 0.9 rev.44.refs_14_
  92.9 1.0 broadcast_select_fusion.4.refs_10_.refs_3_
  93.9 20.7 %edge_cells.1 = (bf16[3,16,16,256]{3,2,1,0:T(8,128)(2,1)}, bf16[3,16,16,256]{3,2,1,0:T(8,128)(2,1)}, bf16[3,16,16,256]{3,2,1,0:T(8,128)(2,1)}, bf16[3,16,16,256]{3,2,1,0:T(8,128)(2,1)}, bf16[3,3,128,256]{3,2,1,0:T(8,128)(2,1)}) custom-call(s32[2]{0:T(128)} %add_convert_fusion.refs_0_, f32[3,16,128,256]{3,2,1,0:T(8,128)} %conv_partial_rest.1.refs_1_.refs_2_.refs_3_.refs_0_, ...), custom_call_target="tpu_custom_call" | custom-call | flops 23000000512 | bytes 2162688 | tf_op jit(solution)/shard_map/edge_cells/pallas_call | solution.py:565
  114.6 1.0 slice_bitcast_fusion.3
  115.7 0.9 slice_bitcast_fusion.2
  117.0 0.9 fusion.3
  117.9 3.8 %all-to-all-start.3 = ((bf16[8,200,256]{2,1,0:T(8,128)(2,1)}), bf16[8,200,256]{2,1,0:T(8,128)(2,1)S(1)}, u32[]{:S(2)}, u32[]{:S(2)}) async-start(bf16[8,200,256]{2,1,0:T(8,128)(2,1)} %fusion.3), calls=%async_computation.3 | async-start | bytes 1638400 | tf_op jit(solution)/shard_map/all_to_all | solution.py:632
  121.7 11.0 %interior_cells.2 = (bf16[3,16,128,256]{3,2,1,0:T(8,128)(2,1)}, bf16[3,16,128,256]{3,2,1,0:T(8,128)(2,1)}) custom-call(f32[3,16,128,256]{3,2,1,0:T(8,128)} %conv_partial_rest.1.refs_1_.refs_2_.refs_3_.refs_0_, bf16[3,16,128,256]{3,2,1,0:T(8,128)(2,1)} %refs_1_.2, bf16[3,16,128,256]{3,2,1,0:T(8,128)(2,1)} %refs_1_.3, ...), custom_call_target="tpu_custom_call" | custom-call | flops 8000000000 | bytes 6291456 | tf_op jit(solution)/shard_map/interior_cells/pallas_call | solution.py:565
  132.7 1.7 all-to-all-done.3
  134.8 0.9 slice_bitcast_fusion
  135.7 3.4 %side_strips.1 = (f32[3,16,8,256]{3,2,1,0:T(8,128)}, f32[3,16,8,256]{3,2,1,0:T(8,128)}) custom-call(bf16[3,22,8,256]{3,2,1,0:T(8,128)(2,1)} %get-tuple-element.66.refs_0_, bf16[3,22,8,256]{3,2,1,0:T(8,128)(2,1)} %get-tuple-element.65.refs_1_, f32[2,56,128]{2,1,0:T(8,128)} %pad.63.refs_16_.refs_2_.refs_8_), custom_call_target="tpu_custom_call" | custom-call | flops 10000000000 | bytes 393216 | tf_op jit(solution)/shard_map/side_strips/pallas_call | solution.py:565
  139.1 1.0 slice.262
  140.4 1.0 fusion.5
  141.9 1.1 broadcast_in_dim.169
  143.0 3.5 %all-to-all-start.4 = ((bf16[4,3,4,3,16,256]{5,4,3,2,1,0:T(8,128)(2,1)}), bf16[4,3,4,3,16,256]{5,4,3,2,1,0:T(8,128)(2,1)S(1)}, u32[]{:S(2)}, u32[]{:S(2)}) async-start(bf16[4,3,4,3,16,256]{5,4,3,2,1,0:T(8,128)(2,1)} %broadcast_in_dim.169), calls=%async_computation.4 | async-start | bytes 2359296 | tf_op jit(solution)/shard_map/all_to_all | solution.py:595
  146.5 18.7 %interior_cells.3 = (bf16[3,16,128,256]{3,2,1,0:T(8,128)(2,1)}, bf16[3,16,128,256]{3,2,1,0:T(8,128)(2,1)}) custom-call(f32[3,16,128,256]{3,2,1,0:T(8,128)} %conv_partial_rest.1.refs_1_.refs_2_.refs_3_.refs_0_, bf16[3,16,128,256]{3,2,1,0:T(8,128)(2,1)} %refs_1_.2, bf16[3,16,128,256]{3,2,1,0:T(8,128)(2,1)} %refs_1_.3, ...), custom_call_target="tpu_custom_call", output_to_operand_aliasing={{0}: (16, {}), {1}: (17, {})} | custom-call | flops 16000000000 | bytes 6291456 | tf_op jit(solution)/shard_map/interior_cells/pallas_call | solution.py:565
  165.2 1.3 fusion.15
  166.5 1.3 collective-permute-start.3
  167.9 1.3 collective-permute-start.4
  169.2 8.9 %conv_gradient.1.refs_2_ = f32[3,16,128,256]{3,2,1,0:T(8,128)} custom-call(bf16[3,16,128,256]{3,2,1,0:T(8,128)(2,1)} %get-tuple-element.48.refs_0_, f32[2,80,128]{2,1,0:T(8,128)} %bitcast_bitcast_fusion.refs_1_), custom_call_target="tpu_custom_call" | custom-call | flops 8999999488 | bytes 3145728 | tf_op jit(solution)/shard_map/conv_gradient/pallas_call | solution.py:565
  179.1 3.3 %collective-permute-start.5 = (bf16[3,2,3,16,256]{4,2,3,0,1:T(4,128)(2,1)S(1)}, bf16[3,2,3,16,256]{4,2,3,0,1:T(4,128)(2,1)S(1)}, u32[]{:S(2)}, u32[]{:S(2)}) collective-permute-start(bf16[3,2,3,16,256]{4,2,3,0,1:T(4,128)(2,1)S(1)} %slice.311), channel_id=1, source_target_pairs={{0,7},{1,6},{2,5},{3,4},{4,3},{5,2},{6,1},{7,0},{8,15},{9,14},{10,... | collective-permute-start | bytes 442376 | tf_op jit(solution)/shard_map/ppermute | solution.py:600
  182.4 0.6 constant_dynamic-update-slice_fusion.15
  184.9 0.6 constant_dynamic-update-slice_fusion.11
  185.6 0.6 constant_dynamic-update-slice_fusion.10
  186.2 0.6 constant_dynamic-update-slice_fusion.9
  187.5 3.6 %all-to-all-start.5 = ((bf16[8,144,256]{2,1,0:T(8,128)(2,1)}), bf16[8,144,256]{2,1,0:T(8,128)(2,1)S(1)}, u32[]{:S(2)}, u32[]{:S(2)}) async-start(bf16[8,144,256]{2,1,0:T(8,128)(2,1)} %constant_dynamic-update-slice_fusion.8), calls=%async_computation.5 | async-start | bytes 1179648 | tf_op jit(solution)/shard_map/all_to_all | solution.py:661
  191.1 15.4 %conv_gradient_rest.1.refs_0_ = f32[3,16,128,256]{3,2,1,0:T(8,128)} custom-call(bf16[3,16,128,256]{3,2,1,0:T(8,128)(2,1)} %get-tuple-element.48.refs_0_, f32[2,80,128]{2,1,0:T(8,128)} %bitcast_bitcast_fusion.refs_1_, f32[3,16,128,256]{3,2,1,0:T(8,128)} %conv_gradient.1.refs_2_), custom_call_target="tpu_custom_call", output_to_operand_aliasing={{}: (2, {})} | custom-call | flops 17999998976 | bytes 3145728 | tf_op jit(solution)/shard_map/conv_gradient_rest/pallas_call | solution.py:565
  207.0 0.9 pad.68.refs_7_
  207.9 0.8 pad.67.refs_6_
  208.8 0.7 rev.49
  209.5 1.0 broadcast_select_fusion.3
  210.5 0.9 reverse_select_fusion.refs_5_
  211.4 0.8 copy-done.14
  212.2 9.4 %join.1 = bf16[3,16,128,256]{3,2,1,0:T(8,128)(2,1)} custom-call(f32[3,16,128,256]{3,2,1,0:T(8,128)} %conv_gradient_rest.1.refs_0_, bf16[3,16,128,256]{3,2,1,0:T(8,128)(2,1)} %refs_1_.3, bf16[3,3,128,256]{3,2,1,0:T(8,128)(2,1)} %copy-done.14, bf16[3,3,128,256]{3,2,1,0:T(8,128)(2,1)} %collective-permute-done.4.refs_3_, ...), custom_call_target="tpu_custom_call" | custom-call | flops 10000000000 | bytes 3145728 | tf_op jit(solution)/shard_map/join/pallas_call | solution.py:565
  (178 shorter events, 13.5 us)
Async XLA Ops:
  1.6 1.1 slice-start
  4.6 0.7 copy-start.13
  4.6 0.7 copy-start.6
  5.7 10.4 %copy-start = (s32[48]{0:T(128)S(1)}, s32[48]{0:T(128)}, u32[]{:S(2)}) copy-start(s32[48]{0:T(128)} %param.26) | copy-start | bytes 580
  6.7 20.6 %all-to-all-start = ((bf16[8,168,256]{2,1,0:T(8,128)(2,1)}), bf16[8,168,256]{2,1,0:T(8,128)(2,1)S(1)}, u32[]{:S(2)}, u32[]{:S(2)}) async-start(bf16[8,168,256]{2,1,0:T(8,128)(2,1)} %pad_maximum_fusion), calls=%async_computation | async-start | bytes 1376256 | tf_op jit(solution)/shard_map/all_to_all | solution.py:632
  13.4 4.6 %copy-start.12 = (f32[256]{0:T(256)S(1)}, f32[256]{0:T(256)}, u32[]{:S(2)}) copy-start(f32[256]{0:T(256)} %param.24) | copy-start | bytes 3076
  13.4 4.6 %copy-start.8 = (f32[256]{0:T(256)S(1)}, f32[256]{0:T(256)}, u32[]{:S(2)}) copy-start(f32[256]{0:T(256)} %param.25) | copy-start | bytes 3076
  13.4 4.6 %copy-start.7 = (f32[256]{0:T(256)S(1)}, f32[256]{0:T(256)}, u32[]{:S(2)}) copy-start(f32[256]{0:T(256)} %param.19) | copy-start | bytes 3076
  13.4 5.5 %copy-start.4 = (bf16[1024,256]{1,0:T(8,128)(2,1)S(1)}, bf16[1024,256]{1,0:T(8,128)(2,1)}, u32[]{:S(2)}) copy-start(bf16[1024,256]{1,0:T(8,128)(2,1)} %refs_13_.3) | copy-start | bytes 1572868
  13.4 13.7 %collective-permute-start = (bf16[3,2,3,16,256]{4,2,3,0,1:T(4,128)(2,1)S(1)}, bf16[3,2,3,16,256]{4,2,3,0,1:T(4,128)(2,1)S(1)}, u32[]{:S(2)}, u32[]{:S(2)}) collective-permute-start(bf16[3,2,3,16,256]{4,2,3,0,1:T(4,128)(2,1)S(1)} %maximum_bitcast_fusion.1), channel_id=1, source_target_pairs={{0,7},{1,6},{2,5},{3,4},{4,3},{5,2},{6,1},{7,0},{8,15},{9,14},{10,... | collective-permute-start | bytes 442376 | tf_op jit(solution)/shard_map/ppermute | solution.py:600
  16.8 3.1 %copy-start.3 = (bf16[256,1024]{1,0:T(8,128)(2,1)S(1)}, bf16[256,1024]{1,0:T(8,128)(2,1)}, u32[]{:S(2)}) copy-start(bf16[256,1024]{1,0:T(8,128)(2,1)} %refs_12_.3) | copy-start | bytes 1572868
  16.8 4.1 %copy-start.11 = (f32[256]{0:T(256)S(1)}, f32[256]{0:T(256)}, u32[]{:S(2)}) copy-start(f32[256]{0:T(256)} %param.20) | copy-start | bytes 3076
  18.9 8.4 %copy-start.9 = (pred[3,2]{0,1:T(4,128)(4,1)}, pred[3,2]{0,1:T(4,128)(4,1)S(1)}, u32[]{:S(2)}) copy-start(pred[3,2]{0,1:T(4,128)(4,1)S(1)} %copy.95) | copy-start | bytes 22
  30.6 27.6 %collective-permute-start.1 = (bf16[3,3,128,256]{3,2,1,0:T(8,128)(2,1)}, bf16[3,3,128,256]{3,2,1,0:T(8,128)(2,1)S(1)}, u32[]{:S(2)}, u32[]{:S(2)}) collective-permute-start(bf16[3,3,128,256]{3,2,1,0:T(8,128)(2,1)} %get-tuple-element.58), channel_id=1, source_target_pairs={{0,1},{1,2},{2,3},{3,4},{4,5},{5,6},{6,7},{8,9},{9,10},{10,11},{11... | collective-permute-start | bytes 1769480 | tf_op jit(solution)/shard_map/ppermute | solution.py:668
  32.9 25.3 %collective-permute-start.2 = (bf16[3,3,128,256]{3,2,1,0:T(8,128)(2,1)S(1)}, bf16[3,3,128,256]{3,2,1,0:T(8,128)(2,1)S(1)}, u32[]{:S(2)}, u32[]{:S(2)}) collective-permute-start(bf16[3,3,128,256]{3,2,1,0:T(8,128)(2,1)S(1)} %get-tuple-element.57), channel_id=1, source_target_pairs={{1,0},{2,1},{3,2},{4,3},{5,4},{6,5},{7,6},{9,8},{10,9},{11,10},{12... | collective-permute-start | bytes 1769480 | tf_op jit(solution)/shard_map/ppermute | solution.py:669
  35.3 34.7 %all-to-all-start.1 = ((bf16[4,3,4,3,16,256]{5,4,3,2,1,0:T(8,128)(2,1)}), bf16[4,3,4,3,16,256]{5,4,3,2,1,0:T(8,128)(2,1)S(1)}, u32[]{:S(2)}, u32[]{:S(2)}) async-start(bf16[4,3,4,3,16,256]{5,4,3,2,1,0:T(8,128)(2,1)} %broadcast_in_dim.157), calls=%async_computation.1 | async-start | bytes 2359296 | tf_op jit(solution)/shard_map/all_to_all | solution.py:595
  56.5 14.2 %copy-start.5 = (f32[56,2,128]{2,0,1:T(8,128)}, f32[56,2,128]{2,0,1:T(8,128)S(1)}, u32[]{:S(2)}) copy-start(f32[56,2,128]{2,0,1:T(8,128)S(1)} %copy.106) | copy-start | bytes 172036
  70.9 5.0 %copy-start.1 = (bf16[3,4,3,16,256]{4,2,3,0,1:T(4,128)(2,1)}, bf16[3,4,3,16,256]{4,2,3,0,1:T(4,128)(2,1)S(1)}, u32[]{:S(2)}) copy-start(bf16[3,4,3,16,256]{4,2,3,0,1:T(4,128)(2,1)S(1)} %copy.101) | copy-start | bytes 884740
  72.2 16.4 %all-to-all-start.2 = ((bf16[8,200,256]{2,1,0:T(8,128)(2,1)}), bf16[8,200,256]{2,1,0:T(8,128)(2,1)S(1)}, u32[]{:S(2)}, u32[]{:S(2)}) async-start(bf16[8,200,256]{2,1,0:T(8,128)(2,1)} %fusion.2), calls=%async_computation.2 | async-start | bytes 1638400 | tf_op jit(solution)/shard_map/all_to_all | solution.py:661
  75.9 12.8 %slice-start.1 = ((bf16[3,4,3,16,256]{4,2,3,0,1:T(4,128)(2,1)}), bf16[3,2,3,16,256]{4,2,3,0,1:T(4,128)(2,1)S(1)}, s32[]{:S(2)}) async-start(bf16[3,4,3,16,256]{4,2,3,0,1:T(4,128)(2,1)} %copy-done.1), calls=%async_computation.7 | async-start | bytes 393216 | tf_op jit(solution)/shard_map/slice | solution.py:735
  114.6 2.2 %copy-start.2 = (bf16[3,3,128,256]{3,2,1,0:T(8,128)(2,1)S(1)}, bf16[3,3,128,256]{3,2,1,0:T(8,128)(2,1)}, u32[]{:S(2)}) copy-start(bf16[3,3,128,256]{3,2,1,0:T(8,128)(2,1)} %get-tuple-element.34) | copy-start | bytes 1769476
  117.9 16.4 %all-to-all-start.3 = ((bf16[8,200,256]{2,1,0:T(8,128)(2,1)}), bf16[8,200,256]{2,1,0:T(8,128)(2,1)S(1)}, u32[]{:S(2)}, u32[]{:S(2)}) async-start(bf16[8,200,256]{2,1,0:T(8,128)(2,1)} %fusion.3), calls=%async_computation.3 | async-start | bytes 1638400 | tf_op jit(solution)/shard_map/all_to_all | solution.py:632
  143.0 35.1 %all-to-all-start.4 = ((bf16[4,3,4,3,16,256]{5,4,3,2,1,0:T(8,128)(2,1)}), bf16[4,3,4,3,16,256]{5,4,3,2,1,0:T(8,128)(2,1)S(1)}, u32[]{:S(2)}, u32[]{:S(2)}) async-start(bf16[4,3,4,3,16,256]{5,4,3,2,1,0:T(8,128)(2,1)} %broadcast_in_dim.169), calls=%async_computation.4 | async-start | bytes 2359296 | tf_op jit(solution)/shard_map/all_to_all | solution.py:595
  166.5 44.9 %collective-permute-start.3 = (bf16[3,3,128,256]{3,2,1,0:T(8,128)(2,1)S(1)}, bf16[3,3,128,256]{3,2,1,0:T(8,128)(2,1)S(1)}, u32[]{:S(2)}, u32[]{:S(2)}) collective-permute-start(bf16[3,3,128,256]{3,2,1,0:T(8,128)(2,1)S(1)} %get-tuple-element.56), channel_id=1, source_target_pairs={{0,1},{1,2},{2,3},{3,4},{4,5},{5,6},{6,7},{8,9},{9,10},{10,11},{11... | collective-permute-start | bytes 1769480 | tf_op jit(solution)/shard_map/ppermute | solution.py:668
  167.9 43.6 %collective-permute-start.4 = (bf16[3,3,128,256]{3,2,1,0:T(8,128)(2,1)S(1)}, bf16[3,3,128,256]{3,2,1,0:T(8,128)(2,1)}, u32[]{:S(2)}, u32[]{:S(2)}) collective-permute-start(bf16[3,3,128,256]{3,2,1,0:T(8,128)(2,1)S(1)} %get-tuple-element.55), channel_id=1, source_target_pairs={{1,0},{2,1},{3,2},{4,3},{5,4},{6,5},{7,6},{9,8},{10,9},{11,10},{12... | collective-permute-start | bytes 1769480 | tf_op jit(solution)/shard_map/ppermute | solution.py:669
  179.1 27.4 %collective-permute-start.5 = (bf16[3,2,3,16,256]{4,2,3,0,1:T(4,128)(2,1)S(1)}, bf16[3,2,3,16,256]{4,2,3,0,1:T(4,128)(2,1)S(1)}, u32[]{:S(2)}, u32[]{:S(2)}) collective-permute-start(bf16[3,2,3,16,256]{4,2,3,0,1:T(4,128)(2,1)S(1)} %slice.311), channel_id=1, source_target_pairs={{0,7},{1,6},{2,5},{3,4},{4,3},{5,2},{6,1},{7,0},{8,15},{9,14},{10,... | collective-permute-start | bytes 442376 | tf_op jit(solution)/shard_map/ppermute | solution.py:600
  187.5 21.2 %all-to-all-start.5 = ((bf16[8,144,256]{2,1,0:T(8,128)(2,1)}), bf16[8,144,256]{2,1,0:T(8,128)(2,1)S(1)}, u32[]{:S(2)}, u32[]{:S(2)}) async-start(bf16[8,144,256]{2,1,0:T(8,128)(2,1)} %constant_dynamic-update-slice_fusion.8), calls=%async_computation.5 | async-start | bytes 1179648 | tf_op jit(solution)/shard_map/all_to_all | solution.py:661
  191.1 15.4 %copy-start.10 = (pred[3,2]{0,1:T(4,128)(4,1)S(1)}, pred[3,2]{0,1:T(4,128)(4,1)}, u32[]{:S(2)}) copy-start(pred[3,2]{0,1:T(4,128)(4,1)} %copy-done.9) | copy-start | bytes 22
  211.4 0.8 copy-start.14
